TPU v7x, 256 devices: a whole 4x4x8 slice. The times are simulated.
256 devices in a mesh: seq: 16 (over y, x), head: 16 (over z, core).
Axes of the slice: x: 4, y: 4, z: 8, core: 2. Of those that a mesh axis runs over, the one named last changes fastest.
Arguments:
- query_rows: bfloat16 [4, 8192, 8192], P(None, 'seq', 'head'), may hold values from -6 to 6
- key_rows: bfloat16 [4, 8192, 8192], P(None, 'seq', 'head'), may hold values from -6 to 6
- value_rows: bfloat16 [4, 8192, 8192], P(None, 'seq', 'head'), may hold values from -6 to 6
- prior_state: float32 [4, 64, 128, 128], P(None, 'head'), may hold values from -512 to 512
- tree_query: bfloat16 [4, 256, 8192], P(None, 'seq', 'head'), may hold values from -6 to 6
- tree_key: bfloat16 [4, 256, 8192], P(None, 'seq', 'head'), may hold values from -6 to 6
- tree_value: bfloat16 [4, 256, 8192], P(None, 'seq', 'head'), may hold values from -12 to 12
- parents: int32 [4, 256], replicated, may hold values from 0 to 254, as said below
- out_weight: bfloat16 [8192, 8192], P('head', 'seq'), may hold values from -0.0625 to 0.0625
Outputs:
- prefill_out: bfloat16 [4, 8192, 8192], P(None, 'seq', 'head')
- verified: bfloat16 [1024, 8192], P('head', 'seq')
Inputs may be any that keep to these rules, and one draw needn't show every extreme that they name: parents[r, 0] is 0; for every node n >= 1, parents[r, n] lies between n - 4 and n - 1 and is at least 0.
All inputs are finite; a program needn't handle non-finite values.
Results may differ from a plain program's by a relative error of at most 0.023.
Values may be sent and summed in bfloat16 or wider, within the bound.
No kernel may reach another device: no remote copies, remote signals or barrier semaphores. Data moves between devices by JAX's collectives and lax.ppermute only.
A program may use at most 64 MiB of HBM per device.

v0:
```python
import jax
import jax.numpy as jnp
from jax import lax
from jax.sharding import Mesh
from jax.sharding import PartitionSpec as P

DH = 128
NODES = 256
SEQ = ("seq_0", "seq_1")


epsilon = 1e-05


def nothing_yet(shard, identity):
    return jnp.zeros_like(shard) + jnp.asarray(identity, shard.dtype)


def entering(shard, axes, combine, identity):
    before = start = nothing_yet(shard, identity)
    subtotal = shard
    for axis in reversed(axes):
        peers, place = (lax.axis_size(axis), lax.axis_index(axis))
        pieces = lax.all_gather(subtotal.astype(jnp.bfloat16), axis)
        inside, subtotal = (start, start)
        for k in range(peers):
            passed = k < place
            subtotal = combine(subtotal, pieces[k].astype(shard.dtype))
            inside = jnp.where(passed, subtotal, inside)
        before = combine(inside, before)
    return before


def split_up(shard, dim, peers):
    before, after = (shard.shape[:dim], shard.shape[dim + 1 :])
    return jnp.moveaxis(shard.reshape(*before, peers, -1, *after), dim, 0)


def sum_at_owner(shard, axis, dim):
    peers = lax.axis_size(axis)
    tiles = lax.all_to_all(split_up(shard, dim, peers), axis, 0, 0, tiled=True)
    return jnp.sum(tiles.astype(jnp.float32), axis=0)


def in_one_piece(arrays, axis, split_dim, concat_dim, along):
    widths = [a.shape[along] for a in arrays]
    both = jnp.concatenate(arrays, axis=along)
    out = lax.all_to_all(both, axis, split_axis=split_dim, concat_axis=concat_dim, tiled=True)
    return tuple(jnp.split(out, [sum(widths[:k]) for k in range(1, len(widths))], axis=along))


def laid_out(tiles, dim):
    shape = list(tiles.shape[1:])
    shape[dim] *= tiles.shape[0]
    return jnp.moveaxis(tiles, 0, dim).reshape(shape)


def from_everyone(shard, axis):
    copies = jnp.broadcast_to(shard, (lax.axis_size(axis), *shard.shape))
    return lax.all_to_all(copies, axis, split_axis=0, concat_axis=0, tiled=True)


def collect(shard, axis, dim):
    return laid_out(from_everyone(shard, axis), dim)


def head_norm(field):
    return field * lax.rsqrt(jnp.mean(field * field, axis=-1, keepdims=True) + epsilon)


def on_device(
    query_rows,
    key_rows,
    value_rows,
    prior_state,
    tree_query,
    tree_key,
    tree_value,
    parents,
    out_weight,
):
    requests, tokens, width = query_rows.shape
    heads_here = width // DH
    block = min(512, tokens)
    blocks = tokens // block
    seq_index = lax.axis_index(SEQ)
    seq_count = lax.axis_size(SEQ)
    pieces_dev = requests * heads_here // seq_count
    shape_five = (requests, blocks, block, heads_here, DH)
    q_blocks = query_rows.reshape(shape_five)
    k_blocks = key_rows.reshape(shape_five)
    v_blocks = value_rows.reshape(shape_five)
    block_states = jnp.einsum(
        "rnchd,rnche->rnhde", k_blocks, v_blocks, preferred_element_type=jnp.float32
    )
    span_state = jnp.sum(block_states, axis=1)
    leading = jnp.zeros_like(block_states)
    running = jnp.concatenate([leading, jnp.cumsum(block_states, axis=1)[:, :-1]], axis=1)
    scores = jnp.einsum(
        "rnbhd,rnchd->rnhbc", q_blocks, k_blocks, preferred_element_type=jnp.float32
    )
    causal = jnp.arange(block)[:, None] >= jnp.arange(block)[None, :]
    weights = jnp.where(causal, scores, 0.0).astype(jnp.bfloat16)
    inner = jnp.einsum("rnhbc,rnchd->rnbhd", weights, v_blocks, preferred_element_type=jnp.float32)
    prefix = entering(
        span_state, SEQ, lambda earlier, later: earlier + later, jnp.zeros_like(span_state)
    )
    owned = sum_at_owner(
        span_state.reshape(requests * heads_here, DH, DH).astype(jnp.bfloat16), SEQ, 0
    )
    base_state = prior_state + prefix
    block_base = (base_state[:, None] + running).astype(jnp.bfloat16)
    context = jnp.einsum(
        "rnbhd,rnhde->rnbhe", q_blocks, block_base, preferred_element_type=jnp.float32
    )
    prefill_out = head_norm(context + inner).astype(jnp.bfloat16).reshape(requests, tokens, width)
    nodes_here = tree_query.shape[1]

    def to_owners(field):
        grouped = field.reshape(requests, nodes_here, heads_here, DH).transpose(0, 2, 1, 3)
        return grouped.reshape(seq_count, pieces_dev, nodes_here, DH)

    owner_query, owner_key, owner_value = in_one_piece(
        (to_owners(tree_query), to_owners(tree_key), to_owners(tree_value)), SEQ, 0, 2, 1
    )
    owner_query = owner_query[0]
    owner_key = owner_key[0]
    owner_value = owner_value[0]
    flat_prior = prior_state.reshape(requests * heads_here, DH, DH)
    owned_prior = lax.dynamic_slice_in_dim(flat_prior, seq_index * pieces_dev, pieces_dev, 0)
    owned_total = (owned + owned_prior).astype(jnp.bfloat16)
    piece_ids = seq_index * pieces_dev + jnp.arange(pieces_dev)
    request_ids = piece_ids // heads_here
    own_parents = jnp.take(parents, request_ids, axis=0)
    node_ids = jnp.arange(NODES)
    links = (own_parents[:, :, None] == node_ids[None, None, :]) & (node_ids[None, :, None] >= 1)
    itself = (node_ids[:, None] == node_ids[None, :])[None]
    reach = (links | itself).astype(jnp.bfloat16)
    for level in range((NODES - 1).bit_length()):
        square = jnp.einsum("pij,pjk->pik", reach, reach, preferred_element_type=jnp.float32)
        reach = jnp.minimum(square, 1.0).astype(jnp.bfloat16)
    tree_context = jnp.einsum(
        "pkd,pde->pke", owner_query, owned_total, preferred_element_type=jnp.float32
    )
    tree_scores = jnp.einsum(
        "pkd,pmd->pkm", owner_query, owner_key, preferred_element_type=jnp.float32
    )
    tree_weights = jnp.where(reach > 0, tree_scores, 0.0).astype(jnp.bfloat16)
    tree_mixed = jnp.einsum(
        "pkm,pmd->pkd", tree_weights, owner_value, preferred_element_type=jnp.float32
    )
    node_out = head_norm(tree_context + tree_mixed).astype(jnp.bfloat16)
    gathered = collect(node_out, SEQ, 0)
    merged = (
        gathered.reshape(requests, heads_here, NODES, DH)
        .transpose(0, 2, 1, 3)
        .reshape(requests * NODES, width)
    )
    verified = sum_at_owner(
        jnp.dot(merged, out_weight, preferred_element_type=jnp.float32).astype(jnp.bfloat16),
        "head",
        0,
    ).astype(jnp.bfloat16)
    return (prefill_out, verified)


def solution(mesh):
    torus = Mesh(mesh.devices.reshape(4, 4, mesh.shape["head"]), ("seq_0", "seq_1", "head"))
    return jax.shard_map(
        on_device,
        mesh=torus,
        in_specs=(
            P(None, SEQ, "head"),
            P(None, SEQ, "head"),
            P(None, SEQ, "head"),
            P(None, "head", None, None),
            P(None, SEQ, "head"),
            P(None, SEQ, "head"),
            P(None, SEQ, "head"),
            P(),
            P("head", SEQ),
        ),
        out_specs=(P(None, SEQ, "head"), P("head", SEQ)),
        check_vma=False,
    )
```

profile of v0, /device:TPU:1, one launch (start us, length us, event | category | flops | bytes accessed | tf_op | source)
XLA Modules:
  0.0 134.6 jit_solution(13934349782942184379)
XLA Ops:
  7.2 4.3 %copy.55 = bf16[4,512,512]{1,2,0:T(8,128)(2,1)} copy(bf16[4,512,512]{2,1,0:T(8,128)(2,1)} %param.11) | data formatting | bytes 4194304 | tf_op jit(solution)/shard_map/reshape.1
  11.5 3.8 %fusion.16 = bf16[4,4,128,128]{3,2,1,0:T(8,128)(2,1)} fusion(bf16[4,512,4,128]{1,3,2,0:T(8,128)(2,1)} %bitcast.134, bf16[4,512,512]{2,1,0:T(8,128)(2,1)} %param.10), kind=kOutput, calls=%fused_computation.21 | convolution fusion | flops 268697600 | bytes 4718592 | tf_op jit(solution)/shard_map/rnchd,rnche->rnhde/dot_general | solution.py:93
  15.6 0.7 copy.48
  16.3 7.6 %all-to-all-start = ((bf16[16,3,16,128]{3,2,1,0:T(8,128)(2,1)}), bf16[16,3,16,128]{3,2,1,0:T(8,128)(2,1)S(1)}, u32[]{:S(2)}, u32[]{:S(2)}) async-start(bf16[16,3,16,128]{3,2,1,0:T(8,128)(2,1)} %copy.48), calls=%async_computation | async-start | bytes 393216 | tf_op jit(solution)/shard_map/all_to_all | solution.py:48
  23.9 0.7 broadcast_select_fusion
  24.6 0.6 fusion.20
  25.2 5.8 %all-to-all-done = bf16[16,3,16,128]{3,2,1,0:T(8,128)(2,1)S(1)} async-done(((bf16[16,3,16,128]{3,2,1,0:T(8,128)(2,1)}), bf16[16,3,16,128]{3,2,1,0:T(8,128)(2,1)S(1)}, u32[]{:S(2)}, u32[]{:S(2)}) %all-to-all-start) | async-done | bytes 196640 | tf_op jit(solution)/shard_map/all_to_all | solution.py:48
  31.0 3.6 %all-to-all-start.1 = ((bf16[16,1,128,128]{3,2,1,0:T(8,128)(2,1)}), bf16[16,1,128,128]{3,2,1,0:T(8,128)(2,1)S(1)}, u32[]{:S(2)}, u32[]{:S(2)}) async-start(bf16[16,1,128,128]{3,2,1,0:T(8,128)(2,1)} %bitcast.19), calls=%async_computation.1 | async-start | bytes 1048576 | tf_op jit(solution)/shard_map/all_to_all | solution.py:41
  34.6 0.4 fusion.22
  35.1 0.4 fusion.24
  35.5 0.5 fusion.30
  36.0 15.3 %all-to-all-done.1 = bf16[16,1,128,128]{3,2,1,0:T(8,128)(2,1)S(1)} async-done(((bf16[16,1,128,128]{3,2,1,0:T(8,128)(2,1)}), bf16[16,1,128,128]{3,2,1,0:T(8,128)(2,1)S(1)}, u32[]{:S(2)}, u32[]{:S(2)}) %all-to-all-start.1) | async-done | bytes 524320 | tf_op jit(solution)/shard_map/all_to_all | solution.py:41
  51.3 0.1 convert_reduce_fusion
  51.3 1.1 fusion.80
  52.4 0.4 multiply_reduce_fusion
  52.8 0.1 copy.51
  52.9 1.2 broadcast_in_dim.48
  54.1 3.7 %all-to-all-start.2 = ((bf16[16,1,256,128]{3,2,1,0:T(8,128)(2,1)}), bf16[16,1,256,128]{3,2,1,0:T(8,128)(2,1)S(1)}, u32[]{:S(2)}, u32[]{:S(2)}) async-start(bf16[16,1,256,128]{3,2,1,0:T(8,128)(2,1)} %broadcast_in_dim.48), calls=%async_computation.2 | async-start | bytes 2097152 | tf_op jit(solution)/shard_map/all_to_all | solution.py:60
  57.8 0.2 all-gather.6.cloned.1.call-done
  58.1 2.7 %fusion.45 = bf16[1,4,4,128,128]{4,3,2,1,0:T(8,128)(2,1)} fusion(bf16[16,4,128,128]{3,2,1,0:T(8,128)(2,1)} %all-gather.6.cloned.1.call-done), kind=kLoop, calls=%fused_computation.61 | loop fusion | flops 2097152 | bytes 2621440 | tf_op jit(solution)/shard_map/convert_element_type | solution.py:24
  60.8 11.2 %all-to-all-done.2 = bf16[16,1,256,128]{3,2,1,0:T(8,128)(2,1)S(1)} async-done(((bf16[16,1,256,128]{3,2,1,0:T(8,128)(2,1)}), bf16[16,1,256,128]{3,2,1,0:T(8,128)(2,1)S(1)}, u32[]{:S(2)}, u32[]{:S(2)}) %all-to-all-start.2) | async-done | bytes 1048608 | tf_op jit(solution)/shard_map/all_to_all | solution.py:60
  72.0 0.8 copy.52
  72.8 0.2 copy-done.4
  73.0 1.8 %convolution_convert_fusion = bf16[1024,512]{1,0:T(8,128)(2,1)} fusion(bf16[512,512]{1,0:T(8,128)(2,1)S(1)} %copy-done.4, bf16[128,8,4,128]{3,2,1,0:T(4,128)(2,1)S(1)} %bitcast.139), kind=kOutput, calls=%fused_computation.16 | convolution fusion | flops 537395200 | bytes 2621440 | tf_op jit(solution)/shard_map/dot_general | solution.py:160
  74.8 12.8 %all-to-all-start.3 = ((bf16[16,64,512]{2,1,0:T(8,128)(2,1)}), bf16[16,64,512]{2,1,0:T(8,128)(2,1)S(1)}, u32[]{:S(2)}, u32[]{:S(2)}) async-start(bf16[16,64,512]{2,1,0:T(8,128)(2,1)} %bitcast.138), calls=%async_computation.3 | async-start | bytes 2097152 | tf_op jit(solution)/shard_map/all_to_all | solution.py:41
  87.6 0.1 iota_compare_fusion
  87.7 9.2 %fusion.2 = f32[4,4,512,128]{2,3,1,0:T(8,128)} fusion(bf16[4,512,4,128]{1,3,2,0:T(8,128)(2,1)} %bitcast.135, pred[512,512]{1,0:T(8,128)(4,1)S(1)} %iota_compare_fusion, bf16[4,512,512]{2,1,0:T(8,128)(2,1)S(1)} %copy-done, bf16[4,512,512]{2,1,0:T(8,128)(2,1)} %param.10), kind=kOutput, calls=%fused_computation.6 | convolution fusion | flops 2155872256 | bytes 10747904 | tf_op jit(solution)/shard_map/rnhbc,rnchd->rnbhd/dot_general | solution.py:104
  96.9 18.7 %all-to-all-done.3 = bf16[16,64,512]{2,1,0:T(8,128)(2,1)S(1)} async-done(((bf16[16,64,512]{2,1,0:T(8,128)(2,1)}), bf16[16,64,512]{2,1,0:T(8,128)(2,1)S(1)}, u32[]{:S(2)}, u32[]{:S(2)}) %all-to-all-start.3) | async-done | bytes 1048608 | tf_op jit(solution)/shard_map/all_to_all | solution.py:41
  115.6 0.8 reduce_sum.49
  116.4 5.2 %fusion = (f32[4,512,4]{1,2,0:T(4,128)S(1)}, f32[4,4,128,512]{3,2,1,0:T(8,128)S(1)}) fusion(f32[4,4,512,128]{2,3,1,0:T(8,128)} %fusion.2, f32[4,4,128,128]{3,2,1,0:T(8,128)} %param.12, bf16[4,4,4,128,128]{4,3,2,1,0:T(8,128)(2,1)} %all-gather.4.cloned.1.call-done, pred[]{:T(512)S(6)} %gt.35, pred[]{:T(512)S(6)} %gt.36, pred[]{:T(512)S(6)} %gt.37, ...), kind=kOutput, calls=%fused_computation.3 | convolution fusion | flops 278126592 | bytes 15761416 | tf_op jit(solution)/shard_map/rnbhd,rnhde->rnbhe/dot_general | solution.py:113
  121.6 2.0 %fusion.1 = bf16[4,1,512,4,128]{2,4,3,0,1:T(8,128)(2,1)} fusion(f32[4,4,128,512]{3,2,1,0:T(8,128)S(1)} %get-tuple-element.22, f32[4,512,4]{1,2,0:T(4,128)S(1)} %add_rsqrt_fusion), kind=kLoop, calls=%fused_computation.4 | loop fusion | flops 2097152 | bytes 6324224 | tf_op jit(solution)/shard_map/convert_element_type | solution.py:116
  123.7 4.1 %copy.53 = bf16[4,512,512]{2,1,0:T(8,128)(2,1)} copy(bf16[4,512,512]{1,2,0:T(8,128)(2,1)} %bitcast.132) | data formatting | bytes 4194304
  (26 shorter events, 0.3 us)
Async XLA Ops:
  7.2 80.5 %copy-start = (bf16[4,512,512]{2,1,0:T(8,128)(2,1)S(1)}, bf16[4,512,512]{2,1,0:T(8,128)(2,1)}, u32[]{:S(2)}) copy-start(bf16[4,512,512]{2,1,0:T(8,128)(2,1)} %param.9) | copy-start | bytes 6291460
  7.2 50.9 %all-gather.6.cloned.1.call-start = ((), (), s32[]{:S(2)}) async-start(), calls=%async_computation.5 | async-start | bytes 2621440 | tf_op jit(solution)/shard_map/all_gather | solution.py:24
  11.5 3.9 %copy-start.1 = (bf16[4,16,512]{2,1,0:T(8,128)(2,1)S(1)}, bf16[4,16,512]{2,1,0:T(8,128)(2,1)}, u32[]{:S(2)}) copy-start(bf16[4,16,512]{2,1,0:T(8,128)(2,1)} %param.15) | copy-start | bytes 196612
  11.5 3.9 %copy-start.2 = (bf16[4,16,512]{2,1,0:T(8,128)(2,1)S(1)}, bf16[4,16,512]{2,1,0:T(8,128)(2,1)}, u32[]{:S(2)}) copy-start(bf16[4,16,512]{2,1,0:T(8,128)(2,1)} %param.14) | copy-start | bytes 196612
  11.5 4.0 %copy-start.3 = (bf16[4,16,512]{2,1,0:T(8,128)(2,1)S(1)}, bf16[4,16,512]{2,1,0:T(8,128)(2,1)}, u32[]{:S(2)}) copy-start(bf16[4,16,512]{2,1,0:T(8,128)(2,1)} %param.13) | copy-start | bytes 196612
  16.3 14.8 %all-to-all-start = ((bf16[16,3,16,128]{3,2,1,0:T(8,128)(2,1)}), bf16[16,3,16,128]{3,2,1,0:T(8,128)(2,1)S(1)}, u32[]{:S(2)}, u32[]{:S(2)}) async-start(bf16[16,3,16,128]{3,2,1,0:T(8,128)(2,1)} %copy.48), calls=%async_computation | async-start | bytes 393216 | tf_op jit(solution)/shard_map/all_to_all | solution.py:48
  31.0 20.2 %all-to-all-start.1 = ((bf16[16,1,128,128]{3,2,1,0:T(8,128)(2,1)}), bf16[16,1,128,128]{3,2,1,0:T(8,128)(2,1)S(1)}, u32[]{:S(2)}, u32[]{:S(2)}) async-start(bf16[16,1,128,128]{3,2,1,0:T(8,128)(2,1)} %bitcast.19), calls=%async_computation.1 | async-start | bytes 1048576 | tf_op jit(solution)/shard_map/all_to_all | solution.py:41
  54.1 17.9 %all-to-all-start.2 = ((bf16[16,1,256,128]{3,2,1,0:T(8,128)(2,1)}), bf16[16,1,256,128]{3,2,1,0:T(8,128)(2,1)S(1)}, u32[]{:S(2)}, u32[]{:S(2)}) async-start(bf16[16,1,256,128]{3,2,1,0:T(8,128)(2,1)} %broadcast_in_dim.48), calls=%async_computation.2 | async-start | bytes 2097152 | tf_op jit(solution)/shard_map/all_to_all | solution.py:60
  57.8 58.6 %all-gather.4.cloned.1.call-start = ((), (), s32[]{:S(2)}) async-start(), calls=%async_computation.4 | async-start | bytes 2621440 | tf_op jit(solution)/shard_map/all_gather | solution.py:24
  72.0 1.0 copy-start.4
  74.8 40.8 %all-to-all-start.3 = ((bf16[16,64,512]{2,1,0:T(8,128)(2,1)}), bf16[16,64,512]{2,1,0:T(8,128)(2,1)S(1)}, u32[]{:S(2)}, u32[]{:S(2)}) async-start(bf16[16,64,512]{2,1,0:T(8,128)(2,1)} %bitcast.138), calls=%async_computation.3 | async-start | bytes 2097152 | tf_op jit(solution)/shard_map/all_to_all | solution.py:41
Sparse Core Ops, SparseCore 0:
  15.5 42.5 all-gather.5
  60.9 38.4 all-gather.3
where the time goes:
time: 135 us
  waiting for transfers between devices  51.2 us (38%)
  starting transfers between devices  27.7 us (21%)
  matrix products  23.5 us (17%)
  between operations  14.3 us (11%)
  local copies, waits for them, and re-layouts  11.5 us (9%)
  other arithmetic  6.4 us (5%)
    all_to_all x2, waiting for transfers between devices, sum_at_owner(): tiles = lax.all_to_all(split_up(shard, dim, peers), axis, 0, 0, tiled=True)  33.9 us
    all_to_all x2, starting transfers between devices, sum_at_owner(): tiles = lax.all_to_all(split_up(shard, dim, peers), axis, 0, 0, tiled=True)  16.4 us
    all_to_all x1, waiting for transfers between devices, from_everyone(): return lax.all_to_all(copies, axis, split_axis=0, concat_axis=0, tiled=True)  11.2 us
    dot_general x1, matrix products, on_device(): jnp.einsum('rnhbc,rnchd->rnbhd', weights, v_blocks, preferred_element_typ...  9.23 us
    all_to_all x1, starting transfers between devices, in_one_piece(): lax.all_to_all(both, axis, split_axis=split_dim, concat_axis=concat_dim,...  7.57 us
    all_to_all x1, waiting for transfers between devices, in_one_piece(): lax.all_to_all(both, axis, split_axis=split_dim, concat_axis=concat_dim,...  5.83 us
    dot_general x1, matrix products, on_device(): jnp.einsum('rnbhd,rnhde->rnbhe', q_blocks, block_base, preferred_element_...  5.24 us
    unnamed x11, local copies, waits for them, and re-layouts  4.38 us
  transfers between devices with their start and end apart: 6, of which 5 were waited for; matrix products, arithmetic and copies ran while one was open for 16% of the time, Pallas kernels for 0%

commit v1 on v0

v1 whole, which is shorter than its diff:
```python
import jax
import jax.numpy as jnp
from jax import lax
from jax.experimental import pallas as pl
from jax.experimental.pallas import tpu as pltpu
from jax.sharding import Mesh
from jax.sharding import PartitionSpec as P

DH = 128
NODES = 256
SEQ = ("y", "x")
HEAD = ("zp", "zl", "c")
EPS = 1e-05
BF = jnp.bfloat16
F32 = jnp.float32


def mm(a, b, ca, cb):
    return lax.dot_general(a, b, (((ca,), (cb,)), ((), ())), preferred_element_type=F32)


def normed(raw):
    return raw * lax.rsqrt(jnp.mean(raw * raw, axis=-1, keepdims=True) + EPS)


def room(mib):
    return pltpu.CompilerParams(vmem_limit_bytes=mib << 20)


def cost(flops, nbytes):
    return pl.CostEstimate(flops=flops, bytes_accessed=nbytes, transcendentals=0)


def states_body(k_ref, v_ref, tq_ref, tk_ref, tv_ref, o_ref):
    heads = o_ref.shape[0]
    nodes = tq_ref.shape[1]
    for h in range(heads):
        cols = slice(h * DH, (h + 1) * DH)
        kv = mm(k_ref[0, :, cols], v_ref[0, :, cols], 0, 0)
        o_ref[h, 0:DH, :] = kv.astype(BF)
        for j, ref in enumerate((tq_ref, tk_ref, tv_ref)):
            o_ref[h, DH + j * nodes : DH + (j + 1) * nodes, :] = ref[0, :, cols]


def block_states(k, v, tq, tk, tv):
    requests, tokens, width = k.shape
    heads, nodes = width // DH, tq.shape[1]
    rows = DH + 3 * nodes
    big = pl.BlockSpec((1, tokens, width), lambda r: (r, 0, 0))
    small = pl.BlockSpec((1, nodes, width), lambda r: (r, 0, 0))
    return pl.pallas_call(
        states_body,
        grid=(requests,),
        in_specs=[big, big, small, small, small],
        out_specs=pl.BlockSpec((heads, rows, DH), lambda r: (r, 0, 0)),
        out_shape=jax.ShapeDtypeStruct((requests * heads, rows, DH), BF),
        cost_estimate=cost(2 * requests * tokens * width * DH, 4 * requests * tokens * width),
        compiler_params=room(16),
        name="block_states",
    )(k, v, tq, tk, tv)


def reach_body(parents_ref, o_ref):
    row = lax.broadcasted_iota(jnp.int32, (NODES, NODES), 0)
    col = lax.broadcasted_iota(jnp.int32, (NODES, NODES), 1)
    links = (parents_ref[...] == row) & (col >= 1)
    reach = jnp.where(links | (row == col), 1.0, 0.0).astype(BF)
    for level in range((NODES - 1).bit_length()):
        reach = jnp.minimum(mm(reach, reach, 1, 0), 1.0).astype(BF)
    o_ref[...] = reach.astype(F32).T


def ancestors(own_parents):
    return pl.pallas_call(
        reach_body,
        out_shape=jax.ShapeDtypeStruct((NODES, NODES), F32),
        cost_estimate=cost(16 * NODES**3, 4 * NODES * NODES),
        compiler_params=room(4),
        name="ancestors",
    )(own_parents)


def inner_body(q_ref, k_ref, v_ref, o_ref):
    tokens, width = q_ref.shape[1:]
    half = tokens // 2
    for h in range(width // DH):
        cols = slice(h * DH, (h + 1) * DH)
        for part in range(2):
            rows = slice(part * half, (part + 1) * half)
            upto = (part + 1) * half
            scores = mm(q_ref[0, rows, cols], k_ref[0, 0:upto, cols], 1, 1)
            at = part * half + lax.broadcasted_iota(jnp.int32, scores.shape, 0)
            other = lax.broadcasted_iota(jnp.int32, scores.shape, 1)
            weights = jnp.where(at >= other, scores, 0.0).astype(BF)
            o_ref[0, rows, cols] = mm(weights, v_ref[0, 0:upto, cols], 1, 0)


def inside(q, k, v):
    requests, tokens, width = q.shape
    big = pl.BlockSpec((1, tokens, width), lambda r: (r, 0, 0))
    return pl.pallas_call(
        inner_body,
        grid=(requests,),
        in_specs=[big, big, big],
        out_specs=big,
        out_shape=jax.ShapeDtypeStruct(q.shape, F32),
        cost_estimate=cost(3 * requests * tokens * tokens * width, 10 * requests * tokens * width),
        compiler_params=room(24),
        name="inside",
    )(q, k, v)


def finish_body(q_ref, inner_ref, state_ref, o_ref):
    for h in range(state_ref.shape[0]):
        cols = slice(h * DH, (h + 1) * DH)
        raw = mm(q_ref[0, :, cols], state_ref[h], 1, 0) + inner_ref[0, :, cols]
        o_ref[0, :, cols] = normed(raw).astype(BF)


def finish(q, inner, states):
    requests, tokens, width = q.shape
    heads = width // DH
    big = pl.BlockSpec((1, tokens, width), lambda r: (r, 0, 0))
    return pl.pallas_call(
        finish_body,
        grid=(requests,),
        in_specs=[big, big, pl.BlockSpec((heads, DH, DH), lambda r: (r, 2, 0))],
        out_specs=big,
        out_shape=jax.ShapeDtypeStruct(q.shape, BF),
        cost_estimate=cost(2 * requests * tokens * width * DH, 8 * requests * tokens * width),
        compiler_params=room(24),
        name="finish",
    )(q, inner, states)


def tree_body(at_ref, got_ref, prior_ref, reach_ref, *refs):
    outs, hold = refs[:-1], refs[-1]
    peers = got_ref.shape[0]
    nodes = NODES // peers
    total = prior_ref[0]
    for s in range(peers):
        total = total + got_ref[s, 0:DH, :].astype(F32)

    def part(j):
        start = DH + j * nodes
        return got_ref[:, start : start + nodes, :].reshape(NODES, DH)

    q, k, v = part(0), part(1), part(2)
    weights = jnp.where(reach_ref[...] > 0, mm(q, k, 1, 1), 0.0).astype(BF)
    raw = mm(q, total.astype(BF), 1, 0) + mm(weights, v, 1, 0)
    hold[...] = normed(raw).astype(BF).reshape(hold.shape)
    for j, out in enumerate(outs):
        out[...] = hold[at_ref[1] ^ j]


def tree(at, got, prior, reach, groups):
    rows = NODES // groups
    whole = lambda a: pl.BlockSpec(a.shape, lambda i, at: (0,) * a.ndim)
    out = jax.ShapeDtypeStruct((rows, DH), BF)
    return pl.pallas_call(
        tree_body,
        grid_spec=pltpu.PrefetchScalarGridSpec(
            num_scalar_prefetch=1,
            grid=(1,),
            in_specs=[
                whole(got),
                pl.BlockSpec((1, DH, DH), lambda i, at: (at[0], 0, 0)),
                whole(reach),
            ],
            out_specs=[whole(out)] * groups,
            scratch_shapes=[pltpu.VMEM((groups, rows, DH), BF)],
        ),
        out_shape=[out] * groups,
        cost_estimate=cost(6 * NODES * NODES * DH, got.size * 2),
        compiler_params=room(8),
        name="tree",
    )(at, got, prior, reach)


def prefix_body(at_ref, got_ref, prior_ref, o_ref):
    running = prior_ref[0]
    for s in range(got_ref.shape[0]):
        o_ref[s] = running.astype(BF)
        running = running + got_ref[s, 0:DH, :].astype(F32)


def prefixes(at, got, prior):
    peers = got.shape[0]
    return pl.pallas_call(
        prefix_body,
        grid_spec=pltpu.PrefetchScalarGridSpec(
            num_scalar_prefetch=1,
            grid=(1,),
            in_specs=[
                pl.BlockSpec(got.shape, lambda i, at: (0, 0, 0)),
                pl.BlockSpec((1, DH, DH), lambda i, at: (at[0], 0, 0)),
            ],
            out_specs=pl.BlockSpec((peers, DH, DH), lambda i, at: (0, 2, 0)),
        ),
        out_shape=jax.ShapeDtypeStruct((peers, NODES + DH, DH), BF),
        cost_estimate=cost(peers * DH * DH, peers * DH * DH * 4),
        compiler_params=room(8),
        name="prefixes",
    )(at, got, prior)


def pack_body(*refs):
    pieces, o_ref = refs[:-2], refs[-1]
    for s in range(o_ref.shape[0]):
        for j, piece in enumerate(pieces):
            o_ref[s, j * piece.shape[0] : (j + 1) * piece.shape[0], :] = piece[...]


def packed(pieces, onto):
    peers = onto.shape[0]
    return pl.pallas_call(
        pack_body,
        grid=(1,),
        in_specs=[pl.BlockSpec(p.shape, lambda i: (0, 0)) for p in pieces]
        + [pl.BlockSpec(memory_space=pl.ANY)],
        out_specs=pl.BlockSpec((peers, NODES, DH), lambda i: (0, 0, 0)),
        out_shape=jax.ShapeDtypeStruct(onto.shape, BF),
        input_output_aliases={len(pieces): 0},
        cost_estimate=cost(0, peers * NODES * DH * 2),
        compiler_params=room(8),
        name="packed",
    )(*pieces, onto)


def project_body(at_ref, rows_ref, *refs):
    groups = (len(refs) - 1) // 2
    weights, outs, hold = refs[:groups], refs[groups:-1], refs[-1]
    requests = len(outs)
    heads = rows_ref.shape[0] // requests
    nodes = outs[0].shape[0]
    total = None
    for j in range(groups):
        lhs = jnp.concatenate(
            [
                jnp.concatenate([rows_ref[r * heads + h, j * nodes : (j + 1) * nodes, :] for h in range(heads)], axis=1)
                for r in range(requests)
            ],
            axis=0,
        )
        part = mm(lhs, weights[j][...], 1, 0)
        total = part if total is None else total + part
    hold[...] = total.astype(BF).reshape(hold.shape)
    for s, out in enumerate(outs):
        out[...] = hold[(at_ref[2] + s) % requests]


def project(at, rows, weights, requests):
    groups = len(weights)
    nodes = NODES // groups
    wide = weights[0].shape[1]
    whole = lambda a: pl.BlockSpec(a.shape, lambda i, at: (0,) * a.ndim)
    out = jax.ShapeDtypeStruct((nodes, wide), BF)
    return pl.pallas_call(
        project_body,
        grid_spec=pltpu.PrefetchScalarGridSpec(
            num_scalar_prefetch=1,
            grid=(1,),
            in_specs=[pl.BlockSpec((rows.shape[0], NODES, DH), lambda i, at: (0, 0, 0))]
            + [whole(w) for w in weights],
            out_specs=[whole(out)] * requests,
            scratch_shapes=[pltpu.VMEM((requests, nodes, wide), BF)],
        ),
        out_shape=[out] * requests,
        cost_estimate=cost(2 * rows.size * wide, 2 * rows.size + 2 * groups * weights[0].size),
        compiler_params=room(16),
        name="project",
    )(at, rows, *weights)


def on_device(q, k, v, prior, tq, tk, tv, parents, weight):
    requests, tokens, width = q.shape
    heads = width // DH
    y = lax.axis_index("y")
    seq_index = lax.axis_index(SEQ)
    zp = lax.axis_index("zp")
    group = lax.axis_index("zl") * 2 + lax.axis_index("c")
    at = jnp.stack([seq_index, group, zp]).astype(jnp.int32)
    pairs = lax.axis_size("zp")

    swap = [(0, 1), (1, 0)]
    quad = ("zl", "c")
    crossed = [(g, g ^ 3) for g in range(4)]

    sent = block_states(k, v, tq, tk, tv)
    got = lax.all_to_all(sent, SEQ, 0, 0, tiled=True)

    w_z = lax.ppermute(weight, "zl", swap)
    w_c = lax.ppermute(weight, "c", swap)

    reach = ancestors(lax.dynamic_slice_in_dim(parents, y, 1, 0))
    inner = inside(q, k, v)
    got, w_c, w_z, reach, inner = lax.optimization_barrier((got, w_c, w_z, reach, inner))
    w_zc = lax.ppermute(w_z, "c", swap)

    flat_prior = prior.reshape(requests * heads, DH, DH)
    mine, for_c, for_z, for_zc = tree(at, got, flat_prior, reach, 4)
    from_c = lax.ppermute(for_c, "c", swap)
    from_z = lax.ppermute(for_z, "zl", swap)
    from_zc = lax.ppermute(for_zc, quad, crossed)
    behind = prefixes(at, got, flat_prior)
    rows = lax.all_to_all(
        packed((mine, from_c, from_z, from_zc), behind), SEQ, 0, 0, tiled=True
    )

    parts = project(at, rows, (weight, w_c, w_z, w_zc), requests)
    total = parts[0].astype(F32)
    for s in range(1, pairs):
        ring = [(i, (i + s) % pairs) for i in range(pairs)]
        total = total + lax.ppermute(parts[s], "zp", ring).astype(F32)
    verified = total.astype(BF)

    prefill_out = finish(q, inner, rows)
    return prefill_out, verified


def solution(mesh):
    torus = Mesh(mesh.devices.reshape(4, 4, 4, 2, 2), (*SEQ, *HEAD))
    return jax.shard_map(
        on_device,
        mesh=torus,
        in_specs=(
            P(None, SEQ, HEAD),
            P(None, SEQ, HEAD),
            P(None, SEQ, HEAD),
            P(None, HEAD, None, None),
            P(None, SEQ, HEAD),
            P(None, SEQ, HEAD),
            P(None, SEQ, HEAD),
            P(),
            P(HEAD, SEQ),
        ),
        out_specs=(P(None, SEQ, HEAD), P(HEAD, SEQ)),
        check_vma=False,
    )
```

time: 135 us -> 91.2 us (0.68)
  waiting for transfers between devices: 51.2 us -> 23.9 us
  matrix products: 23.5 us -> 0 us
  Pallas kernels: 0 us -> 19 us
  between operations: 14.3 us -> 0.76 us
  other arithmetic: 6.4 us -> 0.74 us
  local copies, waits for them, and re-layouts: 11.5 us -> 15.9 us
  starting transfers between devices: 27.7 us -> 29.9 us
    all_to_all x4 -> x2, waiting for transfers between devices: 51 us -> 21.5 us  [the longest x1 21.5 us: on_device(): lax.all_to_all(packed((mine, from_c, from_z, from_zc), behind), SEQ, 0, 0...]
    dot_general x10 -> x0, matrix products: 23.5 us -> none  [the longest x1 9.23 us: on_device(): jnp.einsum('rnhbc,rnchd->rnbhd', weights, v_blocks, preferred_element_typ...]
    pallas_call x0 -> x8, Pallas kernels: none -> 19 us  [the longest x1 5.78 us: inside(): pl.pallas_call(inner_body, grid=(requests,), in_specs=[big, big, big], ou...]
    ppermute x0 -> x9, starting transfers between devices: none -> 15.3 us  [the longest x3 9.65 us: on_device(): total = total + lax.ppermute(parts[s], 'zp', ring).astype(F32)]
    all_to_all x4 -> x2, starting transfers between devices: 27.6 us -> 14.6 us  [the longest x1 7.7 us: on_device(): got = lax.all_to_all(sent, SEQ, 0, 0, tiled=True)]
    unnamed x11 -> x32, local copies, waits for them, and re-layouts: 4.38 us -> 15.9 us
    another operation x1 -> x0, local copies, waits for them, and re-layouts: 4.27 us -> none
    convert_element_type x3 -> x1, other arithmetic: 4.71 us -> 0.67 us  [on_device(): verified = total.astype(BF)]
  transfers between devices with their start and end apart: 6 -> 11, of which waited for: 5 -> 3; matrix products, arithmetic and copies ran while one was open for 16% -> 0% of each run, Pallas kernels for 0% -> 13%
where the time goes in v1:
time: 91.2 us; the launch traced here: 90.3 us
  starting transfers between devices  29.9 us (33%)
  waiting for transfers between devices  23.9 us (26%)
  Pallas kernels  19 us (21%)
  local copies, waits for them, and re-layouts  15.9 us (17%)
    all_to_all x1, waiting for transfers between devices, on_device(): lax.all_to_all(packed((mine, from_c, from_z, from_zc), behind), SEQ, 0, 0...  21.5 us
    unnamed x32, local copies, waits for them, and re-layouts  15.9 us
    ppermute x3, starting transfers between devices, on_device(): total = total + lax.ppermute(parts[s], 'zp', ring).astype(F32)  9.65 us
    all_to_all x1, starting transfers between devices, on_device(): got = lax.all_to_all(sent, SEQ, 0, 0, tiled=True)  7.7 us
    all_to_all x1, starting transfers between devices, on_device(): lax.all_to_all(packed((mine, from_c, from_z, from_zc), behind), SEQ, 0, 0...  6.93 us
    pallas_call x1, Pallas kernels, inside(): pl.pallas_call(inner_body, grid=(requests,), in_specs=[big, big, big], ou...  5.78 us
    pallas_call x1, Pallas kernels, finish(): pl.pallas_call(finish_body, grid=(requests,), in_specs=[big, big, pl.Bloc...  3.16 us
    pallas_call x1, Pallas kernels, project(): pl.pallas_call(project_body, grid_spec=pltpu.PrefetchScalarGridSpec(num_s...  2.56 us
  transfers between devices with their start and end apart: 11, of which 3 were waited for; matrix products, arithmetic and copies ran while one was open for 0% of the time, Pallas kernels for 13%

profile of v1, /device:TPU:1, one launch (start us, length us, event | category | flops | bytes accessed | tf_op | source)
XLA Modules:
  0.0 90.3 jit_solution(17267195332882964574)
XLA Ops:
  0.7 1.6 %copy-done.5 = bf16[4,512,512]{2,1,0:T(8,128)(2,1)S(1)} copy-done((bf16[4,512,512]{2,1,0:T(8,128)(2,1)S(1)}, bf16[4,512,512]{2,1,0:T(8,128)(2,1)}, u32[]{:S(2)}) %copy-start.5) | copy-done | bytes 2097176
  2.2 1.6 %copy-done.7 = bf16[4,512,512]{2,1,0:T(8,128)(2,1)S(1)} copy-done((bf16[4,512,512]{2,1,0:T(8,128)(2,1)S(1)}, bf16[4,512,512]{2,1,0:T(8,128)(2,1)}, u32[]{:S(2)}) %copy-start.7) | copy-done | bytes 2097176
  3.8 0.8 copy-done.13
  4.7 0.8 copy-done.14
  5.5 0.8 copy-done.15
  6.4 2.4 %block_states.1 = bf16[16,176,128]{2,1,0:T(8,128)(2,1)} custom-call(bf16[4,512,512]{2,1,0:T(8,128)(2,1)S(1)} %copy-done.5, bf16[4,512,512]{2,1,0:T(8,128)(2,1)S(1)} %copy-done.7, bf16[4,16,512]{2,1,0:T(8,128)(2,1)S(1)} %copy-done.13, bf16[4,16,512]{2,1,0:T(8,128)(2,1)S(1)} %copy-done.14, bf16[4,16,512]{2,1,0:T(8,128)(2,1)S(1)} %copy-done.15), custom_call_target="tpu_custom_call" | custom-call | flops 268435456 | bytes 4194304 | tf_op jit(solution)/shard_map/block_states/pallas_call | solution.py:51
  8.8 7.7 %all-to-all-start = ((bf16[16,176,128]{2,1,0:T(8,128)(2,1)}), bf16[16,176,128]{2,1,0:T(8,128)(2,1)S(1)}, u32[]{:S(2)}, u32[]{:S(2)}) async-start(bf16[16,176,128]{2,1,0:T(8,128)(2,1)} %block_states.1), calls=%async_computation | async-start | bytes 1441792 | tf_op jit(solution)/shard_map/all_to_all | solution.py:290
  16.5 1.0 %collective-permute-start = (bf16[512,512]{1,0:T(8,128)(2,1)S(1)}, bf16[512,512]{1,0:T(8,128)(2,1)}, u32[]{:S(2)}, u32[]{:S(2)}) collective-permute-start(bf16[512,512]{1,0:T(8,128)(2,1)S(1)} %copy-done.10), channel_id=1, source_target_pairs={{0,1},{1,0},{2,3},{3,2},{4,5},{5,4},{6,7},{7,6},{8,9},{9,8},{10,11... | collective-permute-start | bytes 1572872 | tf_op jit(solution)/shard_map/ppermute | solution.py:293
  17.5 1.6 %collective-permute-start.1 = (bf16[512,512]{1,0:T(8,128)(2,1)S(1)}, bf16[512,512]{1,0:T(8,128)(2,1)}, u32[]{:S(2)}, u32[]{:S(2)}) collective-permute-start(bf16[512,512]{1,0:T(8,128)(2,1)S(1)} %copy-done.10), channel_id=1, source_target_pairs={{0,2},{2,0},{1,3},{3,1},{4,6},{6,4},{5,7},{7,5},{8,10},{10,8},{9,1... | collective-permute-start | bytes 1572872 | tf_op jit(solution)/shard_map/ppermute | solution.py:292
  19.2 1.6 %ancestors.1.reach_ref = f32[256,256]{1,0:T(8,128)S(1)} custom-call(s32[1,256]{1,0:T(1,128)S(1)} %constant_dynamic-slice_fusion.parents_ref), custom_call_target="tpu_custom_call" | custom-call | flops 268435456 | bytes 262144 | tf_op jit(solution)/shard_map/ancestors/pallas_call | solution.py:74
  20.8 0.7 copy-done.11
  21.6 1.6 %copy-done.6 = bf16[4,512,512]{2,1,0:T(8,128)(2,1)S(1)} copy-done((bf16[4,512,512]{2,1,0:T(8,128)(2,1)S(1)}, bf16[4,512,512]{2,1,0:T(8,128)(2,1)}, u32[]{:S(2)}) %copy-start.6) | copy-done | bytes 2097176
  23.2 1.6 %copy-done.8 = bf16[4,512,512]{2,1,0:T(8,128)(2,1)S(1)} copy-done((bf16[4,512,512]{2,1,0:T(8,128)(2,1)S(1)}, bf16[4,512,512]{2,1,0:T(8,128)(2,1)}, u32[]{:S(2)}) %copy-start.8) | copy-done | bytes 2097176
  24.8 5.8 %inside.1.inner_ref = f32[4,512,512]{2,1,0:T(8,128)S(1)} custom-call(bf16[4,512,512]{2,1,0:T(8,128)(2,1)S(1)} %copy-done.3, bf16[4,512,512]{2,1,0:T(8,128)(2,1)S(1)} %copy-done.6, bf16[4,512,512]{2,1,0:T(8,128)(2,1)S(1)} %copy-done.8), custom_call_target="tpu_custom_call" | custom-call | flops 1610612736 | bytes 10485760 | tf_op jit(solution)/shard_map/inside/pallas_call | solution.py:101
  30.6 1.9 %copy-done.1 = f32[4,512,512]{2,1,0:T(8,128)} copy-done((f32[4,512,512]{2,1,0:T(8,128)}, f32[4,512,512]{2,1,0:T(8,128)S(1)}, u32[]{:S(2)}) %copy-start.1) | copy-done | bytes 4194328
  32.5 1.2 %copy-done.9 = f32[4,4,128,128]{3,2,1,0:T(8,128)S(1)} copy-done((f32[4,4,128,128]{3,2,1,0:T(8,128)S(1)}, f32[4,4,128,128]{3,2,1,0:T(8,128)}, u32[]{:S(2)}) %copy-start.9) | copy-done | bytes 1048600
  33.7 0.9 %copy-done.12 = f32[256,256]{1,0:T(8,128)S(1)} copy-done((f32[256,256]{1,0:T(8,128)S(1)}, f32[256,256]{1,0:T(8,128)}, u32[]{:S(2)}) %copy-start.12) | copy-done | bytes 262168
  34.7 1.0 %tree.1 = (bf16[64,128]{1,0:T(8,128)(2,1)S(1)}, bf16[64,128]{1,0:T(8,128)(2,1)S(1)}, bf16[64,128]{1,0:T(8,128)(2,1)S(1)}, bf16[64,128]{1,0:T(8,128)(2,1)S(1)}) custom-call(s32[3]{0:T(128)S(1)} %pad_add_fusion.at_ref, bf16[16,176,128]{2,1,0:T(8,128)(2,1)S(1)} %all-to-all-done.got_ref, f32[16,128,128]{2,1,0:T(8,128)S(1)} %bitcast.4, f32[256,256]{1,0:T(8,128)S(1)} %copy-done.12), custom_call_target="tpu_custom_call" | custom-call | flops 50331648 | bytes 720896 | tf_op jit(solution)/shard_map/tree/pallas_call | solution.py:160
  36.2 0.7 collective-permute-start.3
  36.9 1.0 %collective-permute-start.4 = (bf16[64,128]{1,0:T(8,128)(2,1)S(1)}, bf16[64,128]{1,0:T(8,128)(2,1)S(1)}, u32[]{:S(2)}, u32[]{:S(2)}) collective-permute-start(bf16[64,128]{1,0:T(8,128)(2,1)S(1)} %get-tuple-element.21), channel_id=1, source_target_pairs={{0,3},{1,2},{2,1},{3,0},{4,7},{5,6},{6,5},{7,4},{8,11},{9,10},{10,... | collective-permute-start | bytes 49160 | tf_op jit(solution)/shard_map/ppermute | solution.py:304
  37.9 1.4 %prefixes.1.refs_4_ = bf16[16,384,128]{2,1,0:T(8,128)(2,1)} custom-call(s32[3]{0:T(128)S(1)} %pad_add_fusion.at_ref, bf16[16,176,128]{2,1,0:T(8,128)(2,1)S(1)} %all-to-all-done.got_ref, f32[16,128,128]{2,1,0:T(8,128)S(1)} %bitcast.5), custom_call_target="tpu_custom_call" | custom-call | flops 262144 | bytes 1048576 | tf_op jit(solution)/shard_map/prefixes/pallas_call | solution.py:189
  40.1 1.1 %packed.1 = bf16[16,384,128]{2,1,0:T(8,128)(2,1)} custom-call(bf16[64,128]{1,0:T(8,128)(2,1)S(1)} %get-tuple-element.18.refs_0_, bf16[64,128]{1,0:T(8,128)(2,1)S(1)} %collective-permute-done.2.refs_1_, bf16[64,128]{1,0:T(8,128)(2,1)S(1)} %collective-permute-done.3.refs_2_, ...), custom_call_target="tpu_custom_call", output_to_operand_aliasing={{}: (4, {})} | custom-call | bytes 1048576 | tf_op jit(solution)/shard_map/packed/pallas_call | solution.py:216
  41.2 6.9 %all-to-all-start.1 = ((bf16[16,384,128]{2,1,0:T(8,128)(2,1)}), bf16[16,384,128]{2,1,0:T(8,128)(2,1)S(1)}, u32[]{:S(2)}, u32[]{:S(2)}) async-start(bf16[16,384,128]{2,1,0:T(8,128)(2,1)} %packed.1), calls=%async_computation.1 | async-start | bytes 3145728 | tf_op jit(solution)/shard_map/all_to_all | solution.py:306
  48.1 0.7 collective-permute-start.5
  48.8 1.7 %collective-permute-done.5.refs_3_ = bf16[512,512]{1,0:T(8,128)(2,1)S(1)} collective-permute-done((bf16[512,512]{1,0:T(8,128)(2,1)}, bf16[512,512]{1,0:T(8,128)(2,1)S(1)}, u32[]{:S(2)}, u32[]{:S(2)}) %collective-permute-start.5) | collective-permute-done | bytes 524320 | tf_op jit(solution)/shard_map/ppermute | solution.py:298
  50.6 21.5 %all-to-all-done.1.state_ref.rows_ref = bf16[16,384,128]{2,1,0:T(8,128)(2,1)S(1)} async-done(((bf16[16,384,128]{2,1,0:T(8,128)(2,1)}), bf16[16,384,128]{2,1,0:T(8,128)(2,1)S(1)}, u32[]{:S(2)}, u32[]{:S(2)}) %all-to-all-start.1) | async-done | bytes 1572896 | tf_op jit(solution)/shard_map/all_to_all | solution.py:306
  72.1 2.6 %project.1 = (bf16[64,512]{1,0:T(8,128)(2,1)S(1)}, bf16[64,512]{1,0:T(8,128)(2,1)S(1)}, bf16[64,512]{1,0:T(8,128)(2,1)S(1)}, bf16[64,512]{1,0:T(8,128)(2,1)S(1)}) custom-call(s32[3]{0:T(128)S(1)} %pad_add_fusion.at_ref, bf16[16,384,128]{2,1,0:T(8,128)(2,1)S(1)} %all-to-all-done.1.state_ref.rows_ref, bf16[512,512]{1,0:T(8,128)(2,1)S(1)} %copy-done.10, ...), custom_call_target="tpu_custom_call" | custom-call | flops 805306368 | bytes 3670016 | tf_op jit(solution)/shard_map/project/pallas_call | solution.py:258
  74.6 3.1 %collective-permute-start.6 = (bf16[64,512]{1,0:T(8,128)(2,1)S(1)}, bf16[64,512]{1,0:T(8,128)(2,1)S(1)}, u32[]{:S(2)}, u32[]{:S(2)}) collective-permute-start(bf16[64,512]{1,0:T(8,128)(2,1)S(1)} %get-tuple-element.25), channel_id=1, source_target_pairs={{0,4},{4,8},{8,12},{12,0},{1,5},{5,9},{9,13},{13,1},{2,6},{6,10},{... | collective-permute-start | bytes 196616 | tf_op jit(solution)/shard_map/ppermute | solution.py:314
  77.7 4.2 %collective-permute-start.7 = (bf16[64,512]{1,0:T(8,128)(2,1)S(1)}, bf16[64,512]{1,0:T(8,128)(2,1)S(1)}, u32[]{:S(2)}, u32[]{:S(2)}) collective-permute-start(bf16[64,512]{1,0:T(8,128)(2,1)S(1)} %get-tuple-element.26), channel_id=1, source_target_pairs={{0,8},{4,12},{8,0},{12,4},{1,9},{5,13},{9,1},{13,5},{2,10},{6,14},... | collective-permute-start | bytes 196616 | tf_op jit(solution)/shard_map/ppermute | solution.py:314
  81.9 2.4 %collective-permute-start.8 = (bf16[64,512]{1,0:T(8,128)(2,1)S(1)}, bf16[64,512]{1,0:T(8,128)(2,1)S(1)}, u32[]{:S(2)}, u32[]{:S(2)}) collective-permute-start(bf16[64,512]{1,0:T(8,128)(2,1)S(1)} %get-tuple-element.27), channel_id=1, source_target_pairs={{0,12},{4,0},{8,4},{12,8},{1,13},{5,1},{9,5},{13,9},{2,14},{6,2},{... | collective-permute-start | bytes 196616 | tf_op jit(solution)/shard_map/ppermute | solution.py:314
  84.3 2.2 %copy-done.2 = f32[4,512,512]{2,1,0:T(8,128)S(1)} copy-done((f32[4,512,512]{2,1,0:T(8,128)S(1)}, f32[4,512,512]{2,1,0:T(8,128)}, u32[]{:S(2)}) %copy-start.2) | copy-done | bytes 4194328
  86.5 3.2 %finish.1 = bf16[4,512,512]{2,1,0:T(8,128)(2,1)} custom-call(bf16[4,512,512]{2,1,0:T(8,128)(2,1)S(1)} %copy-done.4, f32[4,512,512]{2,1,0:T(8,128)S(1)} %copy-done.2, bf16[16,384,128]{2,1,0:T(8,128)(2,1)S(1)} %all-to-all-done.1.state_ref.rows_ref), custom_call_target="tpu_custom_call" | custom-call | flops 268435456 | bytes 8388608 | tf_op jit(solution)/shard_map/finish/pallas_call | solution.py:124
  (33 shorter events, 2.0 us)
Async XLA Ops:
  0.6 18.5 %copy-start = (s32[4,256]{1,0:T(4,128)S(1)}, s32[4,256]{1,0:T(4,128)}, u32[]{:S(2)}) copy-start(s32[4,256]{1,0:T(4,128)} %param.16) | copy-start | bytes 12292
  0.6 1.6 %copy-start.5 = (bf16[4,512,512]{2,1,0:T(8,128)(2,1)S(1)}, bf16[4,512,512]{2,1,0:T(8,128)(2,1)}, u32[]{:S(2)}) copy-start(bf16[4,512,512]{2,1,0:T(8,128)(2,1)} %k_ref.3) | copy-start | bytes 6291460
  2.2 1.6 %copy-start.7 = (bf16[4,512,512]{2,1,0:T(8,128)(2,1)S(1)}, bf16[4,512,512]{2,1,0:T(8,128)(2,1)}, u32[]{:S(2)}) copy-start(bf16[4,512,512]{2,1,0:T(8,128)(2,1)} %v_ref.3) | copy-start | bytes 6291460
  3.8 0.8 copy-start.13
  4.7 0.8 copy-start.14
  5.5 0.8 copy-start.15
  6.4 10.1 %copy-start.10 = (bf16[512,512]{1,0:T(8,128)(2,1)S(1)}, bf16[512,512]{1,0:T(8,128)(2,1)}, u32[]{:S(2)}) copy-start(bf16[512,512]{1,0:T(8,128)(2,1)} %refs_0_.1) | copy-start | bytes 1572868
  8.8 12.8 %copy-start.3 = (bf16[4,512,512]{2,1,0:T(8,128)(2,1)S(1)}, bf16[4,512,512]{2,1,0:T(8,128)(2,1)}, u32[]{:S(2)}) copy-start(bf16[4,512,512]{2,1,0:T(8,128)(2,1)} %q_ref.3) | copy-start | bytes 6291460
  8.8 23.7 %all-to-all-start = ((bf16[16,176,128]{2,1,0:T(8,128)(2,1)}), bf16[16,176,128]{2,1,0:T(8,128)(2,1)S(1)}, u32[]{:S(2)}, u32[]{:S(2)}) async-start(bf16[16,176,128]{2,1,0:T(8,128)(2,1)} %block_states.1), calls=%async_computation | async-start | bytes 1441792 | tf_op jit(solution)/shard_map/all_to_all | solution.py:290
  16.5 16.0 %collective-permute-start = (bf16[512,512]{1,0:T(8,128)(2,1)S(1)}, bf16[512,512]{1,0:T(8,128)(2,1)}, u32[]{:S(2)}, u32[]{:S(2)}) collective-permute-start(bf16[512,512]{1,0:T(8,128)(2,1)S(1)} %copy-done.10), channel_id=1, source_target_pairs={{0,1},{1,0},{2,3},{3,2},{4,5},{5,4},{6,7},{7,6},{8,9},{9,8},{10,11... | collective-permute-start | bytes 1572872 | tf_op jit(solution)/shard_map/ppermute | solution.py:293
  17.5 15.0 %collective-permute-start.1 = (bf16[512,512]{1,0:T(8,128)(2,1)S(1)}, bf16[512,512]{1,0:T(8,128)(2,1)}, u32[]{:S(2)}, u32[]{:S(2)}) collective-permute-start(bf16[512,512]{1,0:T(8,128)(2,1)S(1)} %copy-done.10), channel_id=1, source_target_pairs={{0,2},{2,0},{1,3},{3,1},{4,6},{6,4},{5,7},{7,5},{8,10},{10,8},{9,1... | collective-permute-start | bytes 1572872 | tf_op jit(solution)/shard_map/ppermute | solution.py:292
  20.8 0.7 copy-start.11
  21.6 1.6 %copy-start.6 = (bf16[4,512,512]{2,1,0:T(8,128)(2,1)S(1)}, bf16[4,512,512]{2,1,0:T(8,128)(2,1)}, u32[]{:S(2)}) copy-start(bf16[4,512,512]{2,1,0:T(8,128)(2,1)} %k_ref.3) | copy-start | bytes 6291460
  23.2 1.6 %copy-start.8 = (bf16[4,512,512]{2,1,0:T(8,128)(2,1)S(1)}, bf16[4,512,512]{2,1,0:T(8,128)(2,1)}, u32[]{:S(2)}) copy-start(bf16[4,512,512]{2,1,0:T(8,128)(2,1)} %v_ref.3) | copy-start | bytes 6291460
  30.5 2.0 %copy-start.1 = (f32[4,512,512]{2,1,0:T(8,128)}, f32[4,512,512]{2,1,0:T(8,128)S(1)}, u32[]{:S(2)}) copy-start(f32[4,512,512]{2,1,0:T(8,128)S(1)} %inside.1.inner_ref) | copy-start | bytes 12582916
  32.5 1.2 %copy-start.9 = (f32[4,4,128,128]{3,2,1,0:T(8,128)S(1)}, f32[4,4,128,128]{3,2,1,0:T(8,128)}, u32[]{:S(2)}) copy-start(f32[4,4,128,128]{3,2,1,0:T(8,128)} %param.12) | copy-start | bytes 3145732
  33.7 0.9 %copy-start.12 = (f32[256,256]{1,0:T(8,128)S(1)}, f32[256,256]{1,0:T(8,128)}, u32[]{:S(2)}) copy-start(f32[256,256]{1,0:T(8,128)} %copy-done.11) | copy-start | bytes 786436
  35.7 3.7 %collective-permute-start.2 = (bf16[64,128]{1,0:T(8,128)(2,1)S(1)}, bf16[64,128]{1,0:T(8,128)(2,1)S(1)}, u32[]{:S(2)}, u32[]{:S(2)}) collective-permute-start(bf16[64,128]{1,0:T(8,128)(2,1)S(1)} %get-tuple-element.19), channel_id=1, source_target_pairs={{0,1},{1,0},{2,3},{3,2},{4,5},{5,4},{6,7},{7,6},{8,9},{9,8},{10,11... | collective-permute-start | bytes 49160 | tf_op jit(solution)/shard_map/ppermute | solution.py:302
  36.2 3.2 %collective-permute-start.3 = (bf16[64,128]{1,0:T(8,128)(2,1)S(1)}, bf16[64,128]{1,0:T(8,128)(2,1)S(1)}, u32[]{:S(2)}, u32[]{:S(2)}) collective-permute-start(bf16[64,128]{1,0:T(8,128)(2,1)S(1)} %get-tuple-element.20), channel_id=1, source_target_pairs={{0,2},{2,0},{1,3},{3,1},{4,6},{6,4},{5,7},{7,5},{8,10},{10,8},{9,1... | collective-permute-start | bytes 49160 | tf_op jit(solution)/shard_map/ppermute | solution.py:303
  36.9 3.2 %collective-permute-start.4 = (bf16[64,128]{1,0:T(8,128)(2,1)S(1)}, bf16[64,128]{1,0:T(8,128)(2,1)S(1)}, u32[]{:S(2)}, u32[]{:S(2)}) collective-permute-start(bf16[64,128]{1,0:T(8,128)(2,1)S(1)} %get-tuple-element.21), channel_id=1, source_target_pairs={{0,3},{1,2},{2,1},{3,0},{4,7},{5,6},{6,5},{7,4},{8,11},{9,10},{10,... | collective-permute-start | bytes 49160 | tf_op jit(solution)/shard_map/ppermute | solution.py:304
  41.2 30.9 %all-to-all-start.1 = ((bf16[16,384,128]{2,1,0:T(8,128)(2,1)}), bf16[16,384,128]{2,1,0:T(8,128)(2,1)S(1)}, u32[]{:S(2)}, u32[]{:S(2)}) async-start(bf16[16,384,128]{2,1,0:T(8,128)(2,1)} %packed.1), calls=%async_computation.1 | async-start | bytes 3145728 | tf_op jit(solution)/shard_map/all_to_all | solution.py:306
  48.1 2.5 %collective-permute-start.5 = (bf16[512,512]{1,0:T(8,128)(2,1)}, bf16[512,512]{1,0:T(8,128)(2,1)S(1)}, u32[]{:S(2)}, u32[]{:S(2)}) collective-permute-start(bf16[512,512]{1,0:T(8,128)(2,1)} %collective-permute-done.1.refs_2_), channel_id=1, source_target_pairs={{0,1},{1,0},{2,3},{3,2},{4,5},{5,4},{6,7},{7,6},{8,9},{9,8},{10,11... | collective-permute-start | bytes 1572872 | tf_op jit(solution)/shard_map/ppermute | solution.py:298
  72.1 12.2 %copy-start.4 = (bf16[4,512,512]{2,1,0:T(8,128)(2,1)S(1)}, bf16[4,512,512]{2,1,0:T(8,128)(2,1)}, u32[]{:S(2)}) copy-start(bf16[4,512,512]{2,1,0:T(8,128)(2,1)} %q_ref.3) | copy-start | bytes 6291460
  74.6 15.0 %collective-permute-start.6 = (bf16[64,512]{1,0:T(8,128)(2,1)S(1)}, bf16[64,512]{1,0:T(8,128)(2,1)S(1)}, u32[]{:S(2)}, u32[]{:S(2)}) collective-permute-start(bf16[64,512]{1,0:T(8,128)(2,1)S(1)} %get-tuple-element.25), channel_id=1, source_target_pairs={{0,4},{4,8},{8,12},{12,0},{1,5},{5,9},{9,13},{13,1},{2,6},{6,10},{... | collective-permute-start | bytes 196616 | tf_op jit(solution)/shard_map/ppermute | solution.py:314
  77.7 12.0 %collective-permute-start.7 = (bf16[64,512]{1,0:T(8,128)(2,1)S(1)}, bf16[64,512]{1,0:T(8,128)(2,1)S(1)}, u32[]{:S(2)}, u32[]{:S(2)}) collective-permute-start(bf16[64,512]{1,0:T(8,128)(2,1)S(1)} %get-tuple-element.26), channel_id=1, source_target_pairs={{0,8},{4,12},{8,0},{12,4},{1,9},{5,13},{9,1},{13,5},{2,10},{6,14},... | collective-permute-start | bytes 196616 | tf_op jit(solution)/shard_map/ppermute | solution.py:314
  81.9 7.8 %collective-permute-start.8 = (bf16[64,512]{1,0:T(8,128)(2,1)S(1)}, bf16[64,512]{1,0:T(8,128)(2,1)S(1)}, u32[]{:S(2)}, u32[]{:S(2)}) collective-permute-start(bf16[64,512]{1,0:T(8,128)(2,1)S(1)} %get-tuple-element.27), channel_id=1, source_target_pairs={{0,12},{4,0},{8,4},{12,8},{1,13},{5,1},{9,5},{13,9},{2,14},{6,2},{... | collective-permute-start | bytes 196616 | tf_op jit(solution)/shard_map/ppermute | solution.py:314
  84.3 2.2 %copy-start.2 = (f32[4,512,512]{2,1,0:T(8,128)S(1)}, f32[4,512,512]{2,1,0:T(8,128)}, u32[]{:S(2)}) copy-start(f32[4,512,512]{2,1,0:T(8,128)} %copy-done.1) | copy-start | bytes 12582916

commit v2 on v1

--- a/solution.py
+++ b/solution.py
@@ -25,6 +25,10 @@
 
 def room(mib):
     return pltpu.CompilerParams(vmem_limit_bytes=mib << 20)
+
+
+def far(array):
+    return pltpu.with_memory_space_constraint(array, pltpu.HBM)
 
 
 def cost(flops, nbytes):
@@ -57,7 +61,7 @@
         cost_estimate=cost(2 * requests * tokens * width * DH, 4 * requests * tokens * width),
         compiler_params=room(16),
         name="block_states",
-    )(k, v, tq, tk, tv)
+    )(far(k), far(v), far(tq), far(tk), far(tv))
 
 
 def reach_body(parents_ref, o_ref):
@@ -103,11 +107,11 @@
         grid=(requests,),
         in_specs=[big, big, big],
         out_specs=big,
-        out_shape=jax.ShapeDtypeStruct(q.shape, F32),
+        out_shape=pltpu.HBM(q.shape, F32),
         cost_estimate=cost(3 * requests * tokens * tokens * width, 10 * requests * tokens * width),
         compiler_params=room(24),
         name="inside",
-    )(q, k, v)
+    )(far(q), far(k), far(v))
 
 
 def finish_body(q_ref, inner_ref, state_ref, o_ref):
@@ -130,7 +134,7 @@
         cost_estimate=cost(2 * requests * tokens * width * DH, 8 * requests * tokens * width),
         compiler_params=room(24),
         name="finish",
-    )(q, inner, states)
+    )(far(q), far(inner), states)
 
 
 def tree_body(at_ref, got_ref, prior_ref, reach_ref, *refs):
@@ -174,7 +178,7 @@
         cost_estimate=cost(6 * NODES * NODES * DH, got.size * 2),
         compiler_params=room(8),
         name="tree",
-    )(at, got, prior, reach)
+    )(at, got, far(prior), reach)
 
 
 def prefix_body(at_ref, got_ref, prior_ref, o_ref):
@@ -201,7 +205,7 @@
         cost_estimate=cost(peers * DH * DH, peers * DH * DH * 4),
         compiler_params=room(8),
         name="prefixes",
-    )(at, got, prior)
+    )(at, got, far(prior))
 
 
 def pack_body(*refs):

time: 91.2 us -> 86.6 us (0.950)
  local copies, waits for them, and re-layouts: 15.9 us -> 1.86 us
  Pallas kernels: 19 us -> 26.8 us
  waiting for transfers between devices: 23.9 us -> 25 us
  starting transfers between devices: 29.9 us -> 30.9 us
    unnamed x32 -> x8, local copies, waits for them, and re-layouts: 15.9 us -> 1.86 us
    pallas_call x1, Pallas kernels: 5.78 us -> 8.5 us  [inside(): pl.pallas_call(inner_body, grid=(requests,), in_specs=[big, big, big], ou...]
    pallas_call x1, Pallas kernels: 3.16 us -> 5.54 us  [finish(): pl.pallas_call(finish_body, grid=(requests,), in_specs=[big, big, pl.Bloc...]
    pallas_call x1, Pallas kernels: 2.41 us -> 4.63 us  [block_states(): pl.pallas_call(states_body, grid=(requests,), in_specs=[big, big, small,...]
    ppermute x1, waiting for transfers between devices: 0.01 us -> 1.9 us  [on_device(): w_z = lax.ppermute(weight, 'zl', swap)]
    pallas_call x1, Pallas kernels: 2.56 us -> 1.29 us  [project(): pl.pallas_call(project_body, grid_spec=pltpu.PrefetchScalarGridSpec(num_s...]
  transfers between devices with their start and end apart: 11 -> 11, of which waited for: 3 -> 4; matrix products, arithmetic and copies ran while one was open for 0% -> 0% of each run, Pallas kernels for 13% -> 21%
where the time goes in v2:
time: 86.6 us; the launch traced here: 86 us
  starting transfers between devices  30.9 us (36%)
  Pallas kernels  26.8 us (31%)
  waiting for transfers between devices  25 us (29%)
  local copies, waits for them, and re-layouts  1.86 us (2%)
    all_to_all x1, waiting for transfers between devices, on_device(): lax.all_to_all(packed((mine, from_c, from_z, from_zc), behind), SEQ, 0, 0...  20.9 us
    ppermute x3, starting transfers between devices, on_device(): total = total + lax.ppermute(parts[s], 'zp', ring).astype(F32)  10.4 us
    pallas_call x1, Pallas kernels, inside(): pl.pallas_call(inner_body, grid=(requests,), in_specs=[big, big, big], ou...  8.5 us
    all_to_all x1, starting transfers between devices, on_device(): got = lax.all_to_all(sent, SEQ, 0, 0, tiled=True)  7.57 us
    all_to_all x1, starting transfers between devices, on_device(): lax.all_to_all(packed((mine, from_c, from_z, from_zc), behind), SEQ, 0, 0...  6.93 us
    pallas_call x1, Pallas kernels, finish(): pl.pallas_call(finish_body, grid=(requests,), in_specs=[big, big, pl.Bloc...  5.54 us
    pallas_call x1, Pallas kernels, block_states(): pl.pallas_call(states_body, grid=(requests,), in_specs=[big, big, small,...  4.63 us
    pallas_call x1, Pallas kernels, prefixes(): pl.pallas_call(prefix_body, grid_spec=pltpu.PrefetchScalarGridSpec(num_sc...  2.26 us
  transfers between devices with their start and end apart: 11, of which 4 were waited for; matrix products, arithmetic and copies ran while one was open for 0% of the time, Pallas kernels for 21%

profile of v2, /device:TPU:1, one launch (start us, length us, event | category | flops | bytes accessed | tf_op | source)
XLA Modules:
  0.0 86.0 jit_solution(4745622840682933130)
XLA Ops:
  0.6 0.0 copy-start
  0.7 4.6 %block_states.1 = bf16[16,176,128]{2,1,0:T(8,128)(2,1)} custom-call(bf16[4,512,512]{2,1,0:T(8,128)(2,1)} %k_ref.3, bf16[4,512,512]{2,1,0:T(8,128)(2,1)} %v_ref.3, bf16[4,16,512]{2,1,0:T(8,128)(2,1)} %tq_ref.1, bf16[4,16,512]{2,1,0:T(8,128)(2,1)} %tk_ref.1, bf16[4,16,512]{2,1,0:T(8,128)(2,1)} %tv_ref.1), custom_call_target="tpu_custom_call" | custom-call | flops 268435456 | bytes 4194304 | tf_op jit(solution)/shard_map/block_states/pallas_call | solution.py:55
  5.3 7.6 %all-to-all-start = ((bf16[16,176,128]{2,1,0:T(8,128)(2,1)}), bf16[16,176,128]{2,1,0:T(8,128)(2,1)S(1)}, u32[]{:S(2)}, u32[]{:S(2)}) async-start(bf16[16,176,128]{2,1,0:T(8,128)(2,1)} %block_states.1), calls=%async_computation | async-start | bytes 1441792 | tf_op jit(solution)/shard_map/all_to_all | solution.py:294
  12.9 1.0 %collective-permute-start = (bf16[512,512]{1,0:T(8,128)(2,1)S(1)}, bf16[512,512]{1,0:T(8,128)(2,1)S(1)}, u32[]{:S(2)}, u32[]{:S(2)}) collective-permute-start(bf16[512,512]{1,0:T(8,128)(2,1)S(1)} %copy-done.1), channel_id=1, source_target_pairs={{0,1},{1,0},{2,3},{3,2},{4,5},{5,4},{6,7},{7,6},{8,9},{9,8},{10,11... | collective-permute-start | bytes 1572872 | tf_op jit(solution)/shard_map/ppermute | solution.py:297
  13.9 1.6 %collective-permute-start.1 = (bf16[512,512]{1,0:T(8,128)(2,1)S(1)}, bf16[512,512]{1,0:T(8,128)(2,1)S(1)}, u32[]{:S(2)}, u32[]{:S(2)}) collective-permute-start(bf16[512,512]{1,0:T(8,128)(2,1)S(1)} %copy-done.1), channel_id=1, source_target_pairs={{0,2},{2,0},{1,3},{3,1},{4,6},{6,4},{5,7},{7,5},{8,10},{10,8},{9,1... | collective-permute-start | bytes 1572872 | tf_op jit(solution)/shard_map/ppermute | solution.py:296
  15.6 1.6 %ancestors.1.reach_ref = f32[256,256]{1,0:T(8,128)S(1)} custom-call(s32[1,256]{1,0:T(1,128)S(1)} %constant_dynamic-slice_fusion.parents_ref), custom_call_target="tpu_custom_call" | custom-call | flops 268435456 | bytes 262144 | tf_op jit(solution)/shard_map/ancestors/pallas_call | solution.py:78
  17.2 0.1 pad_add_fusion.at_ref
  17.2 8.5 %inside.1.inner_ref = f32[4,512,512]{2,1,0:T(8,128)} custom-call(bf16[4,512,512]{2,1,0:T(8,128)(2,1)} %q_ref.3, bf16[4,512,512]{2,1,0:T(8,128)(2,1)} %k_ref.3, bf16[4,512,512]{2,1,0:T(8,128)(2,1)} %v_ref.3), custom_call_target="tpu_custom_call" | custom-call | flops 1610612736 | bytes 10485760 | tf_op jit(solution)/shard_map/inside/pallas_call | solution.py:105
  25.8 0.0 collective-permute-done.refs_1_
  25.8 1.9 %collective-permute-done.1.refs_2_ = bf16[512,512]{1,0:T(8,128)(2,1)S(1)} collective-permute-done((bf16[512,512]{1,0:T(8,128)(2,1)S(1)}, bf16[512,512]{1,0:T(8,128)(2,1)S(1)}, u32[]{:S(2)}, u32[]{:S(2)}) %collective-permute-start.1) | collective-permute-done | bytes 524320 | tf_op jit(solution)/shard_map/ppermute | solution.py:296
  27.7 1.8 %tree.1 = (bf16[64,128]{1,0:T(8,128)(2,1)S(1)}, bf16[64,128]{1,0:T(8,128)(2,1)S(1)}, bf16[64,128]{1,0:T(8,128)(2,1)S(1)}, bf16[64,128]{1,0:T(8,128)(2,1)S(1)}) custom-call(s32[3]{0:T(128)S(1)} %pad_add_fusion.at_ref, bf16[16,176,128]{2,1,0:T(8,128)(2,1)S(1)} %all-to-all-done.got_ref, f32[16,128,128]{2,1,0:T(8,128)} %bitcast.4, f32[256,256]{1,0:T(8,128)S(1)} %ancestors.1.reach_ref), custom_call_target="tpu_custom_call" | custom-call | flops 50331648 | bytes 720896 | tf_op jit(solution)/shard_map/tree/pallas_call | solution.py:164
  29.5 0.9 %collective-permute-start.2 = (bf16[64,128]{1,0:T(8,128)(2,1)S(1)}, bf16[64,128]{1,0:T(8,128)(2,1)S(1)}, u32[]{:S(2)}, u32[]{:S(2)}) collective-permute-start(bf16[64,128]{1,0:T(8,128)(2,1)S(1)} %get-tuple-element.19), channel_id=1, source_target_pairs={{0,1},{1,0},{2,3},{3,2},{4,5},{5,4},{6,7},{7,6},{8,9},{9,8},{10,11... | collective-permute-start | bytes 49160 | tf_op jit(solution)/shard_map/ppermute | solution.py:306
  30.4 1.5 %collective-permute-start.3 = (bf16[64,128]{1,0:T(8,128)(2,1)S(1)}, bf16[64,128]{1,0:T(8,128)(2,1)S(1)}, u32[]{:S(2)}, u32[]{:S(2)}) collective-permute-start(bf16[64,128]{1,0:T(8,128)(2,1)S(1)} %get-tuple-element.20), channel_id=1, source_target_pairs={{0,2},{2,0},{1,3},{3,1},{4,6},{6,4},{5,7},{7,5},{8,10},{10,8},{9,1... | collective-permute-start | bytes 49160 | tf_op jit(solution)/shard_map/ppermute | solution.py:307
  31.8 0.3 collective-permute-start.4
  32.1 2.3 %prefixes.1.refs_4_ = bf16[16,384,128]{2,1,0:T(8,128)(2,1)} custom-call(s32[3]{0:T(128)S(1)} %pad_add_fusion.at_ref, bf16[16,176,128]{2,1,0:T(8,128)(2,1)S(1)} %all-to-all-done.got_ref, f32[16,128,128]{2,1,0:T(8,128)} %bitcast.5), custom_call_target="tpu_custom_call" | custom-call | flops 262144 | bytes 1048576 | tf_op jit(solution)/shard_map/prefixes/pallas_call | solution.py:193
  34.4 0.0 collective-permute-done.2.refs_1_
  34.4 0.0 collective-permute-done.3.refs_2_
  34.4 0.6 collective-permute-done.4.refs_3_
  35.0 1.1 %packed.1 = bf16[16,384,128]{2,1,0:T(8,128)(2,1)} custom-call(bf16[64,128]{1,0:T(8,128)(2,1)S(1)} %get-tuple-element.18.refs_0_, bf16[64,128]{1,0:T(8,128)(2,1)S(1)} %collective-permute-done.2.refs_1_, bf16[64,128]{1,0:T(8,128)(2,1)S(1)} %collective-permute-done.3.refs_2_, ...), custom_call_target="tpu_custom_call", output_to_operand_aliasing={{}: (4, {})} | custom-call | bytes 1048576 | tf_op jit(solution)/shard_map/packed/pallas_call | solution.py:220
  36.1 6.9 %all-to-all-start.1 = ((bf16[16,384,128]{2,1,0:T(8,128)(2,1)}), bf16[16,384,128]{2,1,0:T(8,128)(2,1)S(1)}, u32[]{:S(2)}, u32[]{:S(2)}) async-start(bf16[16,384,128]{2,1,0:T(8,128)(2,1)} %packed.1), calls=%async_computation.1 | async-start | bytes 3145728 | tf_op jit(solution)/shard_map/all_to_all | solution.py:310
  43.1 0.7 collective-permute-start.5
  43.8 1.5 %collective-permute-done.5.refs_3_ = bf16[512,512]{1,0:T(8,128)(2,1)S(1)} collective-permute-done((bf16[512,512]{1,0:T(8,128)(2,1)S(1)}, bf16[512,512]{1,0:T(8,128)(2,1)S(1)}, u32[]{:S(2)}, u32[]{:S(2)}) %collective-permute-start.5) | collective-permute-done | bytes 524320 | tf_op jit(solution)/shard_map/ppermute | solution.py:302
  45.3 0.8 copy-done.2
  46.1 20.9 %all-to-all-done.1.state_ref.rows_ref = bf16[16,384,128]{2,1,0:T(8,128)(2,1)S(1)} async-done(((bf16[16,384,128]{2,1,0:T(8,128)(2,1)}), bf16[16,384,128]{2,1,0:T(8,128)(2,1)S(1)}, u32[]{:S(2)}, u32[]{:S(2)}) %all-to-all-start.1) | async-done | bytes 1572896 | tf_op jit(solution)/shard_map/all_to_all | solution.py:310
  67.0 1.0 %copy-done.3 = bf16[512,512]{1,0:T(8,128)(2,1)S(1)} copy-done((bf16[512,512]{1,0:T(8,128)(2,1)S(1)}, bf16[512,512]{1,0:T(8,128)(2,1)}, u32[]{:S(2)}) %copy-start.3) | copy-done | bytes 524312
  68.1 1.3 %project.1 = (bf16[64,512]{1,0:T(8,128)(2,1)S(1)}, bf16[64,512]{1,0:T(8,128)(2,1)S(1)}, bf16[64,512]{1,0:T(8,128)(2,1)S(1)}, bf16[64,512]{1,0:T(8,128)(2,1)S(1)}) custom-call(s32[3]{0:T(128)S(1)} %pad_add_fusion.at_ref, bf16[16,384,128]{2,1,0:T(8,128)(2,1)S(1)} %all-to-all-done.1.state_ref.rows_ref, bf16[512,512]{1,0:T(8,128)(2,1)S(1)} %copy-done.1, ...), custom_call_target="tpu_custom_call" | custom-call | flops 805306368 | bytes 3670016 | tf_op jit(solution)/shard_map/project/pallas_call | solution.py:262
  69.4 3.1 %collective-permute-start.6 = (bf16[64,512]{1,0:T(8,128)(2,1)S(1)}, bf16[64,512]{1,0:T(8,128)(2,1)S(1)}, u32[]{:S(2)}, u32[]{:S(2)}) collective-permute-start(bf16[64,512]{1,0:T(8,128)(2,1)S(1)} %get-tuple-element.25), channel_id=1, source_target_pairs={{0,4},{4,8},{8,12},{12,0},{1,5},{5,9},{9,13},{13,1},{2,6},{6,10},{... | collective-permute-start | bytes 196616 | tf_op jit(solution)/shard_map/ppermute | solution.py:318
  72.4 4.9 %collective-permute-start.7 = (bf16[64,512]{1,0:T(8,128)(2,1)S(1)}, bf16[64,512]{1,0:T(8,128)(2,1)S(1)}, u32[]{:S(2)}, u32[]{:S(2)}) collective-permute-start(bf16[64,512]{1,0:T(8,128)(2,1)S(1)} %get-tuple-element.26), channel_id=1, source_target_pairs={{0,8},{4,12},{8,0},{12,4},{1,9},{5,13},{9,1},{13,5},{2,10},{6,14},... | collective-permute-start | bytes 196616 | tf_op jit(solution)/shard_map/ppermute | solution.py:318
  77.3 2.4 %collective-permute-start.8 = (bf16[64,512]{1,0:T(8,128)(2,1)S(1)}, bf16[64,512]{1,0:T(8,128)(2,1)S(1)}, u32[]{:S(2)}, u32[]{:S(2)}) collective-permute-start(bf16[64,512]{1,0:T(8,128)(2,1)S(1)} %get-tuple-element.27), channel_id=1, source_target_pairs={{0,12},{4,0},{8,4},{12,8},{1,13},{5,1},{9,5},{13,9},{2,14},{6,2},{... | collective-permute-start | bytes 196616 | tf_op jit(solution)/shard_map/ppermute | solution.py:318
  79.7 5.5 %finish.1 = bf16[4,512,512]{2,1,0:T(8,128)(2,1)} custom-call(bf16[4,512,512]{2,1,0:T(8,128)(2,1)} %q_ref.3, f32[4,512,512]{2,1,0:T(8,128)} %inside.1.inner_ref, bf16[16,384,128]{2,1,0:T(8,128)(2,1)S(1)} %all-to-all-done.1.state_ref.rows_ref), custom_call_target="tpu_custom_call" | custom-call | flops 268435456 | bytes 8388608 | tf_op jit(solution)/shard_map/finish/pallas_call | solution.py:128
  85.3 0.0 collective-permute-done.6
  85.3 0.7 add_convert_fusion
  (9 shorter events, 0.0 us)
Async XLA Ops:
  0.6 14.9 %copy-start = (s32[4,256]{1,0:T(4,128)S(1)}, s32[4,256]{1,0:T(4,128)}, u32[]{:S(2)}) copy-start(s32[4,256]{1,0:T(4,128)} %param.16) | copy-start | bytes 12292
  0.6 12.2 %copy-start.1 = (bf16[512,512]{1,0:T(8,128)(2,1)S(1)}, bf16[512,512]{1,0:T(8,128)(2,1)}, u32[]{:S(2)}) copy-start(bf16[512,512]{1,0:T(8,128)(2,1)} %refs_0_.1) | copy-start | bytes 1572868
  5.3 22.4 %all-to-all-start = ((bf16[16,176,128]{2,1,0:T(8,128)(2,1)}), bf16[16,176,128]{2,1,0:T(8,128)(2,1)S(1)}, u32[]{:S(2)}, u32[]{:S(2)}) async-start(bf16[16,176,128]{2,1,0:T(8,128)(2,1)} %block_states.1), calls=%async_computation | async-start | bytes 1441792 | tf_op jit(solution)/shard_map/all_to_all | solution.py:294
  12.9 12.9 %collective-permute-start = (bf16[512,512]{1,0:T(8,128)(2,1)S(1)}, bf16[512,512]{1,0:T(8,128)(2,1)S(1)}, u32[]{:S(2)}, u32[]{:S(2)}) collective-permute-start(bf16[512,512]{1,0:T(8,128)(2,1)S(1)} %copy-done.1), channel_id=1, source_target_pairs={{0,1},{1,0},{2,3},{3,2},{4,5},{5,4},{6,7},{7,6},{8,9},{9,8},{10,11... | collective-permute-start | bytes 1572872 | tf_op jit(solution)/shard_map/ppermute | solution.py:297
  13.9 13.7 %collective-permute-start.1 = (bf16[512,512]{1,0:T(8,128)(2,1)S(1)}, bf16[512,512]{1,0:T(8,128)(2,1)S(1)}, u32[]{:S(2)}, u32[]{:S(2)}) collective-permute-start(bf16[512,512]{1,0:T(8,128)(2,1)S(1)} %copy-done.1), channel_id=1, source_target_pairs={{0,2},{2,0},{1,3},{3,1},{4,6},{6,4},{5,7},{7,5},{8,10},{10,8},{9,1... | collective-permute-start | bytes 1572872 | tf_op jit(solution)/shard_map/ppermute | solution.py:296
  29.5 4.9 %collective-permute-start.2 = (bf16[64,128]{1,0:T(8,128)(2,1)S(1)}, bf16[64,128]{1,0:T(8,128)(2,1)S(1)}, u32[]{:S(2)}, u32[]{:S(2)}) collective-permute-start(bf16[64,128]{1,0:T(8,128)(2,1)S(1)} %get-tuple-element.19), channel_id=1, source_target_pairs={{0,1},{1,0},{2,3},{3,2},{4,5},{5,4},{6,7},{7,6},{8,9},{9,8},{10,11... | collective-permute-start | bytes 49160 | tf_op jit(solution)/shard_map/ppermute | solution.py:306
  30.4 4.0 %collective-permute-start.3 = (bf16[64,128]{1,0:T(8,128)(2,1)S(1)}, bf16[64,128]{1,0:T(8,128)(2,1)S(1)}, u32[]{:S(2)}, u32[]{:S(2)}) collective-permute-start(bf16[64,128]{1,0:T(8,128)(2,1)S(1)} %get-tuple-element.20), channel_id=1, source_target_pairs={{0,2},{2,0},{1,3},{3,1},{4,6},{6,4},{5,7},{7,5},{8,10},{10,8},{9,1... | collective-permute-start | bytes 49160 | tf_op jit(solution)/shard_map/ppermute | solution.py:307
  31.8 3.2 %collective-permute-start.4 = (bf16[64,128]{1,0:T(8,128)(2,1)S(1)}, bf16[64,128]{1,0:T(8,128)(2,1)S(1)}, u32[]{:S(2)}, u32[]{:S(2)}) collective-permute-start(bf16[64,128]{1,0:T(8,128)(2,1)S(1)} %get-tuple-element.21), channel_id=1, source_target_pairs={{0,3},{1,2},{2,1},{3,0},{4,7},{5,6},{6,5},{7,4},{8,11},{9,10},{10,... | collective-permute-start | bytes 49160 | tf_op jit(solution)/shard_map/ppermute | solution.py:308
  36.1 30.9 %all-to-all-start.1 = ((bf16[16,384,128]{2,1,0:T(8,128)(2,1)}), bf16[16,384,128]{2,1,0:T(8,128)(2,1)S(1)}, u32[]{:S(2)}, u32[]{:S(2)}) async-start(bf16[16,384,128]{2,1,0:T(8,128)(2,1)} %packed.1), calls=%async_computation.1 | async-start | bytes 3145728 | tf_op jit(solution)/shard_map/all_to_all | solution.py:310
  43.1 2.3 %collective-permute-start.5 = (bf16[512,512]{1,0:T(8,128)(2,1)S(1)}, bf16[512,512]{1,0:T(8,128)(2,1)S(1)}, u32[]{:S(2)}, u32[]{:S(2)}) collective-permute-start(bf16[512,512]{1,0:T(8,128)(2,1)S(1)} %collective-permute-done.1.refs_2_), channel_id=1, source_target_pairs={{0,1},{1,0},{2,3},{3,2},{4,5},{5,4},{6,7},{7,6},{8,9},{9,8},{10,11... | collective-permute-start | bytes 1572872 | tf_op jit(solution)/shard_map/ppermute | solution.py:302
  45.3 0.8 copy-start.2
  67.0 1.0 %copy-start.3 = (bf16[512,512]{1,0:T(8,128)(2,1)S(1)}, bf16[512,512]{1,0:T(8,128)(2,1)}, u32[]{:S(2)}) copy-start(bf16[512,512]{1,0:T(8,128)(2,1)} %copy-done.2) | copy-start | bytes 1572868
  69.4 15.9 %collective-permute-start.6 = (bf16[64,512]{1,0:T(8,128)(2,1)S(1)}, bf16[64,512]{1,0:T(8,128)(2,1)S(1)}, u32[]{:S(2)}, u32[]{:S(2)}) collective-permute-start(bf16[64,512]{1,0:T(8,128)(2,1)S(1)} %get-tuple-element.25), channel_id=1, source_target_pairs={{0,4},{4,8},{8,12},{12,0},{1,5},{5,9},{9,13},{13,1},{2,6},{6,10},{... | collective-permute-start | bytes 196616 | tf_op jit(solution)/shard_map/ppermute | solution.py:318
  72.4 12.9 %collective-permute-start.7 = (bf16[64,512]{1,0:T(8,128)(2,1)S(1)}, bf16[64,512]{1,0:T(8,128)(2,1)S(1)}, u32[]{:S(2)}, u32[]{:S(2)}) collective-permute-start(bf16[64,512]{1,0:T(8,128)(2,1)S(1)} %get-tuple-element.26), channel_id=1, source_target_pairs={{0,8},{4,12},{8,0},{12,4},{1,9},{5,13},{9,1},{13,5},{2,10},{6,14},... | collective-permute-start | bytes 196616 | tf_op jit(solution)/shard_map/ppermute | solution.py:318
  77.3 8.0 %collective-permute-start.8 = (bf16[64,512]{1,0:T(8,128)(2,1)S(1)}, bf16[64,512]{1,0:T(8,128)(2,1)S(1)}, u32[]{:S(2)}, u32[]{:S(2)}) collective-permute-start(bf16[64,512]{1,0:T(8,128)(2,1)S(1)} %get-tuple-element.27), channel_id=1, source_target_pairs={{0,12},{4,0},{8,4},{12,8},{1,13},{5,1},{9,5},{13,9},{2,14},{6,2},{... | collective-permute-start | bytes 196616 | tf_op jit(solution)/shard_map/ppermute | solution.py:318

commit v3 on v2

--- a/solution.py
+++ b/solution.py
@@ -96,7 +96,7 @@
             at = part * half + lax.broadcasted_iota(jnp.int32, scores.shape, 0)
             other = lax.broadcasted_iota(jnp.int32, scores.shape, 1)
             weights = jnp.where(at >= other, scores, 0.0).astype(BF)
-            o_ref[0, rows, cols] = mm(weights, v_ref[0, 0:upto, cols], 1, 0)
+            o_ref[0, rows, cols] = mm(weights, v_ref[0, 0:upto, cols], 1, 0).astype(BF)
 
 
 def inside(q, k, v):
@@ -107,7 +107,7 @@
         grid=(requests,),
         in_specs=[big, big, big],
         out_specs=big,
-        out_shape=pltpu.HBM(q.shape, F32),
+        out_shape=pltpu.HBM(q.shape, BF),
         cost_estimate=cost(3 * requests * tokens * tokens * width, 10 * requests * tokens * width),
         compiler_params=room(24),
         name="inside",
@@ -117,7 +117,7 @@
 def finish_body(q_ref, inner_ref, state_ref, o_ref):
     for h in range(state_ref.shape[0]):
         cols = slice(h * DH, (h + 1) * DH)
-        raw = mm(q_ref[0, :, cols], state_ref[h], 1, 0) + inner_ref[0, :, cols]
+        raw = mm(q_ref[0, :, cols], state_ref[h], 1, 0) + inner_ref[0, :, cols].astype(F32)
         o_ref[0, :, cols] = normed(raw).astype(BF)
 
 
@@ -137,11 +137,19 @@
     )(far(q), far(inner), states)
 
 
+def smem():
+    return pl.BlockSpec(memory_space=pltpu.SMEM)
+
+
+def vmem(count):
+    return [pl.BlockSpec(memory_space=pltpu.VMEM)] * count
+
+
 def tree_body(at_ref, got_ref, prior_ref, reach_ref, *refs):
     outs, hold = refs[:-1], refs[-1]
     peers = got_ref.shape[0]
     nodes = NODES // peers
-    total = prior_ref[0]
+    total = prior_ref[...]
     for s in range(peers):
         total = total + got_ref[s, 0:DH, :].astype(F32)
 
@@ -154,65 +162,50 @@
     raw = mm(q, total.astype(BF), 1, 0) + mm(weights, v, 1, 0)
     hold[...] = normed(raw).astype(BF).reshape(hold.shape)
     for j, out in enumerate(outs):
-        out[...] = hold[at_ref[1] ^ j]
+        out[...] = hold[at_ref[0] ^ j]
 
 
 def tree(at, got, prior, reach, groups):
     rows = NODES // groups
-    whole = lambda a: pl.BlockSpec(a.shape, lambda i, at: (0,) * a.ndim)
-    out = jax.ShapeDtypeStruct((rows, DH), BF)
     return pl.pallas_call(
         tree_body,
-        grid_spec=pltpu.PrefetchScalarGridSpec(
-            num_scalar_prefetch=1,
-            grid=(1,),
-            in_specs=[
-                whole(got),
-                pl.BlockSpec((1, DH, DH), lambda i, at: (at[0], 0, 0)),
-                whole(reach),
-            ],
-            out_specs=[whole(out)] * groups,
-            scratch_shapes=[pltpu.VMEM((groups, rows, DH), BF)],
-        ),
-        out_shape=[out] * groups,
+        in_specs=[smem()] + vmem(3),
+        out_specs=vmem(groups),
+        scratch_shapes=[pltpu.VMEM((groups, rows, DH), BF)],
+        out_shape=[jax.ShapeDtypeStruct((rows, DH), BF)] * groups,
         cost_estimate=cost(6 * NODES * NODES * DH, got.size * 2),
-        compiler_params=room(8),
+        compiler_params=room(4),
         name="tree",
-    )(at, got, far(prior), reach)
-
-
-def prefix_body(at_ref, got_ref, prior_ref, o_ref):
-    running = prior_ref[0]
+    )(at, got, prior, reach)
+
+
+def prefix_body(got_ref, prior_ref, o_ref):
+    running = prior_ref[...]
     for s in range(got_ref.shape[0]):
         o_ref[s] = running.astype(BF)
         running = running + got_ref[s, 0:DH, :].astype(F32)
 
 
-def prefixes(at, got, prior):
+def prefixes(got, prior):
     peers = got.shape[0]
     return pl.pallas_call(
         prefix_body,
-        grid_spec=pltpu.PrefetchScalarGridSpec(
-            num_scalar_prefetch=1,
-            grid=(1,),
-            in_specs=[
-                pl.BlockSpec(got.shape, lambda i, at: (0, 0, 0)),
-                pl.BlockSpec((1, DH, DH), lambda i, at: (at[0], 0, 0)),
-            ],
-            out_specs=pl.BlockSpec((peers, DH, DH), lambda i, at: (0, 2, 0)),
-        ),
-        out_shape=jax.ShapeDtypeStruct((peers, NODES + DH, DH), BF),
+        grid=(1,),
+        in_specs=vmem(2),
+        out_specs=pl.BlockSpec((peers, DH, DH), lambda i: (0, NODES // DH, 0)),
+        out_shape=pltpu.HBM((peers, NODES + DH, DH), BF),
         cost_estimate=cost(peers * DH * DH, peers * DH * DH * 4),
-        compiler_params=room(8),
+        compiler_params=room(4),
         name="prefixes",
-    )(at, got, far(prior))
+    )(got, prior)
 
 
 def pack_body(*refs):
     pieces, o_ref = refs[:-2], refs[-1]
-    for s in range(o_ref.shape[0]):
-        for j, piece in enumerate(pieces):
-            o_ref[s, j * piece.shape[0] : (j + 1) * piece.shape[0], :] = piece[...]
+    for j, piece in enumerate(pieces):
+        block = piece[...]
+        for s in range(o_ref.shape[0]):
+            o_ref[s, j * piece.shape[0] : (j + 1) * piece.shape[0], :] = block
 
 
 def packed(pieces, onto):
@@ -220,58 +213,68 @@
     return pl.pallas_call(
         pack_body,
         grid=(1,),
-        in_specs=[pl.BlockSpec(p.shape, lambda i: (0, 0)) for p in pieces]
-        + [pl.BlockSpec(memory_space=pl.ANY)],
+        in_specs=vmem(len(pieces)) + [pl.BlockSpec(memory_space=pltpu.HBM)],
         out_specs=pl.BlockSpec((peers, NODES, DH), lambda i: (0, 0, 0)),
-        out_shape=jax.ShapeDtypeStruct(onto.shape, BF),
+        out_shape=pltpu.HBM(onto.shape, BF),
         input_output_aliases={len(pieces): 0},
         cost_estimate=cost(0, peers * NODES * DH * 2),
-        compiler_params=room(8),
+        compiler_params=room(4),
         name="packed",
     )(*pieces, onto)
 
 
 def project_body(at_ref, rows_ref, *refs):
-    groups = (len(refs) - 1) // 2
-    weights, outs, hold = refs[:groups], refs[groups:-1], refs[-1]
+    groups = (len(refs) - 3) // 2
+    weights, outs = refs[:groups], refs[groups:-3]
+    hold, slab, sems = refs[-3:]
     requests = len(outs)
     heads = rows_ref.shape[0] // requests
     nodes = outs[0].shape[0]
+    copies = [
+        pltpu.make_async_copy(weights[j], slab.at[j], sems.at[j]) for j in range(groups)
+    ]
+    for copy in copies:
+        copy.start()
     total = None
     for j in range(groups):
         lhs = jnp.concatenate(
             [
-                jnp.concatenate([rows_ref[r * heads + h, j * nodes : (j + 1) * nodes, :] for h in range(heads)], axis=1)
+                jnp.concatenate(
+                    [
+                        rows_ref[r * heads + h, j * nodes : (j + 1) * nodes, :]
+                        for h in range(heads)
+                    ],
+                    axis=1,
+                )
                 for r in range(requests)
             ],
             axis=0,
         )
-        part = mm(lhs, weights[j][...], 1, 0)
+        copies[j].wait()
+        part = mm(lhs, slab[j], 1, 0)
         total = part if total is None else total + part
     hold[...] = total.astype(BF).reshape(hold.shape)
     for s, out in enumerate(outs):
-        out[...] = hold[(at_ref[2] + s) % requests]
+        out[...] = hold[(at_ref[1] + s) % requests]
 
 
 def project(at, rows, weights, requests):
     groups = len(weights)
     nodes = NODES // groups
-    wide = weights[0].shape[1]
-    whole = lambda a: pl.BlockSpec(a.shape, lambda i, at: (0,) * a.ndim)
-    out = jax.ShapeDtypeStruct((nodes, wide), BF)
+    deep, wide = weights[0].shape
+    peers = rows.shape[0]
     return pl.pallas_call(
         project_body,
-        grid_spec=pltpu.PrefetchScalarGridSpec(
-            num_scalar_prefetch=1,
-            grid=(1,),
-            in_specs=[pl.BlockSpec((rows.shape[0], NODES, DH), lambda i, at: (0, 0, 0))]
-            + [whole(w) for w in weights],
-            out_specs=[whole(out)] * requests,
-            scratch_shapes=[pltpu.VMEM((requests, nodes, wide), BF)],
-        ),
-        out_shape=[out] * requests,
-        cost_estimate=cost(2 * rows.size * wide, 2 * rows.size + 2 * groups * weights[0].size),
-        compiler_params=room(16),
+        in_specs=[smem()] + vmem(1) + [pl.BlockSpec(memory_space=pl.ANY)] * groups,
+        out_specs=vmem(requests),
+        scratch_shapes=[
+            pltpu.VMEM((requests, nodes, wide), BF),
+            pltpu.VMEM((groups, deep, wide), BF),
+            pltpu.SemaphoreType.DMA((groups,)),
+        ],
+        out_shape=[jax.ShapeDtypeStruct((nodes, wide), BF)] * requests,
+        cost_estimate=cost(2 * peers * NODES * DH * wide, 2 * rows.size + 2 * groups * deep * wide),
+        compiler_params=room(8),
         name="project",
     )(at, rows, *weights)
 
@@ -280,10 +283,9 @@
     requests, tokens, width = q.shape
     heads = width // DH
     y = lax.axis_index("y")
-    seq_index = lax.axis_index(SEQ)
     zp = lax.axis_index("zp")
     group = lax.axis_index("zl") * 2 + lax.axis_index("c")
-    at = jnp.stack([seq_index, group, zp]).astype(jnp.int32)
+    at = jnp.stack([group, zp]).astype(jnp.int32)
     pairs = lax.axis_size("zp")
 
     swap = [(0, 1), (1, 0)]
@@ -295,21 +297,22 @@
 
     w_z = lax.ppermute(weight, "zl", swap)
     w_c = lax.ppermute(weight, "c", swap)
-
     reach = ancestors(lax.dynamic_slice_in_dim(parents, y, 1, 0))
-    inner = inside(q, k, v)
-    got, w_c, w_z, reach, inner = lax.optimization_barrier((got, w_c, w_z, reach, inner))
-    w_zc = lax.ppermute(w_z, "c", swap)
-
     flat_prior = prior.reshape(requests * heads, DH, DH)
-    mine, for_c, for_z, for_zc = tree(at, got, flat_prior, reach, 4)
+    own_prior = lax.dynamic_index_in_dim(flat_prior, lax.axis_index(SEQ), 0, keepdims=False)
+    got, reach, own_prior = lax.optimization_barrier((got, reach, own_prior))
+
+    mine, for_c, for_z, for_zc = tree(at, got, own_prior, reach, 4)
     from_c = lax.ppermute(for_c, "c", swap)
     from_z = lax.ppermute(for_z, "zl", swap)
     from_zc = lax.ppermute(for_zc, quad, crossed)
-    behind = prefixes(at, got, flat_prior)
-    rows = lax.all_to_all(
-        packed((mine, from_c, from_z, from_zc), behind), SEQ, 0, 0, tiled=True
-    )
+    behind = prefixes(got, own_prior)
+    full = packed((mine, from_c, from_z, from_zc), behind)
+    full, q, k, v, w_z = lax.optimization_barrier((full, q, k, v, w_z))
+    rows = lax.all_to_all(full, SEQ, 0, 0, tiled=True)
+    w_zc = lax.ppermute(w_z, "c", swap)
+    inner = inside(q, k, v)
+    rows, inner = lax.optimization_barrier((rows, inner))
 
     parts = project(at, rows, (weight, w_c, w_z, w_zc), requests)
     total = parts[0].astype(F32)

time: 86.6 us -> 83.7 us (0.967)
  starting transfers between devices: 30.9 us -> 27.2 us
  waiting for transfers between devices: 25 us -> 26.9 us
  Pallas kernels: 26.8 us -> 25 us
    all_to_all x1, waiting for transfers between devices: 0.01 us -> 8.42 us  [on_device(): got = lax.all_to_all(sent, SEQ, 0, 0, tiled=True)]
    all_to_all x1, waiting for transfers between devices: 20.9 us -> 16.3 us  [on_device(): rows = lax.all_to_all(full, SEQ, 0, 0, tiled=True)]
    all_to_all x1, starting transfers between devices: 6.93 us -> 3.71 us  [on_device(): rows = lax.all_to_all(full, SEQ, 0, 0, tiled=True)]
    ppermute x1, waiting for transfers between devices: 1.9 us -> 0.01 us  [on_device(): w_z = lax.ppermute(weight, 'zl', swap)]
    ppermute x1, waiting for transfers between devices: 1.54 us -> 0.01 us  [on_device(): w_zc = lax.ppermute(w_z, 'c', swap)]
    ppermute x1, waiting for transfers between devices: 0.63 us -> 2.04 us  [on_device(): from_zc = lax.ppermute(for_zc, quad, crossed)]
    ppermute x1, starting transfers between devices: 0.87 us -> 2.23 us  [on_device(): from_c = lax.ppermute(for_c, 'c', swap)]
    pallas_call x4, Pallas kernels: 6.49 us -> 5.56 us  [the longest x1 2.51 us: project(): pl.pallas_call(project_body, in_specs=[smem()] + vmem(1) + [pl.BlockSpec(...]
  transfers between devices with their start and end apart: 11 -> 11, of which waited for: 4 -> 4; matrix products, arithmetic and copies ran while one was open for 0% -> 1% of each run, Pallas kernels for 21% -> 21%
where the time goes in v3:
time: 83.7 us; the launch traced here: 83.2 us
  starting transfers between devices  27.2 us (32%)
  waiting for transfers between devices  26.9 us (32%)
  Pallas kernels  25 us (30%)
  local copies, waits for them, and re-layouts  2.55 us (3%)
    all_to_all x1, waiting for transfers between devices, on_device(): rows = lax.all_to_all(full, SEQ, 0, 0, tiled=True)  16.3 us
    ppermute x3, starting transfers between devices, on_device(): total = total + lax.ppermute(parts[s], 'zp', ring).astype(F32)  9.66 us
    all_to_all x1, waiting for transfers between devices, on_device(): got = lax.all_to_all(sent, SEQ, 0, 0, tiled=True)  8.42 us
    pallas_call x1, Pallas kernels, inside(): pl.pallas_call(inner_body, grid=(requests,), in_specs=[big, big, big], ou...  8.08 us
    all_to_all x1, starting transfers between devices, on_device(): got = lax.all_to_all(sent, SEQ, 0, 0, tiled=True)  7.57 us
    pallas_call x1, Pallas kernels, finish(): pl.pallas_call(finish_body, grid=(requests,), in_specs=[big, big, pl.Bloc...  5.08 us
    pallas_call x1, Pallas kernels, block_states(): pl.pallas_call(states_body, grid=(requests,), in_specs=[big, big, small,...  4.69 us
    all_to_all x1, starting transfers between devices, on_device(): rows = lax.all_to_all(full, SEQ, 0, 0, tiled=True)  3.71 us
  transfers between devices with their start and end apart: 11, of which 4 were waited for; matrix products, arithmetic and copies ran while one was open for 1% of the time, Pallas kernels for 21%

profile of v3, /device:TPU:1, one launch (start us, length us, event | category | flops | bytes accessed | tf_op | source)
XLA Modules:
  0.0 83.2 jit_solution(10583306065126065698)
XLA Ops:
  0.6 0.0 copy-start
  0.7 4.7 %block_states.1 = bf16[16,176,128]{2,1,0:T(8,128)(2,1)} custom-call(bf16[4,512,512]{2,1,0:T(8,128)(2,1)} %k_ref.2, bf16[4,512,512]{2,1,0:T(8,128)(2,1)} %v_ref.2, bf16[4,16,512]{2,1,0:T(8,128)(2,1)} %tq_ref.1, bf16[4,16,512]{2,1,0:T(8,128)(2,1)} %tk_ref.1, bf16[4,16,512]{2,1,0:T(8,128)(2,1)} %tv_ref.1), custom_call_target="tpu_custom_call" | custom-call | flops 268435456 | bytes 4194304 | tf_op jit(solution)/shard_map/block_states/pallas_call | solution.py:55
  5.3 7.6 %all-to-all-start = ((bf16[16,176,128]{2,1,0:T(8,128)(2,1)}), bf16[16,176,128]{2,1,0:T(8,128)(2,1)S(1)}, u32[]{:S(2)}, u32[]{:S(2)}) async-start(bf16[16,176,128]{2,1,0:T(8,128)(2,1)} %block_states.1), calls=%async_computation | async-start | bytes 1441792 | tf_op jit(solution)/shard_map/all_to_all | solution.py:296
  12.9 1.7 %collective-permute-start.3 = (bf16[512,512]{1,0:T(8,128)(2,1)S(1)}, bf16[512,512]{1,0:T(8,128)(2,1)S(1)}, u32[]{:S(2)}, u32[]{:S(2)}) collective-permute-start(bf16[512,512]{1,0:T(8,128)(2,1)S(1)} %copy-done.1), channel_id=1, source_target_pairs={{0,2},{2,0},{1,3},{3,1},{4,6},{6,4},{5,7},{7,5},{8,10},{10,8},{9,1... | collective-permute-start | bytes 1572872 | tf_op jit(solution)/shard_map/ppermute | solution.py:298
  14.7 0.7 constant_dynamic-slice_fusion.parents_ref
  15.4 1.6 %ancestors.1.reach_ref = f32[256,256]{1,0:T(8,128)S(1)} custom-call(s32[1,256]{1,0:T(1,128)S(1)} %constant_dynamic-slice_fusion.parents_ref), custom_call_target="tpu_custom_call" | custom-call | flops 268435456 | bytes 262144 | tf_op jit(solution)/shard_map/ancestors/pallas_call | solution.py:78
  16.9 0.1 pad_add_fusion.at_ref
  17.0 8.4 %all-to-all-done.got_ref = bf16[16,176,128]{2,1,0:T(8,128)(2,1)S(1)} async-done(((bf16[16,176,128]{2,1,0:T(8,128)(2,1)}), bf16[16,176,128]{2,1,0:T(8,128)(2,1)S(1)}, u32[]{:S(2)}, u32[]{:S(2)}) %all-to-all-start) | async-done | bytes 720928 | tf_op jit(solution)/shard_map/all_to_all | solution.py:296
  25.5 1.0 %tree.1 = (bf16[64,128]{1,0:T(8,128)(2,1)S(1)}, bf16[64,128]{1,0:T(8,128)(2,1)S(1)}, bf16[64,128]{1,0:T(8,128)(2,1)S(1)}, bf16[64,128]{1,0:T(8,128)(2,1)S(1)}) custom-call(s32[2]{0:T(128)S(1)} %pad_add_fusion.at_ref, bf16[16,176,128]{2,1,0:T(8,128)(2,1)S(1)} %all-to-all-done.got_ref, f32[128,128]{1,0:T(8,128)S(1)} %dynamic-slice_bitcast_fusion.prior_ref, ...), custom_call_target="tpu_custom_call" | custom-call | flops 50331648 | bytes 720896 | tf_op jit(solution)/shard_map/tree/pallas_call | solution.py:170
  26.5 2.2 %collective-permute-start = (bf16[64,128]{1,0:T(8,128)(2,1)S(1)}, bf16[64,128]{1,0:T(8,128)(2,1)S(1)}, u32[]{:S(2)}, u32[]{:S(2)}) collective-permute-start(bf16[64,128]{1,0:T(8,128)(2,1)S(1)} %get-tuple-element.24), channel_id=1, source_target_pairs={{0,1},{1,0},{2,3},{3,2},{4,5},{5,4},{6,7},{7,6},{8,9},{9,8},{10,11... | collective-permute-start | bytes 49160 | tf_op jit(solution)/shard_map/ppermute | solution.py:306
  28.7 1.6 %collective-permute-start.1 = (bf16[64,128]{1,0:T(8,128)(2,1)S(1)}, bf16[64,128]{1,0:T(8,128)(2,1)S(1)}, u32[]{:S(2)}, u32[]{:S(2)}) collective-permute-start(bf16[64,128]{1,0:T(8,128)(2,1)S(1)} %get-tuple-element.25), channel_id=1, source_target_pairs={{0,2},{2,0},{1,3},{3,1},{4,6},{6,4},{5,7},{7,5},{8,10},{10,8},{9,1... | collective-permute-start | bytes 49160 | tf_op jit(solution)/shard_map/ppermute | solution.py:307
  30.3 0.1 collective-permute-start.2
  30.4 0.9 %prefixes.1.refs_4_ = bf16[16,384,128]{2,1,0:T(8,128)(2,1)} custom-call(bf16[16,176,128]{2,1,0:T(8,128)(2,1)S(1)} %all-to-all-done.got_ref, f32[128,128]{1,0:T(8,128)S(1)} %dynamic-slice_bitcast_fusion.prior_ref), custom_call_target="tpu_custom_call" | custom-call | flops 262144 | bytes 1048576 | tf_op jit(solution)/shard_map/prefixes/pallas_call | solution.py:191
  31.3 0.0 collective-permute-done.refs_1_
  31.3 0.1 collective-permute-done.1.refs_2_
  31.5 2.0 %collective-permute-done.2.refs_3_ = bf16[64,128]{1,0:T(8,128)(2,1)S(1)} collective-permute-done((bf16[64,128]{1,0:T(8,128)(2,1)S(1)}, bf16[64,128]{1,0:T(8,128)(2,1)S(1)}, u32[]{:S(2)}, u32[]{:S(2)}) %collective-permute-start.2) | collective-permute-done | bytes 16416 | tf_op jit(solution)/shard_map/ppermute | solution.py:308
  33.5 1.2 %packed.1 = bf16[16,384,128]{2,1,0:T(8,128)(2,1)} custom-call(bf16[64,128]{1,0:T(8,128)(2,1)S(1)} %get-tuple-element.23.refs_0_, bf16[64,128]{1,0:T(8,128)(2,1)S(1)} %collective-permute-done.refs_1_, bf16[64,128]{1,0:T(8,128)(2,1)S(1)} %collective-permute-done.1.refs_2_, ...), custom_call_target="tpu_custom_call", output_to_operand_aliasing={{}: (4, {})} | custom-call | bytes 1048576 | tf_op jit(solution)/shard_map/packed/pallas_call | solution.py:213
  34.7 0.0 collective-permute-done.3.refs_2_
  34.7 0.8 copy-done.2
  35.5 3.7 %all-to-all-start.1 = ((bf16[16,384,128]{2,1,0:T(8,128)(2,1)}), bf16[16,384,128]{2,1,0:T(8,128)(2,1)S(1)}, u32[]{:S(2)}, u32[]{:S(2)}) async-start(bf16[16,384,128]{2,1,0:T(8,128)(2,1)} %packed.1), calls=%async_computation.1 | async-start | bytes 3145728 | tf_op jit(solution)/shard_map/all_to_all | solution.py:312
  39.2 0.5 collective-permute-start.4
  39.7 0.1 collective-permute-start.5
  39.8 8.1 %inside.1.inner_ref = bf16[4,512,512]{2,1,0:T(8,128)(2,1)} custom-call(bf16[4,512,512]{2,1,0:T(8,128)(2,1)} %q_ref.1, bf16[4,512,512]{2,1,0:T(8,128)(2,1)} %k_ref.2, bf16[4,512,512]{2,1,0:T(8,128)(2,1)} %v_ref.2), custom_call_target="tpu_custom_call" | custom-call | flops 1610612736 | bytes 10485760 | tf_op jit(solution)/shard_map/inside/pallas_call | solution.py:105
  47.9 16.3 %all-to-all-done.1.state_ref.rows_ref = bf16[16,384,128]{2,1,0:T(8,128)(2,1)S(1)} async-done(((bf16[16,384,128]{2,1,0:T(8,128)(2,1)}), bf16[16,384,128]{2,1,0:T(8,128)(2,1)S(1)}, u32[]{:S(2)}, u32[]{:S(2)}) %all-to-all-start.1) | async-done | bytes 1572896 | tf_op jit(solution)/shard_map/all_to_all | solution.py:312
  64.2 0.0 collective-permute-done.4.refs_1_
  64.2 1.0 %copy-done.3 = bf16[512,512]{1,0:T(8,128)(2,1)S(1)} copy-done((bf16[512,512]{1,0:T(8,128)(2,1)S(1)}, bf16[512,512]{1,0:T(8,128)(2,1)}, u32[]{:S(2)}) %copy-start.3) | copy-done | bytes 524312
  65.2 2.5 %project.1 = (bf16[64,512]{1,0:T(8,128)(2,1)S(1)}, bf16[64,512]{1,0:T(8,128)(2,1)S(1)}, bf16[64,512]{1,0:T(8,128)(2,1)S(1)}, bf16[64,512]{1,0:T(8,128)(2,1)S(1)}) custom-call(s32[2]{0:T(128)S(1)} %pad_add_fusion.at_ref, bf16[16,384,128]{2,1,0:T(8,128)(2,1)S(1)} %all-to-all-done.1.state_ref.rows_ref, bf16[512,512]{1,0:T(8,128)(2,1)S(1)} %copy-done.1, ...), custom_call_target="tpu_custom_call" | custom-call | flops 536870912 | bytes 3670016 | tf_op jit(solution)/shard_map/project/pallas_call | solution.py:266
  67.7 3.1 %collective-permute-start.6 = (bf16[64,512]{1,0:T(8,128)(2,1)S(1)}, bf16[64,512]{1,0:T(8,128)(2,1)S(1)}, u32[]{:S(2)}, u32[]{:S(2)}) collective-permute-start(bf16[64,512]{1,0:T(8,128)(2,1)S(1)} %get-tuple-element.35), channel_id=1, source_target_pairs={{0,4},{4,8},{8,12},{12,0},{1,5},{5,9},{9,13},{13,1},{2,6},{6,10},{... | collective-permute-start | bytes 196616 | tf_op jit(solution)/shard_map/ppermute | solution.py:321
  70.8 4.2 %collective-permute-start.7 = (bf16[64,512]{1,0:T(8,128)(2,1)S(1)}, bf16[64,512]{1,0:T(8,128)(2,1)S(1)}, u32[]{:S(2)}, u32[]{:S(2)}) collective-permute-start(bf16[64,512]{1,0:T(8,128)(2,1)S(1)} %get-tuple-element.36), channel_id=1, source_target_pairs={{0,8},{4,12},{8,0},{12,4},{1,9},{5,13},{9,1},{13,5},{2,10},{6,14},... | collective-permute-start | bytes 196616 | tf_op jit(solution)/shard_map/ppermute | solution.py:321
  75.0 2.4 %collective-permute-start.8 = (bf16[64,512]{1,0:T(8,128)(2,1)S(1)}, bf16[64,512]{1,0:T(8,128)(2,1)S(1)}, u32[]{:S(2)}, u32[]{:S(2)}) collective-permute-start(bf16[64,512]{1,0:T(8,128)(2,1)S(1)} %get-tuple-element.37), channel_id=1, source_target_pairs={{0,12},{4,0},{8,4},{12,8},{1,13},{5,1},{9,5},{13,9},{2,14},{6,2},{... | collective-permute-start | bytes 196616 | tf_op jit(solution)/shard_map/ppermute | solution.py:321
  77.4 5.1 %finish.1 = bf16[4,512,512]{2,1,0:T(8,128)(2,1)} custom-call(bf16[4,512,512]{2,1,0:T(8,128)(2,1)} %q_ref.1, bf16[4,512,512]{2,1,0:T(8,128)(2,1)} %inside.1.inner_ref, bf16[16,384,128]{2,1,0:T(8,128)(2,1)S(1)} %all-to-all-done.1.state_ref.rows_ref), custom_call_target="tpu_custom_call" | custom-call | flops 268435456 | bytes 8388608 | tf_op jit(solution)/shard_map/finish/pallas_call | solution.py:128
  82.5 0.7 add_convert_fusion
  (10 shorter events, 0.0 us)
Async XLA Ops:
  0.6 16.4 %copy-start = (f32[4,4,128,128]{3,2,1,0:T(8,128)S(1)}, f32[4,4,128,128]{3,2,1,0:T(8,128)}, u32[]{:S(2)}) copy-start(f32[4,4,128,128]{3,2,1,0:T(8,128)} %param.12) | copy-start | bytes 3145732
  0.6 12.3 %copy-start.1 = (bf16[512,512]{1,0:T(8,128)(2,1)S(1)}, bf16[512,512]{1,0:T(8,128)(2,1)}, u32[]{:S(2)}) copy-start(bf16[512,512]{1,0:T(8,128)(2,1)} %refs_0_.1) | copy-start | bytes 1572868
  5.3 20.1 %all-to-all-start = ((bf16[16,176,128]{2,1,0:T(8,128)(2,1)}), bf16[16,176,128]{2,1,0:T(8,128)(2,1)S(1)}, u32[]{:S(2)}, u32[]{:S(2)}) async-start(bf16[16,176,128]{2,1,0:T(8,128)(2,1)} %block_states.1), calls=%async_computation | async-start | bytes 1441792 | tf_op jit(solution)/shard_map/all_to_all | solution.py:296
  12.9 21.7 %collective-permute-start.3 = (bf16[512,512]{1,0:T(8,128)(2,1)S(1)}, bf16[512,512]{1,0:T(8,128)(2,1)S(1)}, u32[]{:S(2)}, u32[]{:S(2)}) collective-permute-start(bf16[512,512]{1,0:T(8,128)(2,1)S(1)} %copy-done.1), channel_id=1, source_target_pairs={{0,2},{2,0},{1,3},{3,1},{4,6},{6,4},{5,7},{7,5},{8,10},{10,8},{9,1... | collective-permute-start | bytes 1572872 | tf_op jit(solution)/shard_map/ppermute | solution.py:298
  26.5 4.8 %collective-permute-start = (bf16[64,128]{1,0:T(8,128)(2,1)S(1)}, bf16[64,128]{1,0:T(8,128)(2,1)S(1)}, u32[]{:S(2)}, u32[]{:S(2)}) collective-permute-start(bf16[64,128]{1,0:T(8,128)(2,1)S(1)} %get-tuple-element.24), channel_id=1, source_target_pairs={{0,1},{1,0},{2,3},{3,2},{4,5},{5,4},{6,7},{7,6},{8,9},{9,8},{10,11... | collective-permute-start | bytes 49160 | tf_op jit(solution)/shard_map/ppermute | solution.py:306
  28.7 2.8 %collective-permute-start.1 = (bf16[64,128]{1,0:T(8,128)(2,1)S(1)}, bf16[64,128]{1,0:T(8,128)(2,1)S(1)}, u32[]{:S(2)}, u32[]{:S(2)}) collective-permute-start(bf16[64,128]{1,0:T(8,128)(2,1)S(1)} %get-tuple-element.25), channel_id=1, source_target_pairs={{0,2},{2,0},{1,3},{3,1},{4,6},{6,4},{5,7},{7,5},{8,10},{10,8},{9,1... | collective-permute-start | bytes 49160 | tf_op jit(solution)/shard_map/ppermute | solution.py:307
  30.3 3.2 %collective-permute-start.2 = (bf16[64,128]{1,0:T(8,128)(2,1)S(1)}, bf16[64,128]{1,0:T(8,128)(2,1)S(1)}, u32[]{:S(2)}, u32[]{:S(2)}) collective-permute-start(bf16[64,128]{1,0:T(8,128)(2,1)S(1)} %get-tuple-element.26), channel_id=1, source_target_pairs={{0,3},{1,2},{2,1},{3,0},{4,7},{5,6},{6,5},{7,4},{8,11},{9,10},{10,... | collective-permute-start | bytes 49160 | tf_op jit(solution)/shard_map/ppermute | solution.py:308
  34.7 0.8 copy-start.2
  35.5 28.7 %all-to-all-start.1 = ((bf16[16,384,128]{2,1,0:T(8,128)(2,1)}), bf16[16,384,128]{2,1,0:T(8,128)(2,1)S(1)}, u32[]{:S(2)}, u32[]{:S(2)}) async-start(bf16[16,384,128]{2,1,0:T(8,128)(2,1)} %packed.1), calls=%async_computation.1 | async-start | bytes 3145728 | tf_op jit(solution)/shard_map/all_to_all | solution.py:312
  39.2 25.0 %collective-permute-start.4 = (bf16[512,512]{1,0:T(8,128)(2,1)S(1)}, bf16[512,512]{1,0:T(8,128)(2,1)}, u32[]{:S(2)}, u32[]{:S(2)}) collective-permute-start(bf16[512,512]{1,0:T(8,128)(2,1)S(1)} %copy-done.1), channel_id=1, source_target_pairs={{0,1},{1,0},{2,3},{3,2},{4,5},{5,4},{6,7},{7,6},{8,9},{9,8},{10,11... | collective-permute-start | bytes 1572872 | tf_op jit(solution)/shard_map/ppermute | solution.py:299
  39.7 24.5 %collective-permute-start.5 = (bf16[512,512]{1,0:T(8,128)(2,1)}, bf16[512,512]{1,0:T(8,128)(2,1)}, u32[]{:S(2)}, u32[]{:S(2)}) collective-permute-start(bf16[512,512]{1,0:T(8,128)(2,1)} %copy-done.2), channel_id=1, source_target_pairs={{0,1},{1,0},{2,3},{3,2},{4,5},{5,4},{6,7},{7,6},{8,9},{9,8},{10,11... | collective-permute-start | bytes 1572872 | tf_op jit(solution)/shard_map/ppermute | solution.py:313
  64.2 1.0 %copy-start.3 = (bf16[512,512]{1,0:T(8,128)(2,1)S(1)}, bf16[512,512]{1,0:T(8,128)(2,1)}, u32[]{:S(2)}) copy-start(bf16[512,512]{1,0:T(8,128)(2,1)} %copy-done.2) | copy-start | bytes 1572868
  67.7 14.7 %collective-permute-start.6 = (bf16[64,512]{1,0:T(8,128)(2,1)S(1)}, bf16[64,512]{1,0:T(8,128)(2,1)S(1)}, u32[]{:S(2)}, u32[]{:S(2)}) collective-permute-start(bf16[64,512]{1,0:T(8,128)(2,1)S(1)} %get-tuple-element.35), channel_id=1, source_target_pairs={{0,4},{4,8},{8,12},{12,0},{1,5},{5,9},{9,13},{13,1},{2,6},{6,10},{... | collective-permute-start | bytes 196616 | tf_op jit(solution)/shard_map/ppermute | solution.py:321
  70.8 11.7 %collective-permute-start.7 = (bf16[64,512]{1,0:T(8,128)(2,1)S(1)}, bf16[64,512]{1,0:T(8,128)(2,1)S(1)}, u32[]{:S(2)}, u32[]{:S(2)}) collective-permute-start(bf16[64,512]{1,0:T(8,128)(2,1)S(1)} %get-tuple-element.36), channel_id=1, source_target_pairs={{0,8},{4,12},{8,0},{12,4},{1,9},{5,13},{9,1},{13,5},{2,10},{6,14},... | collective-permute-start | bytes 196616 | tf_op jit(solution)/shard_map/ppermute | solution.py:321
  75.0 7.5 %collective-permute-start.8 = (bf16[64,512]{1,0:T(8,128)(2,1)S(1)}, bf16[64,512]{1,0:T(8,128)(2,1)S(1)}, u32[]{:S(2)}, u32[]{:S(2)}) collective-permute-start(bf16[64,512]{1,0:T(8,128)(2,1)S(1)} %get-tuple-element.37), channel_id=1, source_target_pairs={{0,12},{4,0},{8,4},{12,8},{1,13},{5,1},{9,5},{13,9},{2,14},{6,2},{... | collective-permute-start | bytes 196616 | tf_op jit(solution)/shard_map/ppermute | solution.py:321

commit v4 on v3

v4 whole, which is shorter than its diff:
```python
import jax
import jax.numpy as jnp
from jax import lax
from jax.experimental import pallas as pl
from jax.experimental.pallas import tpu as pltpu
from jax.sharding import Mesh
from jax.sharding import PartitionSpec as P

DH = 128
NODES = 256
SEQ = ("y", "x")
HEAD = ("zp", "zl", "c")
SIDE = 4
EPS = 1e-05
BF = jnp.bfloat16
F32 = jnp.float32


def mm(a, b, ca, cb):
    return lax.dot_general(a, b, (((ca,), (cb,)), ((), ())), preferred_element_type=F32)


def normed(raw):
    return raw * lax.rsqrt(jnp.mean(raw * raw, axis=-1, keepdims=True) + EPS)


def room(mib):
    return pltpu.CompilerParams(vmem_limit_bytes=mib << 20)


def far(array):
    return pltpu.with_memory_space_constraint(array, pltpu.HBM)


def cost(flops, nbytes):
    return pl.CostEstimate(flops=flops, bytes_accessed=nbytes, transcendentals=0)


def smem():
    return pl.BlockSpec(memory_space=pltpu.SMEM)


def vmem(count):
    return [pl.BlockSpec(memory_space=pltpu.VMEM)] * count


def like(shape, dtype=BF):
    return jax.ShapeDtypeStruct(shape, dtype)


def small(body, outs, scratch=(), flops=0):
    def call(at, *arrays):
        nbytes = sum(a.size * a.dtype.itemsize for a in arrays)
        return pl.pallas_call(
            body,
            in_specs=[smem()] + vmem(len(arrays)),
            out_specs=vmem(len(outs)),
            out_shape=list(outs),
            scratch_shapes=list(scratch),
            cost_estimate=cost(flops, 2 * nbytes),
            compiler_params=room(8),
        )(at, *arrays)

    return call


def states_body(k_ref, v_ref, tq_ref, tk_ref, tv_ref, o_ref):
    heads = o_ref.shape[0]
    nodes = tq_ref.shape[1]
    for h in range(heads):
        cols = slice(h * DH, (h + 1) * DH)
        kv = mm(k_ref[0, :, cols], v_ref[0, :, cols], 0, 0)
        o_ref[h, 0:DH, :] = kv.astype(BF)
        for j, ref in enumerate((tq_ref, tk_ref, tv_ref)):
            o_ref[h, DH + j * nodes : DH + (j + 1) * nodes, :] = ref[0, :, cols]


def block_states(k, v, tq, tk, tv):
    requests, tokens, width = k.shape
    heads, nodes = width // DH, tq.shape[1]
    rows = DH + 3 * nodes
    big = pl.BlockSpec((1, tokens, width), lambda r: (r, 0, 0))
    small = pl.BlockSpec((1, nodes, width), lambda r: (r, 0, 0))
    return pl.pallas_call(
        states_body,
        grid=(requests,),
        in_specs=[big, big, small, small, small],
        out_specs=pl.BlockSpec((heads, rows, DH), lambda r: (r, 0, 0)),
        out_shape=like((requests * heads, rows, DH)),
        cost_estimate=cost(2 * requests * tokens * width * DH, 4 * requests * tokens * width),
        compiler_params=room(16),
        name="block_states",
    )(far(k), far(v), far(tq), far(tk), far(tv))


def reach_body(parents_ref, o_ref):
    row = lax.broadcasted_iota(jnp.int32, (NODES, NODES), 0)
    col = lax.broadcasted_iota(jnp.int32, (NODES, NODES), 1)
    links = (parents_ref[...] == row) & (col >= 1)
    reach = jnp.where(links | (row == col), 1.0, 0.0).astype(BF)
    for _ in range((NODES - 1).bit_length()):
        reach = jnp.minimum(mm(reach, reach, 1, 0), 1.0).astype(BF)
    o_ref[...] = reach.astype(F32).T


def ancestors(own_parents):
    return pl.pallas_call(
        reach_body,
        out_shape=like((NODES, NODES), F32),
        cost_estimate=cost(16 * NODES**3, 4 * NODES * NODES),
        compiler_params=room(4),
        name="ancestors",
    )(own_parents)


def tree_body(at_ref, got_ref, prior_ref, reach_ref, *refs):
    outs, hold = refs[:-1], refs[-1]
    peers = got_ref.shape[0]
    nodes = NODES // peers
    total = prior_ref[...]
    for s in range(peers):
        total = total + got_ref[s, 0:DH, :].astype(F32)

    def part(j):
        start = DH + j * nodes
        return got_ref[:, start : start + nodes, :].reshape(NODES, DH)

    q, k, v = part(0), part(1), part(2)
    weights = jnp.where(reach_ref[...] > 0, mm(q, k, 1, 1), 0.0).astype(BF)
    raw = mm(q, total.astype(BF), 1, 0) + mm(weights, v, 1, 0)
    hold[...] = normed(raw).astype(BF).reshape(hold.shape)
    for j, out in enumerate(outs):
        out[...] = hold[at_ref[3] ^ j]


def tree(at, got, prior, reach):
    nodes = NODES // SIDE
    scratch = [pltpu.VMEM((SIDE, nodes, DH), BF)]
    call = small(tree_body, [like((nodes, DH))] * SIDE, scratch, 6 * NODES * NODES * DH)
    return call(at, got, prior, reach)


def prefix_body(at_ref, got_ref, prior_ref, *refs):
    outs, hold = refs[:-1], refs[-1]
    running = prior_ref[...]
    for y in range(SIDE):
        for x in range(SIDE):
            hold[y, x] = running.astype(BF)
            running = running + got_ref[y * SIDE + x, 0:DH, :].astype(F32)
    for s, out in enumerate(outs):
        out[...] = hold[at_ref[1] ^ s]


def prefixes(at, got, prior):
    scratch = [pltpu.VMEM((SIDE, SIDE, DH, DH), BF)]
    outs = [like((SIDE, DH, DH))] * SIDE
    return small(prefix_body, outs, scratch)(at, got, prior)


def regroup_body(at_ref, *refs):
    got, outs = refs[:SIDE], refs[SIDE:]
    for s, out in enumerate(outs):
        for t in range(SIDE):
            out[at_ref[1] ^ t] = got[t][at_ref[0] ^ s]


def regrouped(at, got):
    return small(regroup_body, [like(got[0].shape)] * SIDE)(at, *got)


def join_body(at_ref, *refs):
    o_ref = refs[-1]
    rows = refs[0].shape[0]
    for j, ref in enumerate(refs[:-1]):
        o_ref[j * rows : (j + 1) * rows, :] = ref[...]


def joined(at, pieces):
    rows = sum(p.shape[0] for p in pieces)
    return small(join_body, [like((rows, DH))])(at, *pieces)[0]


def inner_body(q_ref, k_ref, v_ref, o_ref):
    tokens, width = q_ref.shape[1:]
    half = tokens // 2
    for h in range(width // DH):
        cols = slice(h * DH, (h + 1) * DH)
        for part in range(2):
            rows = slice(part * half, (part + 1) * half)
            upto = (part + 1) * half
            scores = mm(q_ref[0, rows, cols], k_ref[0, 0:upto, cols], 1, 1)
            at = part * half + lax.broadcasted_iota(jnp.int32, scores.shape, 0)
            other = lax.broadcasted_iota(jnp.int32, scores.shape, 1)
            weights = jnp.where(at >= other, scores, 0.0).astype(BF)
            o_ref[0, rows, cols] = mm(weights, v_ref[0, 0:upto, cols], 1, 0).astype(BF)


def inside(q, k, v, first, count, onto=None):
    _, tokens, width = q.shape
    big = pl.BlockSpec((1, tokens, width), lambda r: (r + first, 0, 0))
    more = [] if onto is None else [onto]
    body = inner_body if onto is None else lambda q, k, v, _, o: inner_body(q, k, v, o)
    return pl.pallas_call(
        body,
        grid=(count,),
        in_specs=[big, big, big] + [pl.BlockSpec(memory_space=pltpu.HBM)] * len(more),
        out_specs=big,
        out_shape=pltpu.HBM(q.shape, BF),
        input_output_aliases={3: 0} if more else {},
        cost_estimate=cost(3 * count * tokens * tokens * width, 8 * count * tokens * width),
        compiler_params=room(24),
        name="inside",
    )(far(q), far(k), far(v), *more)


def finish_body(at_ref, q_ref, inner_ref, *refs):
    states, o_ref, hold = refs[:SIDE], refs[SIDE], refs[SIDE + 1]
    r = pl.program_id(0)

    @pl.when(r == 0)
    def _():
        for s in range(SIDE):
            hold[at_ref[0] ^ s] = states[s][...]

    for h in range(SIDE):
        cols = slice(h * DH, (h + 1) * DH)
        raw = mm(q_ref[0, :, cols], hold[h, r], 1, 0) + inner_ref[0, :, cols].astype(F32)
        o_ref[0, :, cols] = normed(raw).astype(BF)


def finish(at, q, inner, states):
    requests, tokens, width = q.shape
    big = pl.BlockSpec((1, tokens, width), lambda r: (r, 0, 0))
    return pl.pallas_call(
        finish_body,
        grid=(requests,),
        in_specs=[smem(), big, big] + vmem(SIDE),
        out_specs=big,
        out_shape=like(q.shape),
        scratch_shapes=[pltpu.VMEM((SIDE, requests, DH, DH), BF)],
        cost_estimate=cost(2 * requests * tokens * width * DH, 6 * requests * tokens * width),
        compiler_params=room(16),
        name="finish",
    )(at, far(q), far(inner), *states)


def project_body(at_ref, *refs):
    rows, weights, outs = refs[:SIDE], refs[SIDE : 2 * SIDE], refs[2 * SIDE : 3 * SIDE]
    hold, slab, sems = refs[-3:]
    nodes = outs[0].shape[0]
    copies = [pltpu.make_async_copy(weights[j], slab.at[j], sems.at[j]) for j in range(SIDE)]
    for copy in copies:
        copy.start()
    total = None
    for j in range(SIDE):
        parts = []
        for t in range(SIDE):
            heads = [
                rows[t][pl.ds((at_ref[0] ^ h) * NODES + j * nodes, nodes), :]
                for h in range(SIDE)
            ]
            parts.append(jnp.concatenate(heads, axis=1))
        lhs = jnp.concatenate(parts, axis=0)
        copies[j].wait()
        part = mm(lhs, slab[j], 1, 0)
        total = part if total is None else total + part
    hold[...] = total.astype(BF).reshape(hold.shape)
    for s, out in enumerate(outs):
        out[...] = hold[at_ref[1] ^ at_ref[2] ^ s]


def project(at, rows, weights):
    nodes = NODES // SIDE
    deep, wide = weights[0].shape
    return pl.pallas_call(
        project_body,
        in_specs=[smem()] + vmem(SIDE) + [pl.BlockSpec(memory_space=pl.ANY)] * SIDE,
        out_specs=vmem(SIDE),
        scratch_shapes=[
            pltpu.VMEM((SIDE, nodes, wide), BF),
            pltpu.VMEM((SIDE, deep, wide), BF),
            pltpu.SemaphoreType.DMA((SIDE,)),
        ],
        out_shape=[like((nodes, wide))] * SIDE,
        cost_estimate=cost(2 * SIDE * SIDE * NODES * DH * wide, 8 * deep * wide),
        compiler_params=room(8),
        name="project",
    )(at, *rows, *weights)


def exchanged(arrays, axis):
    pairs = [[(i, i ^ s) for i in range(SIDE)] for s in range(SIDE)]
    got = {s: lax.ppermute(arrays[s], axis, pairs[s]) for s in (2, 1, 3)}
    return [arrays[0], got[1], got[2], got[3]]


def on_device(q, k, v, prior, tq, tk, tv, parents, weight):
    requests, _, _ = q.shape
    x, y, zp = (lax.axis_index(name) for name in ("x", "y", "zp"))
    group = lax.axis_index("zl") * 2 + lax.axis_index("c")
    at = jnp.stack([x, y, zp, group]).astype(jnp.int32)

    swap = [(0, 1), (1, 0)]
    quad = ("zl", "c")
    crossed = [(g, g ^ 3) for g in range(SIDE)]

    sent = block_states(k, v, tq, tk, tv)
    got = lax.all_to_all(sent, SEQ, 0, 0, tiled=True)
    weight, _ = lax.optimization_barrier((weight, sent))
    w_z = lax.ppermute(weight, "zl", swap)
    reach = ancestors(lax.dynamic_slice_in_dim(parents, y, 1, 0))
    flat_prior = prior.reshape(-1, DH, DH)
    own_prior = lax.dynamic_index_in_dim(flat_prior, y * SIDE + x, 0, keepdims=False)
    inner = inside(q, k, v, 0, requests)
    got, reach, own_prior, inner = lax.optimization_barrier((got, reach, own_prior, inner))

    pieces = tree(at, got, own_prior, reach)
    from_c = lax.ppermute(pieces[1], "c", swap)
    from_z = lax.ppermute(pieces[2], "zl", swap)
    from_zc = lax.ppermute(pieces[3], quad, crossed)
    before = prefixes(at, got, own_prior)
    mine = joined(at, (pieces[0], from_c, from_z, from_zc))
    heads = exchanged([mine] * SIDE, "x")
    above = exchanged(before, "y")
    row_of_heads = joined(at, heads)
    weight, w_z, _ = lax.optimization_barrier((weight, w_z, mine))
    w_c = lax.ppermute(weight, "c", swap)
    w_zc = lax.ppermute(w_z, "c", swap)
    rows = exchanged([row_of_heads] * SIDE, "y")
    states = exchanged(regrouped(at, above), "x")

    parts = project(at, rows, (weight, w_c, w_z, w_zc))
    total = parts[0].astype(F32)
    for got in exchanged(parts, "zp")[1:]:
        total = total + got.astype(F32)
    verified = total.astype(BF)

    prefill_out = finish(at, q, inner, states)
    return prefill_out, verified


def solution(mesh):
    torus = Mesh(mesh.devices.reshape(4, 4, 4, 2, 2), (*SEQ, *HEAD))
    return jax.shard_map(
        on_device,
        mesh=torus,
        in_specs=(
            P(None, SEQ, HEAD),
            P(None, SEQ, HEAD),
            P(None, SEQ, HEAD),
            P(None, HEAD, None, None),
            P(None, SEQ, HEAD),
            P(None, SEQ, HEAD),
            P(None, SEQ, HEAD),
            P(),
            P(HEAD, SEQ),
        ),
        out_specs=(P(None, SEQ, HEAD), P(HEAD, SEQ)),
        check_vma=False,
    )
```

time: 83.7 us -> 82.6 us (0.987)
  the two profiles are of different devices: /device:TPU:1 before, /device:TPU:32 now
where the time goes in v4:
time: 82.6 us; the launch traced here: 82.2 us
  starting transfers between devices  35.6 us (43%)
  Pallas kernels  24.5 us (30%)
  waiting for transfers between devices  19.9 us (24%)
    ppermute x15, starting transfers between devices, exchanged(): got = {s: lax.ppermute(arrays[s], axis, pairs[s]) for s in (2, 1, 3)}  25.9 us
    ppermute x15, waiting for transfers between devices, exchanged(): got = {s: lax.ppermute(arrays[s], axis, pairs[s]) for s in (2, 1, 3)}  14.8 us
    pallas_call x1, Pallas kernels, inside(): pl.pallas_call(body, grid=(count,), in_specs=[big, big, big] + [pl.BlockS...  8.08 us
    all_to_all x1, starting transfers between devices, on_device(): got = lax.all_to_all(sent, SEQ, 0, 0, tiled=True)  7.03 us
    pallas_call x1, Pallas kernels, finish(): pl.pallas_call(finish_body, grid=(requests,), in_specs=[smem(), big, big]...  5.16 us
    pallas_call x1, Pallas kernels, block_states(): pl.pallas_call(states_body, grid=(requests,), in_specs=[big, big, small,...  4.69 us
    pallas_call x5, Pallas kernels, call(): pl.pallas_call(body, in_specs=[smem()] + vmem(len(arrays)), out_specs=vme...  3.34 us
    all_to_all x1, waiting for transfers between devices, on_device(): got = lax.all_to_all(sent, SEQ, 0, 0, tiled=True)  3.06 us
  transfers between devices with their start and end apart: 22, of which 7 were waited for; matrix products, arithmetic and copies ran while one was open for 1% of the time, Pallas kernels for 24%

profile of v4, /device:TPU:32, one launch (start us, length us, event | category | flops | bytes accessed | tf_op | source)
XLA Modules:
  0.0 82.2 jit_solution(16939926707340601710)
XLA Ops:
  0.7 4.7 %block_states.1 = bf16[16,176,128]{2,1,0:T(8,128)(2,1)} custom-call(bf16[4,512,512]{2,1,0:T(8,128)(2,1)} %k_ref.3, bf16[4,512,512]{2,1,0:T(8,128)(2,1)} %v_ref.3, bf16[4,16,512]{2,1,0:T(8,128)(2,1)} %tq_ref.1, bf16[4,16,512]{2,1,0:T(8,128)(2,1)} %tk_ref.1, bf16[4,16,512]{2,1,0:T(8,128)(2,1)} %tv_ref.1), custom_call_target="tpu_custom_call" | custom-call | flops 268435456 | bytes 4194304 | tf_op jit(solution)/shard_map/block_states/pallas_call | solution.py:84
  5.3 7.0 %all-to-all-start = ((bf16[16,176,128]{2,1,0:T(8,128)(2,1)}), bf16[16,176,128]{2,1,0:T(8,128)(2,1)S(1)}, u32[]{:S(2)}, u32[]{:S(2)}) async-start(bf16[16,176,128]{2,1,0:T(8,128)(2,1)} %block_states.1), calls=%async_computation | async-start | bytes 1441792 | tf_op jit(solution)/shard_map/all_to_all | solution.py:308
  12.6 0.7 constant_dynamic-slice_fusion.parents_ref
  13.3 1.6 %ancestors.1.reach_ref = f32[256,256]{1,0:T(8,128)S(1)} custom-call(s32[1,256]{1,0:T(1,128)S(1)} %constant_dynamic-slice_fusion.parents_ref), custom_call_target="tpu_custom_call" | custom-call | flops 268435456 | bytes 262144 | tf_op jit(solution)/shard_map/ancestors/pallas_call | solution.py:107
  15.0 8.1 %inside.1.inner_ref = bf16[4,512,512]{2,1,0:T(8,128)(2,1)} custom-call(bf16[4,512,512]{2,1,0:T(8,128)(2,1)} %q_ref.3, bf16[4,512,512]{2,1,0:T(8,128)(2,1)} %k_ref.3, bf16[4,512,512]{2,1,0:T(8,128)(2,1)} %v_ref.3), custom_call_target="tpu_custom_call" | custom-call | flops 1610612736 | bytes 8388608 | tf_op jit(solution)/shard_map/inside/pallas_call | solution.py:203
  23.1 3.1 %all-to-all-done.got_ref = bf16[16,176,128]{2,1,0:T(8,128)(2,1)S(1)} async-done(((bf16[16,176,128]{2,1,0:T(8,128)(2,1)}), bf16[16,176,128]{2,1,0:T(8,128)(2,1)S(1)}, u32[]{:S(2)}, u32[]{:S(2)}) %all-to-all-start) | async-done | bytes 720928 | tf_op jit(solution)/shard_map/all_to_all | solution.py:308
  26.1 1.0 %shard_map.106 = (bf16[64,128]{1,0:T(8,128)(2,1)S(1)}, bf16[64,128]{1,0:T(8,128)(2,1)S(1)}, bf16[64,128]{1,0:T(8,128)(2,1)S(1)}, bf16[64,128]{1,0:T(8,128)(2,1)S(1)}) custom-call(s32[4]{0:T(128)S(1)} %pad_add_fusion.at_ref, bf16[16,176,128]{2,1,0:T(8,128)(2,1)S(1)} %all-to-all-done.got_ref, f32[128,128]{1,0:T(8,128)S(1)} %dynamic-slice_bitcast_fusion.prior_ref, ...), custom_call_target="tpu_custom_call" | custom-call | flops 50331648 | bytes 2097152 | tf_op jit(solution)/shard_map/pallas_call | solution.py:54
  27.4 1.7 %collective-permute-start.8 = (bf16[64,128]{1,0:T(8,128)(2,1)S(1)}, bf16[64,128]{1,0:T(8,128)(2,1)S(1)}, u32[]{:S(2)}, u32[]{:S(2)}) collective-permute-start(bf16[64,128]{1,0:T(8,128)(2,1)S(1)} %get-tuple-element.40), channel_id=1, source_target_pairs={{0,3},{1,2},{2,1},{3,0},{4,7},{5,6},{6,5},{7,4},{8,11},{9,10},{10,... | collective-permute-start | bytes 49160 | tf_op jit(solution)/shard_map/ppermute | solution.py:320
  29.1 2.0 %collective-permute-done.7.refs_2_ = bf16[64,128]{1,0:T(8,128)(2,1)S(1)} collective-permute-done((bf16[64,128]{1,0:T(8,128)(2,1)S(1)}, bf16[64,128]{1,0:T(8,128)(2,1)S(1)}, u32[]{:S(2)}, u32[]{:S(2)}) %collective-permute-start.7) | collective-permute-done | bytes 16416 | tf_op jit(solution)/shard_map/ppermute | solution.py:319
  31.1 0.5 shard_map.107.refs_0_
  31.6 1.5 %collective-permute-start.11 = (bf16[256,128]{1,0:T(8,128)(2,1)S(1)}, bf16[256,128]{1,0:T(8,128)(2,1)S(1)}, u32[]{:S(2)}, u32[]{:S(2)}) collective-permute-start(bf16[256,128]{1,0:T(8,128)(2,1)S(1)} %shard_map.107.refs_0_), channel_id=1, source_target_pairs={{0,48},{16,32},{32,16},{48,0},{1,49},{17,33},{33,17},{49,1},{2,50}... | collective-permute-start | bytes 196616 | tf_op jit(solution)/shard_map/ppermute | solution.py:293
  33.6 1.1 %collective-permute-start.10 = (bf16[256,128]{1,0:T(8,128)(2,1)S(1)}, bf16[256,128]{1,0:T(8,128)(2,1)S(1)}, u32[]{:S(2)}, u32[]{:S(2)}) collective-permute-start(bf16[256,128]{1,0:T(8,128)(2,1)S(1)} %shard_map.107.refs_0_), channel_id=1, source_target_pairs={{0,32},{16,48},{32,0},{48,16},{1,33},{17,49},{33,1},{49,17},{2,34}... | collective-permute-start | bytes 196616 | tf_op jit(solution)/shard_map/ppermute | solution.py:293
  34.8 1.5 %collective-permute-start.9 = (bf16[256,128]{1,0:T(8,128)(2,1)S(1)}, bf16[256,128]{1,0:T(8,128)(2,1)S(1)}, u32[]{:S(2)}, u32[]{:S(2)}) collective-permute-start(bf16[256,128]{1,0:T(8,128)(2,1)S(1)} %shard_map.107.refs_0_), channel_id=1, source_target_pairs={{0,16},{16,0},{32,48},{48,32},{1,17},{17,1},{33,49},{49,33},{2,18}... | collective-permute-start | bytes 196616 | tf_op jit(solution)/shard_map/ppermute | solution.py:293
  36.3 0.7 shard_map.104
  37.4 2.5 %collective-permute-done.10.refs_2_ = bf16[256,128]{1,0:T(8,128)(2,1)S(1)} collective-permute-done((bf16[256,128]{1,0:T(8,128)(2,1)S(1)}, bf16[256,128]{1,0:T(8,128)(2,1)S(1)}, u32[]{:S(2)}, u32[]{:S(2)}) %collective-permute-start.10) | collective-permute-done | bytes 65568 | tf_op jit(solution)/shard_map/ppermute | solution.py:293
  39.8 3.0 %collective-permute-start.1 = (bf16[4,128,128]{2,1,0:T(8,128)(2,1)S(1)}, bf16[4,128,128]{2,1,0:T(8,128)(2,1)S(1)}, u32[]{:S(2)}, u32[]{:S(2)}) collective-permute-start(bf16[4,128,128]{2,1,0:T(8,128)(2,1)S(1)} %get-tuple-element.30), channel_id=1, source_target_pairs={{0,128},{64,192},{128,0},{192,64},{1,129},{65,193},{129,1},{193,65... | collective-permute-start | bytes 393224 | tf_op jit(solution)/shard_map/ppermute | solution.py:293
  42.8 1.2 %collective-permute-start.2 = (bf16[4,128,128]{2,1,0:T(8,128)(2,1)S(1)}, bf16[4,128,128]{2,1,0:T(8,128)(2,1)S(1)}, u32[]{:S(2)}, u32[]{:S(2)}) collective-permute-start(bf16[4,128,128]{2,1,0:T(8,128)(2,1)S(1)} %get-tuple-element.31), channel_id=1, source_target_pairs={{0,192},{64,128},{128,64},{192,0},{1,193},{65,129},{129,65},{193,1... | collective-permute-start | bytes 393224 | tf_op jit(solution)/shard_map/ppermute | solution.py:293
  44.0 0.6 shard_map.108.refs_0_
  44.5 2.2 %collective-permute-start.14 = (bf16[1024,128]{1,0:T(8,128)(2,1)S(1)}, bf16[1024,128]{1,0:T(8,128)(2,1)S(1)}, u32[]{:S(2)}, u32[]{:S(2)}) collective-permute-start(bf16[1024,128]{1,0:T(8,128)(2,1)S(1)} %shard_map.108.refs_0_), channel_id=1, source_target_pairs={{0,192},{64,128},{128,64},{192,0},{1,193},{65,129},{129,65},{193,1... | collective-permute-start | bytes 786440 | tf_op jit(solution)/shard_map/ppermute | solution.py:293
  46.7 2.7 %collective-permute-start.13 = (bf16[1024,128]{1,0:T(8,128)(2,1)S(1)}, bf16[1024,128]{1,0:T(8,128)(2,1)S(1)}, u32[]{:S(2)}, u32[]{:S(2)}) collective-permute-start(bf16[1024,128]{1,0:T(8,128)(2,1)S(1)} %shard_map.108.refs_0_), channel_id=1, source_target_pairs={{0,128},{64,192},{128,0},{192,64},{1,129},{65,193},{129,1},{193,65... | collective-permute-start | bytes 786440 | tf_op jit(solution)/shard_map/ppermute | solution.py:293
  49.4 5.2 %collective-permute-done.2.refs_3_ = bf16[4,128,128]{2,1,0:T(8,128)(2,1)S(1)} collective-permute-done((bf16[4,128,128]{2,1,0:T(8,128)(2,1)S(1)}, bf16[4,128,128]{2,1,0:T(8,128)(2,1)S(1)}, u32[]{:S(2)}, u32[]{:S(2)}) %collective-permute-start.2) | collective-permute-done | bytes 131104 | tf_op jit(solution)/shard_map/ppermute | solution.py:293
  54.6 0.6 shard_map.105
  55.2 5.0 %collective-permute-done.14.refs_3_ = bf16[1024,128]{1,0:T(8,128)(2,1)S(1)} collective-permute-done((bf16[1024,128]{1,0:T(8,128)(2,1)S(1)}, bf16[1024,128]{1,0:T(8,128)(2,1)S(1)}, u32[]{:S(2)}, u32[]{:S(2)}) %collective-permute-start.14) | collective-permute-done | bytes 262176 | tf_op jit(solution)/shard_map/ppermute | solution.py:293
  60.2 0.5 collective-permute-start.3
  60.7 1.9 %collective-permute-start.4 = (bf16[4,128,128]{2,1,0:T(8,128)(2,1)S(1)}, bf16[4,128,128]{2,1,0:T(8,128)(2,1)S(1)}, u32[]{:S(2)}, u32[]{:S(2)}) collective-permute-start(bf16[4,128,128]{2,1,0:T(8,128)(2,1)S(1)} %get-tuple-element.34), channel_id=1, source_target_pairs={{0,32},{16,48},{32,0},{48,16},{1,33},{17,49},{33,1},{49,17},{2,34}... | collective-permute-start | bytes 393224 | tf_op jit(solution)/shard_map/ppermute | solution.py:293
  62.6 2.3 %collective-permute-start.5 = (bf16[4,128,128]{2,1,0:T(8,128)(2,1)S(1)}, bf16[4,128,128]{2,1,0:T(8,128)(2,1)S(1)}, u32[]{:S(2)}, u32[]{:S(2)}) collective-permute-start(bf16[4,128,128]{2,1,0:T(8,128)(2,1)S(1)} %get-tuple-element.35), channel_id=1, source_target_pairs={{0,48},{16,32},{32,16},{48,0},{1,49},{17,33},{33,17},{49,1},{2,50}... | collective-permute-start | bytes 393224 | tf_op jit(solution)/shard_map/ppermute | solution.py:293
  64.9 1.7 %project.1 = (bf16[64,512]{1,0:T(8,128)(2,1)S(1)}, bf16[64,512]{1,0:T(8,128)(2,1)S(1)}, bf16[64,512]{1,0:T(8,128)(2,1)S(1)}, bf16[64,512]{1,0:T(8,128)(2,1)S(1)}) custom-call(s32[4]{0:T(128)S(1)} %pad_add_fusion.at_ref, bf16[1024,128]{1,0:T(8,128)(2,1)S(1)} %shard_map.108.refs_0_, bf16[1024,128]{1,0:T(8,128)(2,1)S(1)} %collective-permute-done.12.refs_1_, ...), custom_call_target="tpu_custom_call" | custom-call | flops 536870912 | bytes 2097152 | tf_op jit(solution)/shard_map/project/pallas_call | solution.py:275
  66.6 3.4 %collective-permute-start.18 = (bf16[64,512]{1,0:T(8,128)(2,1)S(1)}, bf16[64,512]{1,0:T(8,128)(2,1)S(1)}, u32[]{:S(2)}, u32[]{:S(2)}) collective-permute-start(bf16[64,512]{1,0:T(8,128)(2,1)S(1)} %get-tuple-element.45), channel_id=1, source_target_pairs={{0,4},{4,0},{8,12},{12,8},{1,5},{5,1},{9,13},{13,9},{2,6},{6,2},{1... | collective-permute-start | bytes 196616 | tf_op jit(solution)/shard_map/ppermute | solution.py:293
  69.9 4.5 %collective-permute-start.19 = (bf16[64,512]{1,0:T(8,128)(2,1)S(1)}, bf16[64,512]{1,0:T(8,128)(2,1)S(1)}, u32[]{:S(2)}, u32[]{:S(2)}) collective-permute-start(bf16[64,512]{1,0:T(8,128)(2,1)S(1)} %get-tuple-element.46), channel_id=1, source_target_pairs={{0,8},{4,12},{8,0},{12,4},{1,9},{5,13},{9,1},{13,5},{2,10},{6,14},... | collective-permute-start | bytes 196616 | tf_op jit(solution)/shard_map/ppermute | solution.py:293
  74.4 5.2 %finish.1 = bf16[4,512,512]{2,1,0:T(8,128)(2,1)} custom-call(s32[4]{0:T(128)S(1)} %pad_add_fusion.at_ref, bf16[4,512,512]{2,1,0:T(8,128)(2,1)} %q_ref.3, bf16[4,512,512]{2,1,0:T(8,128)(2,1)} %inside.1.inner_ref, bf16[4,128,128]{2,1,0:T(8,128)(2,1)S(1)} %get-tuple-element.32.refs_0_, bf16[4,128,128]{2,1,0:T(8,128)(2,1)S(1)} %collective-permute-done.3.refs_1_, ...), custom_call_target="tpu_custom_call" | custom-call | flops 268435456 | bytes 6291456 | tf_op jit(solution)/shard_map/finish/pallas_call | solution.py:234
  79.6 1.9 %collective-permute-done.20 = bf16[64,512]{1,0:T(8,128)(2,1)S(1)} collective-permute-done((bf16[64,512]{1,0:T(8,128)(2,1)S(1)}, bf16[64,512]{1,0:T(8,128)(2,1)S(1)}, u32[]{:S(2)}, u32[]{:S(2)}) %collective-permute-start.20) | collective-permute-done | bytes 65568 | tf_op jit(solution)/shard_map/ppermute | solution.py:293
  81.5 0.7 add_convert_fusion
  (30 shorter events, 1.5 us)
Async XLA Ops:
  0.6 14.3 %copy-start = (f32[4,4,128,128]{3,2,1,0:T(8,128)S(1)}, f32[4,4,128,128]{3,2,1,0:T(8,128)}, u32[]{:S(2)}) copy-start(f32[4,4,128,128]{3,2,1,0:T(8,128)} %param.12) | copy-start | bytes 3145732
  0.6 11.7 %copy-start.1 = (bf16[512,512]{1,0:T(8,128)(2,1)S(1)}, bf16[512,512]{1,0:T(8,128)(2,1)}, u32[]{:S(2)}) copy-start(bf16[512,512]{1,0:T(8,128)(2,1)} %refs_4_) | copy-start | bytes 1572868
  5.3 20.8 %all-to-all-start = ((bf16[16,176,128]{2,1,0:T(8,128)(2,1)}), bf16[16,176,128]{2,1,0:T(8,128)(2,1)S(1)}, u32[]{:S(2)}, u32[]{:S(2)}) async-start(bf16[16,176,128]{2,1,0:T(8,128)(2,1)} %block_states.1), calls=%async_computation | async-start | bytes 1441792 | tf_op jit(solution)/shard_map/all_to_all | solution.py:308
  12.4 20.7 %collective-permute-start.15 = (bf16[512,512]{1,0:T(8,128)(2,1)S(1)}, bf16[512,512]{1,0:T(8,128)(2,1)S(1)}, u32[]{:S(2)}, u32[]{:S(2)}) collective-permute-start(bf16[512,512]{1,0:T(8,128)(2,1)S(1)} %copy-done.1), channel_id=1, source_target_pairs={{0,2},{2,0},{1,3},{3,1},{4,6},{6,4},{5,7},{7,5},{8,10},{10,8},{9,1... | collective-permute-start | bytes 1572872 | tf_op jit(solution)/shard_map/ppermute | solution.py:310
  27.1 2.0 %collective-permute-start.6 = (bf16[64,128]{1,0:T(8,128)(2,1)S(1)}, bf16[64,128]{1,0:T(8,128)(2,1)S(1)}, u32[]{:S(2)}, u32[]{:S(2)}) collective-permute-start(bf16[64,128]{1,0:T(8,128)(2,1)S(1)} %get-tuple-element.38), channel_id=1, source_target_pairs={{0,1},{1,0},{2,3},{3,2},{4,5},{5,4},{6,7},{7,6},{8,9},{9,8},{10,11... | collective-permute-start | bytes 49160 | tf_op jit(solution)/shard_map/ppermute | solution.py:318
  27.2 3.8 %collective-permute-start.7 = (bf16[64,128]{1,0:T(8,128)(2,1)S(1)}, bf16[64,128]{1,0:T(8,128)(2,1)S(1)}, u32[]{:S(2)}, u32[]{:S(2)}) collective-permute-start(bf16[64,128]{1,0:T(8,128)(2,1)S(1)} %get-tuple-element.39), channel_id=1, source_target_pairs={{0,2},{2,0},{1,3},{3,1},{4,6},{6,4},{5,7},{7,5},{8,10},{10,8},{9,1... | collective-permute-start | bytes 49160 | tf_op jit(solution)/shard_map/ppermute | solution.py:319
  27.4 3.6 %collective-permute-start.8 = (bf16[64,128]{1,0:T(8,128)(2,1)S(1)}, bf16[64,128]{1,0:T(8,128)(2,1)S(1)}, u32[]{:S(2)}, u32[]{:S(2)}) collective-permute-start(bf16[64,128]{1,0:T(8,128)(2,1)S(1)} %get-tuple-element.40), channel_id=1, source_target_pairs={{0,3},{1,2},{2,1},{3,0},{4,7},{5,6},{6,5},{7,4},{8,11},{9,10},{10,... | collective-permute-start | bytes 49160 | tf_op jit(solution)/shard_map/ppermute | solution.py:320
  31.6 5.6 %collective-permute-start.11 = (bf16[256,128]{1,0:T(8,128)(2,1)S(1)}, bf16[256,128]{1,0:T(8,128)(2,1)S(1)}, u32[]{:S(2)}, u32[]{:S(2)}) collective-permute-start(bf16[256,128]{1,0:T(8,128)(2,1)S(1)} %shard_map.107.refs_0_), channel_id=1, source_target_pairs={{0,48},{16,32},{32,16},{48,0},{1,49},{17,33},{33,17},{49,1},{2,50}... | collective-permute-start | bytes 196616 | tf_op jit(solution)/shard_map/ppermute | solution.py:293
  33.1 31.8 %collective-permute-start.16 = (bf16[512,512]{1,0:T(8,128)(2,1)S(1)}, bf16[512,512]{1,0:T(8,128)(2,1)S(1)}, u32[]{:S(2)}, u32[]{:S(2)}) collective-permute-start(bf16[512,512]{1,0:T(8,128)(2,1)S(1)} %copy-done.1), channel_id=1, source_target_pairs={{0,1},{1,0},{2,3},{3,2},{4,5},{5,4},{6,7},{7,6},{8,9},{9,8},{10,11... | collective-permute-start | bytes 1572872 | tf_op jit(solution)/shard_map/ppermute | solution.py:327
  33.1 31.8 %collective-permute-start.17 = (bf16[512,512]{1,0:T(8,128)(2,1)S(1)}, bf16[512,512]{1,0:T(8,128)(2,1)S(1)}, u32[]{:S(2)}, u32[]{:S(2)}) collective-permute-start(bf16[512,512]{1,0:T(8,128)(2,1)S(1)} %collective-permute-done.15.refs_6_), channel_id=1, source_target_pairs={{0,1},{1,0},{2,3},{3,2},{4,5},{5,4},{6,7},{7,6},{8,9},{9,8},{10,11... | collective-permute-start | bytes 1572872 | tf_op jit(solution)/shard_map/ppermute | solution.py:328
  33.6 6.2 %collective-permute-start.10 = (bf16[256,128]{1,0:T(8,128)(2,1)S(1)}, bf16[256,128]{1,0:T(8,128)(2,1)S(1)}, u32[]{:S(2)}, u32[]{:S(2)}) collective-permute-start(bf16[256,128]{1,0:T(8,128)(2,1)S(1)} %shard_map.107.refs_0_), channel_id=1, source_target_pairs={{0,32},{16,48},{32,0},{48,16},{1,33},{17,49},{33,1},{49,17},{2,34}... | collective-permute-start | bytes 196616 | tf_op jit(solution)/shard_map/ppermute | solution.py:293
  34.8 8.1 %collective-permute-start.9 = (bf16[256,128]{1,0:T(8,128)(2,1)S(1)}, bf16[256,128]{1,0:T(8,128)(2,1)S(1)}, u32[]{:S(2)}, u32[]{:S(2)}) collective-permute-start(bf16[256,128]{1,0:T(8,128)(2,1)S(1)} %shard_map.107.refs_0_), channel_id=1, source_target_pairs={{0,16},{16,0},{32,48},{48,32},{1,17},{17,1},{33,49},{49,33},{2,18}... | collective-permute-start | bytes 196616 | tf_op jit(solution)/shard_map/ppermute | solution.py:293
  37.2 7.4 %collective-permute-start = (bf16[4,128,128]{2,1,0:T(8,128)(2,1)S(1)}, bf16[4,128,128]{2,1,0:T(8,128)(2,1)S(1)}, u32[]{:S(2)}, u32[]{:S(2)}) collective-permute-start(bf16[4,128,128]{2,1,0:T(8,128)(2,1)S(1)} %get-tuple-element.29), channel_id=1, source_target_pairs={{0,64},{64,0},{128,192},{192,128},{1,65},{65,1},{129,193},{193,129... | collective-permute-start | bytes 393224 | tf_op jit(solution)/shard_map/ppermute | solution.py:293
  39.8 6.9 %collective-permute-start.1 = (bf16[4,128,128]{2,1,0:T(8,128)(2,1)S(1)}, bf16[4,128,128]{2,1,0:T(8,128)(2,1)S(1)}, u32[]{:S(2)}, u32[]{:S(2)}) collective-permute-start(bf16[4,128,128]{2,1,0:T(8,128)(2,1)S(1)} %get-tuple-element.30), channel_id=1, source_target_pairs={{0,128},{64,192},{128,0},{192,64},{1,129},{65,193},{129,1},{193,65... | collective-permute-start | bytes 393224 | tf_op jit(solution)/shard_map/ppermute | solution.py:293
  42.8 11.8 %collective-permute-start.2 = (bf16[4,128,128]{2,1,0:T(8,128)(2,1)S(1)}, bf16[4,128,128]{2,1,0:T(8,128)(2,1)S(1)}, u32[]{:S(2)}, u32[]{:S(2)}) collective-permute-start(bf16[4,128,128]{2,1,0:T(8,128)(2,1)S(1)} %get-tuple-element.31), channel_id=1, source_target_pairs={{0,192},{64,128},{128,64},{192,0},{1,193},{65,129},{129,65},{193,1... | collective-permute-start | bytes 393224 | tf_op jit(solution)/shard_map/ppermute | solution.py:293
  44.5 15.7 %collective-permute-start.14 = (bf16[1024,128]{1,0:T(8,128)(2,1)S(1)}, bf16[1024,128]{1,0:T(8,128)(2,1)S(1)}, u32[]{:S(2)}, u32[]{:S(2)}) collective-permute-start(bf16[1024,128]{1,0:T(8,128)(2,1)S(1)} %shard_map.108.refs_0_), channel_id=1, source_target_pairs={{0,192},{64,128},{128,64},{192,0},{1,193},{65,129},{129,65},{193,1... | collective-permute-start | bytes 786440 | tf_op jit(solution)/shard_map/ppermute | solution.py:293
  46.7 14.0 %collective-permute-start.13 = (bf16[1024,128]{1,0:T(8,128)(2,1)S(1)}, bf16[1024,128]{1,0:T(8,128)(2,1)S(1)}, u32[]{:S(2)}, u32[]{:S(2)}) collective-permute-start(bf16[1024,128]{1,0:T(8,128)(2,1)S(1)} %shard_map.108.refs_0_), channel_id=1, source_target_pairs={{0,128},{64,192},{128,0},{192,64},{1,129},{65,193},{129,1},{193,65... | collective-permute-start | bytes 786440 | tf_op jit(solution)/shard_map/ppermute | solution.py:293
  54.6 8.0 %collective-permute-start.12 = (bf16[1024,128]{1,0:T(8,128)(2,1)S(1)}, bf16[1024,128]{1,0:T(8,128)(2,1)S(1)}, u32[]{:S(2)}, u32[]{:S(2)}) collective-permute-start(bf16[1024,128]{1,0:T(8,128)(2,1)S(1)} %shard_map.108.refs_0_), channel_id=1, source_target_pairs={{0,64},{64,0},{128,192},{192,128},{1,65},{65,1},{129,193},{193,129... | collective-permute-start | bytes 786440 | tf_op jit(solution)/shard_map/ppermute | solution.py:293
  60.2 14.2 %collective-permute-start.3 = (bf16[4,128,128]{2,1,0:T(8,128)(2,1)S(1)}, bf16[4,128,128]{2,1,0:T(8,128)(2,1)S(1)}, u32[]{:S(2)}, u32[]{:S(2)}) collective-permute-start(bf16[4,128,128]{2,1,0:T(8,128)(2,1)S(1)} %get-tuple-element.33), channel_id=1, source_target_pairs={{0,16},{16,0},{32,48},{48,32},{1,17},{17,1},{33,49},{49,33},{2,18}... | collective-permute-start | bytes 393224 | tf_op jit(solution)/shard_map/ppermute | solution.py:293
  60.7 13.7 %collective-permute-start.4 = (bf16[4,128,128]{2,1,0:T(8,128)(2,1)S(1)}, bf16[4,128,128]{2,1,0:T(8,128)(2,1)S(1)}, u32[]{:S(2)}, u32[]{:S(2)}) collective-permute-start(bf16[4,128,128]{2,1,0:T(8,128)(2,1)S(1)} %get-tuple-element.34), channel_id=1, source_target_pairs={{0,32},{16,48},{32,0},{48,16},{1,33},{17,49},{33,1},{49,17},{2,34}... | collective-permute-start | bytes 393224 | tf_op jit(solution)/shard_map/ppermute | solution.py:293
  62.6 11.9 %collective-permute-start.5 = (bf16[4,128,128]{2,1,0:T(8,128)(2,1)S(1)}, bf16[4,128,128]{2,1,0:T(8,128)(2,1)S(1)}, u32[]{:S(2)}, u32[]{:S(2)}) collective-permute-start(bf16[4,128,128]{2,1,0:T(8,128)(2,1)S(1)} %get-tuple-element.35), channel_id=1, source_target_pairs={{0,48},{16,32},{32,16},{48,0},{1,49},{17,33},{33,17},{49,1},{2,50}... | collective-permute-start | bytes 393224 | tf_op jit(solution)/shard_map/ppermute | solution.py:293
  66.6 13.0 %collective-permute-start.18 = (bf16[64,512]{1,0:T(8,128)(2,1)S(1)}, bf16[64,512]{1,0:T(8,128)(2,1)S(1)}, u32[]{:S(2)}, u32[]{:S(2)}) collective-permute-start(bf16[64,512]{1,0:T(8,128)(2,1)S(1)} %get-tuple-element.45), channel_id=1, source_target_pairs={{0,4},{4,0},{8,12},{12,8},{1,5},{5,1},{9,13},{13,9},{2,6},{6,2},{1... | collective-permute-start | bytes 196616 | tf_op jit(solution)/shard_map/ppermute | solution.py:293
  69.9 9.7 %collective-permute-start.19 = (bf16[64,512]{1,0:T(8,128)(2,1)S(1)}, bf16[64,512]{1,0:T(8,128)(2,1)S(1)}, u32[]{:S(2)}, u32[]{:S(2)}) collective-permute-start(bf16[64,512]{1,0:T(8,128)(2,1)S(1)} %get-tuple-element.46), channel_id=1, source_target_pairs={{0,8},{4,12},{8,0},{12,4},{1,9},{5,13},{9,1},{13,5},{2,10},{6,14},... | collective-permute-start | bytes 196616 | tf_op jit(solution)/shard_map/ppermute | solution.py:293
  74.4 7.1 %collective-permute-start.20 = (bf16[64,512]{1,0:T(8,128)(2,1)S(1)}, bf16[64,512]{1,0:T(8,128)(2,1)S(1)}, u32[]{:S(2)}, u32[]{:S(2)}) collective-permute-start(bf16[64,512]{1,0:T(8,128)(2,1)S(1)} %get-tuple-element.47), channel_id=1, source_target_pairs={{0,12},{4,8},{8,4},{12,0},{1,13},{5,9},{9,5},{13,1},{2,14},{6,10},... | collective-permute-start | bytes 196616 | tf_op jit(solution)/shard_map/ppermute | solution.py:293

commit v5 on v4

--- a/solution.py
+++ b/solution.py
@@ -64,29 +64,72 @@
     return call
 
 
-def states_body(k_ref, v_ref, tq_ref, tk_ref, tv_ref, o_ref):
-    heads = o_ref.shape[0]
-    nodes = tq_ref.shape[1]
-    for h in range(heads):
-        cols = slice(h * DH, (h + 1) * DH)
-        kv = mm(k_ref[0, :, cols], v_ref[0, :, cols], 0, 0)
-        o_ref[h, 0:DH, :] = kv.astype(BF)
-        for j, ref in enumerate((tq_ref, tk_ref, tv_ref)):
-            o_ref[h, DH + j * nodes : DH + (j + 1) * nodes, :] = ref[0, :, cols]
+def states_body(k_ref, v_ref, tq_ref, tk_ref, tv_ref, o_ref, ks, vs, ts, outs, sems, done):
+    requests, tokens = k_ref.shape[:2]
+    nodes, half = tq_ref.shape[1], tokens // 2
+    thin = [
+        pltpu.make_async_copy(ref, ts.at[j], sems.at[2, j])
+        for j, ref in enumerate((tq_ref, tk_ref, tv_ref))
+    ]
+    steps = [(r, slice(t * half, (t + 1) * half)) for r in range(requests) for t in range(2)]
+    loads = [
+        [
+            pltpu.make_async_copy(ref.at[r, rows], buf.at[r, rows], sems.at[m, n])
+            for m, (ref, buf) in enumerate(((k_ref, ks), (v_ref, vs)))
+        ]
+        for n, (r, rows) in enumerate(steps)
+    ]
+    stores = [
+        pltpu.make_async_copy(
+            outs.at[r * SIDE : (r + 1) * SIDE], o_ref.at[r * SIDE : (r + 1) * SIDE], done.at[r]
+        )
+        for r in range(requests)
+    ]
+    for copy in thin + sum(loads, []):
+        copy.start()
+    for n, (r, rows) in enumerate(steps):
+        for copy in loads[n]:
+            copy.wait()
+        if n == 0:
+            for copy in thin:
+                copy.wait()
+        if n % 2 == 0:
+            total = [None] * SIDE
+        for pair in range(SIDE // 2):
+            cols = slice(2 * pair * DH, 2 * (pair + 1) * DH)
+            both = mm(ks[r, rows, cols], vs[r, rows, cols], 0, 0)
+            for h in range(2):
+                kv = both[h * DH : (h + 1) * DH, h * DH : (h + 1) * DH]
+                at = 2 * pair + h
+                total[at] = kv if n % 2 == 0 else total[at] + kv
+        if n % 2 == 1:
+            for h in range(SIDE):
+                outs[r * SIDE + h, 0:DH, :] = total[h].astype(BF)
+                for j in range(3):
+                    rows_at = slice(DH + j * nodes, DH + (j + 1) * nodes)
+                    outs[r * SIDE + h, rows_at, :] = ts[j, r, :, h * DH : (h + 1) * DH]
+            stores[r].start()
+    for copy in stores:
+        copy.wait()
 
 
 def block_states(k, v, tq, tk, tv):
     requests, tokens, width = k.shape
-    heads, nodes = width // DH, tq.shape[1]
+    nodes = tq.shape[1]
     rows = DH + 3 * nodes
-    big = pl.BlockSpec((1, tokens, width), lambda r: (r, 0, 0))
-    small = pl.BlockSpec((1, nodes, width), lambda r: (r, 0, 0))
     return pl.pallas_call(
         states_body,
-        grid=(requests,),
-        in_specs=[big, big, small, small, small],
-        out_specs=pl.BlockSpec((heads, rows, DH), lambda r: (r, 0, 0)),
-        out_shape=like((requests * heads, rows, DH)),
+        in_specs=[pl.BlockSpec(memory_space=pltpu.HBM)] * 5,
+        out_specs=pl.BlockSpec(memory_space=pltpu.HBM),
+        out_shape=pltpu.HBM((requests * SIDE, rows, DH), BF),
+        scratch_shapes=[
+            pltpu.VMEM(k.shape, BF),
+            pltpu.VMEM(v.shape, BF),
+            pltpu.VMEM((3, *tq.shape), BF),
+            pltpu.VMEM((requests * SIDE, rows, DH), BF),
+            pltpu.SemaphoreType.DMA((3, 2 * requests)),
+            pltpu.SemaphoreType.DMA((requests,)),
+        ],
         cost_estimate=cost(2 * requests * tokens * width * DH, 4 * requests * tokens * width),
         compiler_params=room(16),
         name="block_states",
@@ -148,7 +191,8 @@
             hold[y, x] = running.astype(BF)
             running = running + got_ref[y * SIDE + x, 0:DH, :].astype(F32)
     for s, out in enumerate(outs):
-        out[...] = hold[at_ref[1] ^ s]
+        for y in range(SIDE):
+            out[y] = hold[y, at_ref[0] ^ s]
 
 
 def prefixes(at, got, prior):
@@ -161,7 +205,7 @@
     got, outs = refs[:SIDE], refs[SIDE:]
     for s, out in enumerate(outs):
         for t in range(SIDE):
-            out[at_ref[1] ^ t] = got[t][at_ref[0] ^ s]
+            out[at_ref[0] ^ t] = got[t][at_ref[1] ^ s]
 
 
 def regrouped(at, got):
@@ -214,34 +258,37 @@
 
 
 def finish_body(at_ref, q_ref, inner_ref, *refs):
-    states, o_ref, hold = refs[:SIDE], refs[SIDE], refs[SIDE + 1]
-    r = pl.program_id(0)
-
-    @pl.when(r == 0)
-    def _():
-        for s in range(SIDE):
-            hold[at_ref[0] ^ s] = states[s][...]
-
-    for h in range(SIDE):
-        cols = slice(h * DH, (h + 1) * DH)
-        raw = mm(q_ref[0, :, cols], hold[h, r], 1, 0) + inner_ref[0, :, cols].astype(F32)
-        o_ref[0, :, cols] = normed(raw).astype(BF)
+    states, (o_ref, hold, outs, sems) = refs[:SIDE], refs[SIDE:]
+    requests, _, _ = q_ref.shape
+    for s in range(SIDE):
+        hold[at_ref[1] ^ s] = states[s][...]
+    stores = [pltpu.make_async_copy(outs.at[r], o_ref.at[r], sems.at[r]) for r in range(requests)]
+    for r in range(requests):
+        for h in range(SIDE):
+            cols = slice(h * DH, (h + 1) * DH)
+            raw = mm(q_ref[r, :, cols], hold[r, h], 1, 0) + inner_ref[r, :, cols].astype(F32)
+            outs[r, :, cols] = normed(raw).astype(BF)
+        stores[r].start()
+    for copy in stores:
+        copy.wait()
 
 
 def finish(at, q, inner, states):
     requests, tokens, width = q.shape
-    big = pl.BlockSpec((1, tokens, width), lambda r: (r, 0, 0))
     return pl.pallas_call(
         finish_body,
-        grid=(requests,),
-        in_specs=[smem(), big, big] + vmem(SIDE),
-        out_specs=big,
+        in_specs=[smem()] + vmem(2 + SIDE),
+        out_specs=pl.BlockSpec(memory_space=pltpu.HBM),
         out_shape=like(q.shape),
-        scratch_shapes=[pltpu.VMEM((SIDE, requests, DH, DH), BF)],
+        scratch_shapes=[
+            pltpu.VMEM((SIDE, requests, DH, DH), BF),
+            pltpu.VMEM(q.shape, BF),
+            pltpu.SemaphoreType.DMA((requests,)),
+        ],
         cost_estimate=cost(2 * requests * tokens * width * DH, 6 * requests * tokens * width),
         compiler_params=room(16),
         name="finish",
-    )(at, far(q), far(inner), *states)
+    )(at, q, inner, *states)
 
 
 def project_body(at_ref, *refs):
@@ -289,9 +336,10 @@
 
 
 def exchanged(arrays, axis):
-    pairs = [[(i, i ^ s) for i in range(SIDE)] for s in range(SIDE)]
-    got = {s: lax.ppermute(arrays[s], axis, pairs[s]) for s in (2, 1, 3)}
-    return [arrays[0], got[1], got[2], got[3]]
+    got = [arrays[0]]
+    for s in range(1, SIDE):
+        got.append(lax.ppermute(arrays[s], axis, [(i, i ^ s) for i in range(SIDE)]))
+    return got
 
 
 def on_device(q, k, v, prior, tq, tk, tv, parents, weight):
@@ -319,19 +367,22 @@
     from_z = lax.ppermute(pieces[2], "zl", swap)
     from_zc = lax.ppermute(pieces[3], quad, crossed)
     before = prefixes(at, got, own_prior)
+    from_c, from_z, from_zc, *before = lax.optimization_barrier(
+        (from_c, from_z, from_zc, *before)
+    )
     mine = joined(at, (pieces[0], from_c, from_z, from_zc))
     heads = exchanged([mine] * SIDE, "x")
-    above = exchanged(before, "y")
+    beside = exchanged(before, "x")
     row_of_heads = joined(at, heads)
-    weight, w_z, _ = lax.optimization_barrier((weight, w_z, mine))
+    rows = exchanged([row_of_heads] * SIDE, "y")
     w_c = lax.ppermute(weight, "c", swap)
     w_zc = lax.ppermute(w_z, "c", swap)
-    rows = exchanged([row_of_heads] * SIDE, "y")
-    states = exchanged(regrouped(at, above), "x")
+    states = exchanged(regrouped(at, beside), "y")
 
     parts = project(at, rows, (weight, w_c, w_z, w_zc))
     total = parts[0].astype(F32)
-    for got in exchanged(parts, "zp")[1:]:
+    shares = exchanged(parts, "zp")
+    for got in shares[1:]:
         total = total + got.astype(F32)
     verified = total.astype(BF)
 

time: 82.6 us -> 86.9 us (1.052)
  the two profiles are of different devices: /device:TPU:32 before, /device:TPU:24 now
where the time goes in v5:
time: 86.9 us; the launch traced here: 86.6 us
  starting transfers between devices  37.6 us (43%)
  waiting for transfers between devices  23.3 us (27%)
  Pallas kernels  21.7 us (25%)
  local copies, waits for them, and re-layouts  2.38 us (3%)
    ppermute x15, starting transfers between devices, exchanged(): got.append(lax.ppermute(arrays[s], axis, [(i, i ^ s) for i in range(SIDE)]))  26.1 us
    ppermute x15, waiting for transfers between devices, exchanged(): got.append(lax.ppermute(arrays[s], axis, [(i, i ^ s) for i in range(SIDE)]))  18.2 us
    pallas_call x1, Pallas kernels, inside(): pl.pallas_call(body, grid=(count,), in_specs=[big, big, big] + [pl.BlockS...  8.08 us
    all_to_all x1, starting transfers between devices, on_device(): got = lax.all_to_all(sent, SEQ, 0, 0, tiled=True)  7.18 us
    pallas_call x1, Pallas kernels, block_states(): pl.pallas_call(states_body, in_specs=[pl.BlockSpec(memory_space=pltpu.HBM...  3.9 us
    pallas_call x5, Pallas kernels, call(): pl.pallas_call(body, in_specs=[smem()] + vmem(len(arrays)), out_specs=vme...  3.34 us
    pallas_call x1, Pallas kernels, finish(): pl.pallas_call(finish_body, in_specs=[smem()] + vmem(2 + SIDE), out_specs...  2.75 us
    ppermute x1, waiting for transfers between devices, on_device(): w_z = lax.ppermute(weight, 'zl', swap)  2.5 us
  transfers between devices with their start and end apart: 22, of which 10 were waited for; matrix products, arithmetic and copies ran while one was open for 1% of the time, Pallas kernels for 21%

profile of v5, /device:TPU:24, one launch (start us, length us, event | category | flops | bytes accessed | tf_op | source)
XLA Modules:
  0.0 86.6 jit_solution(13110409962895139988)
XLA Ops:
  0.7 3.9 %block_states.1 = bf16[16,176,128]{2,1,0:T(8,128)(2,1)} custom-call(bf16[4,512,512]{2,1,0:T(8,128)(2,1)} %k_ref.3, bf16[4,512,512]{2,1,0:T(8,128)(2,1)} %v_ref.3, bf16[4,16,512]{2,1,0:T(8,128)(2,1)} %tq_ref.1, bf16[4,16,512]{2,1,0:T(8,128)(2,1)} %tk_ref.1, bf16[4,16,512]{2,1,0:T(8,128)(2,1)} %tv_ref.1), custom_call_target="tpu_custom_call" | custom-call | flops 268435456 | bytes 4194304 | tf_op jit(solution)/shard_map/block_states/pallas_call | solution.py:120
  4.6 7.2 %all-to-all-start = ((bf16[16,176,128]{2,1,0:T(8,128)(2,1)}), bf16[16,176,128]{2,1,0:T(8,128)(2,1)S(1)}, u32[]{:S(2)}, u32[]{:S(2)}) async-start(bf16[16,176,128]{2,1,0:T(8,128)(2,1)} %block_states.1), calls=%async_computation | async-start | bytes 1441792 | tf_op jit(solution)/shard_map/all_to_all | solution.py:356
  11.8 2.0 %collective-permute-start.16 = (bf16[512,512]{1,0:T(8,128)(2,1)S(1)}, bf16[512,512]{1,0:T(8,128)(2,1)S(1)}, u32[]{:S(2)}, u32[]{:S(2)}) collective-permute-start(bf16[512,512]{1,0:T(8,128)(2,1)S(1)} %copy-done.3), channel_id=1, source_target_pairs={{0,2},{2,0},{1,3},{3,1},{4,6},{6,4},{5,7},{7,5},{8,10},{10,8},{9,1... | collective-permute-start | bytes 1572872 | tf_op jit(solution)/shard_map/ppermute | solution.py:358
  14.5 8.1 %inside.1.inner_ref = bf16[4,512,512]{2,1,0:T(8,128)(2,1)} custom-call(bf16[4,512,512]{2,1,0:T(8,128)(2,1)} %q_ref.3, bf16[4,512,512]{2,1,0:T(8,128)(2,1)} %k_ref.3, bf16[4,512,512]{2,1,0:T(8,128)(2,1)} %v_ref.3), custom_call_target="tpu_custom_call" | custom-call | flops 1610612736 | bytes 8388608 | tf_op jit(solution)/shard_map/inside/pallas_call | solution.py:247
  22.6 2.5 %collective-permute-done.16.refs_6_ = bf16[512,512]{1,0:T(8,128)(2,1)S(1)} collective-permute-done((bf16[512,512]{1,0:T(8,128)(2,1)S(1)}, bf16[512,512]{1,0:T(8,128)(2,1)S(1)}, u32[]{:S(2)}, u32[]{:S(2)}) %collective-permute-start.16) | collective-permute-done | bytes 524320 | tf_op jit(solution)/shard_map/ppermute | solution.py:358
  25.1 1.6 %ancestors.1.reach_ref = f32[256,256]{1,0:T(8,128)S(1)} custom-call(s32[1,256]{1,0:T(1,128)S(1)} %constant_dynamic-slice_fusion.parents_ref), custom_call_target="tpu_custom_call" | custom-call | flops 268435456 | bytes 262144 | tf_op jit(solution)/shard_map/ancestors/pallas_call | solution.py:150
  27.4 0.9 %copy-done.5 = f32[256,256]{1,0:T(8,128)S(1)} copy-done((f32[256,256]{1,0:T(8,128)S(1)}, f32[256,256]{1,0:T(8,128)}, u32[]{:S(2)}) %copy-start.5) | copy-done | bytes 262168
  28.4 1.0 %shard_map.104 = (bf16[64,128]{1,0:T(8,128)(2,1)S(1)}, bf16[64,128]{1,0:T(8,128)(2,1)S(1)}, bf16[64,128]{1,0:T(8,128)(2,1)S(1)}, bf16[64,128]{1,0:T(8,128)(2,1)S(1)}) custom-call(s32[4]{0:T(128)S(1)} %pad_add_fusion.at_ref, bf16[16,176,128]{2,1,0:T(8,128)(2,1)S(1)} %all-to-all-done.got_ref, f32[128,128]{1,0:T(8,128)S(1)} %dynamic-slice_bitcast_fusion.prior_ref, ...), custom_call_target="tpu_custom_call" | custom-call | flops 50331648 | bytes 2097152 | tf_op jit(solution)/shard_map/pallas_call | solution.py:54
  30.0 1.7 %collective-permute-start.1 = (bf16[64,128]{1,0:T(8,128)(2,1)S(1)}, bf16[64,128]{1,0:T(8,128)(2,1)S(1)}, u32[]{:S(2)}, u32[]{:S(2)}) collective-permute-start(bf16[64,128]{1,0:T(8,128)(2,1)S(1)} %get-tuple-element.35), channel_id=1, source_target_pairs={{0,2},{2,0},{1,3},{3,1},{4,6},{6,4},{5,7},{7,5},{8,10},{10,8},{9,1... | collective-permute-start | bytes 49160 | tf_op jit(solution)/shard_map/ppermute | solution.py:367
  32.4 1.3 %collective-permute-done.1.refs_2_ = bf16[64,128]{1,0:T(8,128)(2,1)S(1)} collective-permute-done((bf16[64,128]{1,0:T(8,128)(2,1)S(1)}, bf16[64,128]{1,0:T(8,128)(2,1)S(1)}, u32[]{:S(2)}, u32[]{:S(2)}) %collective-permute-start.1) | collective-permute-done | bytes 16416 | tf_op jit(solution)/shard_map/ppermute | solution.py:367
  33.7 1.3 %collective-permute-done.2.refs_3_ = bf16[64,128]{1,0:T(8,128)(2,1)S(1)} collective-permute-done((bf16[64,128]{1,0:T(8,128)(2,1)S(1)}, bf16[64,128]{1,0:T(8,128)(2,1)S(1)}, u32[]{:S(2)}, u32[]{:S(2)}) %collective-permute-start.2) | collective-permute-done | bytes 16416 | tf_op jit(solution)/shard_map/ppermute | solution.py:368
  35.6 1.6 %collective-permute-start.9 = (bf16[256,128]{1,0:T(8,128)(2,1)S(1)}, bf16[256,128]{1,0:T(8,128)(2,1)S(1)}, u32[]{:S(2)}, u32[]{:S(2)}) collective-permute-start(bf16[256,128]{1,0:T(8,128)(2,1)S(1)} %shard_map.107.refs_0_), channel_id=1, source_target_pairs={{0,16},{16,0},{32,48},{48,32},{1,17},{17,1},{33,49},{49,33},{2,18}... | collective-permute-start | bytes 196616 | tf_op jit(solution)/shard_map/ppermute | solution.py:341
  37.2 2.7 %collective-permute-start.10 = (bf16[256,128]{1,0:T(8,128)(2,1)S(1)}, bf16[256,128]{1,0:T(8,128)(2,1)S(1)}, u32[]{:S(2)}, u32[]{:S(2)}) collective-permute-start(bf16[256,128]{1,0:T(8,128)(2,1)S(1)} %shard_map.107.refs_0_), channel_id=1, source_target_pairs={{0,32},{16,48},{32,0},{48,16},{1,33},{17,49},{33,1},{49,17},{2,34}... | collective-permute-start | bytes 196616 | tf_op jit(solution)/shard_map/ppermute | solution.py:341
  40.4 1.0 %collective-permute-start.3 = (bf16[4,128,128]{2,1,0:T(8,128)(2,1)S(1)}, bf16[4,128,128]{2,1,0:T(8,128)(2,1)S(1)}, u32[]{:S(2)}, u32[]{:S(2)}) collective-permute-start(bf16[4,128,128]{2,1,0:T(8,128)(2,1)S(1)} %get-tuple-element.42), channel_id=1, source_target_pairs={{0,16},{16,0},{32,48},{48,32},{1,17},{17,1},{33,49},{49,33},{2,18}... | collective-permute-start | bytes 393224 | tf_op jit(solution)/shard_map/ppermute | solution.py:341
  41.5 1.9 %collective-permute-done.10.refs_2_ = bf16[256,128]{1,0:T(8,128)(2,1)S(1)} collective-permute-done((bf16[256,128]{1,0:T(8,128)(2,1)S(1)}, bf16[256,128]{1,0:T(8,128)(2,1)S(1)}, u32[]{:S(2)}, u32[]{:S(2)}) %collective-permute-start.10) | collective-permute-done | bytes 65568 | tf_op jit(solution)/shard_map/ppermute | solution.py:341
  43.4 3.0 %collective-permute-start.4 = (bf16[4,128,128]{2,1,0:T(8,128)(2,1)S(1)}, bf16[4,128,128]{2,1,0:T(8,128)(2,1)S(1)}, u32[]{:S(2)}, u32[]{:S(2)}) collective-permute-start(bf16[4,128,128]{2,1,0:T(8,128)(2,1)S(1)} %get-tuple-element.43), channel_id=1, source_target_pairs={{0,32},{16,48},{32,0},{48,16},{1,33},{17,49},{33,1},{49,17},{2,34}... | collective-permute-start | bytes 393224 | tf_op jit(solution)/shard_map/ppermute | solution.py:341
  47.1 0.9 %collective-permute-start.12 = (bf16[1024,128]{1,0:T(8,128)(2,1)S(1)}, bf16[1024,128]{1,0:T(8,128)(2,1)S(1)}, u32[]{:S(2)}, u32[]{:S(2)}) collective-permute-start(bf16[1024,128]{1,0:T(8,128)(2,1)S(1)} %shard_map.108.refs_0_), channel_id=1, source_target_pairs={{0,64},{64,0},{128,192},{192,128},{1,65},{65,1},{129,193},{193,129... | collective-permute-start | bytes 786440 | tf_op jit(solution)/shard_map/ppermute | solution.py:341
  48.1 2.5 %collective-permute-done.4.refs_2_ = bf16[4,128,128]{2,1,0:T(8,128)(2,1)S(1)} collective-permute-done((bf16[4,128,128]{2,1,0:T(8,128)(2,1)S(1)}, bf16[4,128,128]{2,1,0:T(8,128)(2,1)S(1)}, u32[]{:S(2)}, u32[]{:S(2)}) %collective-permute-start.4) | collective-permute-done | bytes 131104 | tf_op jit(solution)/shard_map/ppermute | solution.py:341
  50.5 1.5 %collective-permute-start.13 = (bf16[1024,128]{1,0:T(8,128)(2,1)S(1)}, bf16[1024,128]{1,0:T(8,128)(2,1)S(1)}, u32[]{:S(2)}, u32[]{:S(2)}) collective-permute-start(bf16[1024,128]{1,0:T(8,128)(2,1)S(1)} %shard_map.108.refs_0_), channel_id=1, source_target_pairs={{0,128},{64,192},{128,0},{192,64},{1,129},{65,193},{129,1},{193,65... | collective-permute-start | bytes 786440 | tf_op jit(solution)/shard_map/ppermute | solution.py:341
  52.0 0.8 collective-permute-done.5.refs_3_
  52.8 1.3 %collective-permute-start.14 = (bf16[1024,128]{1,0:T(8,128)(2,1)S(1)}, bf16[1024,128]{1,0:T(8,128)(2,1)S(1)}, u32[]{:S(2)}, u32[]{:S(2)}) collective-permute-start(bf16[1024,128]{1,0:T(8,128)(2,1)S(1)} %shard_map.108.refs_0_), channel_id=1, source_target_pairs={{0,192},{64,128},{128,64},{192,0},{1,193},{65,129},{129,65},{193,1... | collective-permute-start | bytes 786440 | tf_op jit(solution)/shard_map/ppermute | solution.py:341
  54.9 1.5 %collective-permute-done.12.refs_1_ = bf16[1024,128]{1,0:T(8,128)(2,1)S(1)} collective-permute-done((bf16[1024,128]{1,0:T(8,128)(2,1)S(1)}, bf16[1024,128]{1,0:T(8,128)(2,1)S(1)}, u32[]{:S(2)}, u32[]{:S(2)}) %collective-permute-start.12) | collective-permute-done | bytes 262176 | tf_op jit(solution)/shard_map/ppermute | solution.py:341
  56.4 1.8 %collective-permute-start.7 = (bf16[4,128,128]{2,1,0:T(8,128)(2,1)S(1)}, bf16[4,128,128]{2,1,0:T(8,128)(2,1)S(1)}, u32[]{:S(2)}, u32[]{:S(2)}) collective-permute-start(bf16[4,128,128]{2,1,0:T(8,128)(2,1)S(1)} %get-tuple-element.47), channel_id=1, source_target_pairs={{0,128},{64,192},{128,0},{192,64},{1,129},{65,193},{129,1},{193,65... | collective-permute-start | bytes 393224 | tf_op jit(solution)/shard_map/ppermute | solution.py:341
  58.1 3.1 %collective-permute-done.13.refs_2_ = bf16[1024,128]{1,0:T(8,128)(2,1)S(1)} collective-permute-done((bf16[1024,128]{1,0:T(8,128)(2,1)S(1)}, bf16[1024,128]{1,0:T(8,128)(2,1)S(1)}, u32[]{:S(2)}, u32[]{:S(2)}) %collective-permute-start.13) | collective-permute-done | bytes 262176 | tf_op jit(solution)/shard_map/ppermute | solution.py:341
  61.3 3.5 %collective-permute-start.8 = (bf16[4,128,128]{2,1,0:T(8,128)(2,1)S(1)}, bf16[4,128,128]{2,1,0:T(8,128)(2,1)S(1)}, u32[]{:S(2)}, u32[]{:S(2)}) collective-permute-start(bf16[4,128,128]{2,1,0:T(8,128)(2,1)S(1)} %get-tuple-element.48), channel_id=1, source_target_pairs={{0,192},{64,128},{128,64},{192,0},{1,193},{65,129},{129,65},{193,1... | collective-permute-start | bytes 393224 | tf_op jit(solution)/shard_map/ppermute | solution.py:341
  64.7 3.6 %collective-permute-done.14.refs_3_ = bf16[1024,128]{1,0:T(8,128)(2,1)S(1)} collective-permute-done((bf16[1024,128]{1,0:T(8,128)(2,1)S(1)}, bf16[1024,128]{1,0:T(8,128)(2,1)S(1)}, u32[]{:S(2)}, u32[]{:S(2)}) %collective-permute-start.14) | collective-permute-done | bytes 262176 | tf_op jit(solution)/shard_map/ppermute | solution.py:341
  68.3 2.0 %project.1 = (bf16[64,512]{1,0:T(8,128)(2,1)S(1)}, bf16[64,512]{1,0:T(8,128)(2,1)S(1)}, bf16[64,512]{1,0:T(8,128)(2,1)S(1)}, bf16[64,512]{1,0:T(8,128)(2,1)S(1)}) custom-call(s32[4]{0:T(128)S(1)} %pad_add_fusion.at_ref, bf16[1024,128]{1,0:T(8,128)(2,1)S(1)} %shard_map.108.refs_0_, bf16[1024,128]{1,0:T(8,128)(2,1)S(1)} %collective-permute-done.12.refs_1_, ...), custom_call_target="tpu_custom_call" | custom-call | flops 536870912 | bytes 2097152 | tf_op jit(solution)/shard_map/project/pallas_call | solution.py:322
  70.3 5.5 %collective-permute-start.20 = (bf16[64,512]{1,0:T(8,128)(2,1)S(1)}, bf16[64,512]{1,0:T(8,128)(2,1)S(1)}, u32[]{:S(2)}, u32[]{:S(2)}) collective-permute-start(bf16[64,512]{1,0:T(8,128)(2,1)S(1)} %get-tuple-element.57), channel_id=1, source_target_pairs={{0,12},{4,8},{8,4},{12,0},{1,13},{5,9},{9,5},{13,1},{2,14},{6,10},... | collective-permute-start | bytes 196616 | tf_op jit(solution)/shard_map/ppermute | solution.py:341
  75.8 1.4 %collective-permute-start.19 = (bf16[64,512]{1,0:T(8,128)(2,1)S(1)}, bf16[64,512]{1,0:T(8,128)(2,1)S(1)}, u32[]{:S(2)}, u32[]{:S(2)}) collective-permute-start(bf16[64,512]{1,0:T(8,128)(2,1)S(1)} %get-tuple-element.56), channel_id=1, source_target_pairs={{0,8},{4,12},{8,0},{12,4},{1,9},{5,13},{9,1},{13,5},{2,10},{6,14},... | collective-permute-start | bytes 196616 | tf_op jit(solution)/shard_map/ppermute | solution.py:341
  77.3 1.0 %collective-permute-start.18 = (bf16[64,512]{1,0:T(8,128)(2,1)S(1)}, bf16[64,512]{1,0:T(8,128)(2,1)S(1)}, u32[]{:S(2)}, u32[]{:S(2)}) collective-permute-start(bf16[64,512]{1,0:T(8,128)(2,1)S(1)} %get-tuple-element.55), channel_id=1, source_target_pairs={{0,4},{4,0},{8,12},{12,8},{1,5},{5,1},{9,13},{13,9},{2,6},{6,2},{1... | collective-permute-start | bytes 196616 | tf_op jit(solution)/shard_map/ppermute | solution.py:341
  78.3 2.7 %finish.1 = bf16[4,512,512]{2,1,0:T(8,128)(2,1)} custom-call(s32[4]{0:T(128)S(1)} %pad_add_fusion.at_ref, bf16[4,512,512]{2,1,0:T(8,128)(2,1)S(1)} %copy-done.1, bf16[4,512,512]{2,1,0:T(8,128)(2,1)S(1)} %copy-done.2, bf16[4,128,128]{2,1,0:T(8,128)(2,1)S(1)} %get-tuple-element.45.refs_0_, bf16[4,128,128]{2,1,0:T(8,128)(2,1)S(1)} %collective-permute-done.6.refs_1_, ...), custom_call_target="tpu_custom_call" | custom-call | flops 268435456 | bytes 6291456 | tf_op jit(solution)/shard_map/finish/pallas_call | solution.py:278
  81.1 4.8 %collective-permute-done.19 = bf16[64,512]{1,0:T(8,128)(2,1)S(1)} collective-permute-done((bf16[64,512]{1,0:T(8,128)(2,1)S(1)}, bf16[64,512]{1,0:T(8,128)(2,1)S(1)}, u32[]{:S(2)}, u32[]{:S(2)}) %collective-permute-start.19) | collective-permute-done | bytes 65568 | tf_op jit(solution)/shard_map/ppermute | solution.py:341
  (38 shorter events, 6.1 us)
Async XLA Ops:
  0.6 13.8 %copy-start = (f32[4,4,128,128]{3,2,1,0:T(8,128)S(1)}, f32[4,4,128,128]{3,2,1,0:T(8,128)}, u32[]{:S(2)}) copy-start(f32[4,4,128,128]{3,2,1,0:T(8,128)} %param.12) | copy-start | bytes 3145732
  0.6 11.1 %copy-start.3 = (bf16[512,512]{1,0:T(8,128)(2,1)S(1)}, bf16[512,512]{1,0:T(8,128)(2,1)}, u32[]{:S(2)}) copy-start(bf16[512,512]{1,0:T(8,128)(2,1)} %refs_4_) | copy-start | bytes 1572868
  4.6 22.9 %all-to-all-start = ((bf16[16,176,128]{2,1,0:T(8,128)(2,1)}), bf16[16,176,128]{2,1,0:T(8,128)(2,1)S(1)}, u32[]{:S(2)}, u32[]{:S(2)}) async-start(bf16[16,176,128]{2,1,0:T(8,128)(2,1)} %block_states.1), calls=%async_computation | async-start | bytes 1441792 | tf_op jit(solution)/shard_map/all_to_all | solution.py:356
  11.8 13.4 %collective-permute-start.16 = (bf16[512,512]{1,0:T(8,128)(2,1)S(1)}, bf16[512,512]{1,0:T(8,128)(2,1)S(1)}, u32[]{:S(2)}, u32[]{:S(2)}) collective-permute-start(bf16[512,512]{1,0:T(8,128)(2,1)S(1)} %copy-done.3), channel_id=1, source_target_pairs={{0,2},{2,0},{1,3},{3,1},{4,6},{6,4},{5,7},{7,5},{8,10},{10,8},{9,1... | collective-permute-start | bytes 1572872 | tf_op jit(solution)/shard_map/ppermute | solution.py:358
  13.8 40.9 %collective-permute-start.15 = (bf16[512,512]{1,0:T(8,128)(2,1)S(1)}, bf16[512,512]{1,0:T(8,128)(2,1)S(1)}, u32[]{:S(2)}, u32[]{:S(2)}) collective-permute-start(bf16[512,512]{1,0:T(8,128)(2,1)S(1)} %copy-done.3), channel_id=1, source_target_pairs={{0,1},{1,0},{2,3},{3,2},{4,5},{5,4},{6,7},{7,6},{8,9},{9,8},{10,11... | collective-permute-start | bytes 1572872 | tf_op jit(solution)/shard_map/ppermute | solution.py:378
  25.1 43.2 %collective-permute-start.17 = (bf16[512,512]{1,0:T(8,128)(2,1)S(1)}, bf16[512,512]{1,0:T(8,128)(2,1)}, u32[]{:S(2)}, u32[]{:S(2)}) collective-permute-start(bf16[512,512]{1,0:T(8,128)(2,1)S(1)} %collective-permute-done.16.refs_6_), channel_id=1, source_target_pairs={{0,1},{1,0},{2,3},{3,2},{4,5},{5,4},{6,7},{7,6},{8,9},{9,8},{10,11... | collective-permute-start | bytes 1572872 | tf_op jit(solution)/shard_map/ppermute | solution.py:379
  26.7 0.7 copy-start.4
  27.4 1.0 %copy-start.5 = (f32[256,256]{1,0:T(8,128)S(1)}, f32[256,256]{1,0:T(8,128)}, u32[]{:S(2)}) copy-start(f32[256,256]{1,0:T(8,128)} %copy-done.4) | copy-start | bytes 786436
  29.4 3.0 %collective-permute-start = (bf16[64,128]{1,0:T(8,128)(2,1)S(1)}, bf16[64,128]{1,0:T(8,128)(2,1)S(1)}, u32[]{:S(2)}, u32[]{:S(2)}) collective-permute-start(bf16[64,128]{1,0:T(8,128)(2,1)S(1)} %get-tuple-element.34), channel_id=1, source_target_pairs={{0,1},{1,0},{2,3},{3,2},{4,5},{5,4},{6,7},{7,6},{8,9},{9,8},{10,11... | collective-permute-start | bytes 49160 | tf_op jit(solution)/shard_map/ppermute | solution.py:366
  30.0 3.7 %collective-permute-start.1 = (bf16[64,128]{1,0:T(8,128)(2,1)S(1)}, bf16[64,128]{1,0:T(8,128)(2,1)S(1)}, u32[]{:S(2)}, u32[]{:S(2)}) collective-permute-start(bf16[64,128]{1,0:T(8,128)(2,1)S(1)} %get-tuple-element.35), channel_id=1, source_target_pairs={{0,2},{2,0},{1,3},{3,1},{4,6},{6,4},{5,7},{7,5},{8,10},{10,8},{9,1... | collective-permute-start | bytes 49160 | tf_op jit(solution)/shard_map/ppermute | solution.py:367
  31.7 3.3 %collective-permute-start.2 = (bf16[64,128]{1,0:T(8,128)(2,1)S(1)}, bf16[64,128]{1,0:T(8,128)(2,1)S(1)}, u32[]{:S(2)}, u32[]{:S(2)}) collective-permute-start(bf16[64,128]{1,0:T(8,128)(2,1)S(1)} %get-tuple-element.36), channel_id=1, source_target_pairs={{0,3},{1,2},{2,1},{3,0},{4,7},{5,6},{6,5},{7,4},{8,11},{9,10},{10,... | collective-permute-start | bytes 49160 | tf_op jit(solution)/shard_map/ppermute | solution.py:368
  35.6 42.7 %copy-start.1 = (bf16[4,512,512]{2,1,0:T(8,128)(2,1)S(1)}, bf16[4,512,512]{2,1,0:T(8,128)(2,1)}, u32[]{:S(2)}) copy-start(bf16[4,512,512]{2,1,0:T(8,128)(2,1)} %q_ref.3) | copy-start | bytes 6291460
  35.6 42.7 %copy-start.2 = (bf16[4,512,512]{2,1,0:T(8,128)(2,1)S(1)}, bf16[4,512,512]{2,1,0:T(8,128)(2,1)}, u32[]{:S(2)}) copy-start(bf16[4,512,512]{2,1,0:T(8,128)(2,1)} %inside.1.inner_ref) | copy-start | bytes 6291460
  35.6 4.8 %collective-permute-start.9 = (bf16[256,128]{1,0:T(8,128)(2,1)S(1)}, bf16[256,128]{1,0:T(8,128)(2,1)S(1)}, u32[]{:S(2)}, u32[]{:S(2)}) collective-permute-start(bf16[256,128]{1,0:T(8,128)(2,1)S(1)} %shard_map.107.refs_0_), channel_id=1, source_target_pairs={{0,16},{16,0},{32,48},{48,32},{1,17},{17,1},{33,49},{49,33},{2,18}... | collective-permute-start | bytes 196616 | tf_op jit(solution)/shard_map/ppermute | solution.py:341
  37.2 6.2 %collective-permute-start.10 = (bf16[256,128]{1,0:T(8,128)(2,1)S(1)}, bf16[256,128]{1,0:T(8,128)(2,1)S(1)}, u32[]{:S(2)}, u32[]{:S(2)}) collective-permute-start(bf16[256,128]{1,0:T(8,128)(2,1)S(1)} %shard_map.107.refs_0_), channel_id=1, source_target_pairs={{0,32},{16,48},{32,0},{48,16},{1,33},{17,49},{33,1},{49,17},{2,34}... | collective-permute-start | bytes 196616 | tf_op jit(solution)/shard_map/ppermute | solution.py:341
  39.9 6.5 %collective-permute-start.11 = (bf16[256,128]{1,0:T(8,128)(2,1)S(1)}, bf16[256,128]{1,0:T(8,128)(2,1)S(1)}, u32[]{:S(2)}, u32[]{:S(2)}) collective-permute-start(bf16[256,128]{1,0:T(8,128)(2,1)S(1)} %shard_map.107.refs_0_), channel_id=1, source_target_pairs={{0,48},{16,32},{32,16},{48,0},{1,49},{17,33},{33,17},{49,1},{2,50}... | collective-permute-start | bytes 196616 | tf_op jit(solution)/shard_map/ppermute | solution.py:341
  40.4 6.7 %collective-permute-start.3 = (bf16[4,128,128]{2,1,0:T(8,128)(2,1)S(1)}, bf16[4,128,128]{2,1,0:T(8,128)(2,1)S(1)}, u32[]{:S(2)}, u32[]{:S(2)}) collective-permute-start(bf16[4,128,128]{2,1,0:T(8,128)(2,1)S(1)} %get-tuple-element.42), channel_id=1, source_target_pairs={{0,16},{16,0},{32,48},{48,32},{1,17},{17,1},{33,49},{49,33},{2,18}... | collective-permute-start | bytes 393224 | tf_op jit(solution)/shard_map/ppermute | solution.py:341
  43.4 7.2 %collective-permute-start.4 = (bf16[4,128,128]{2,1,0:T(8,128)(2,1)S(1)}, bf16[4,128,128]{2,1,0:T(8,128)(2,1)S(1)}, u32[]{:S(2)}, u32[]{:S(2)}) collective-permute-start(bf16[4,128,128]{2,1,0:T(8,128)(2,1)S(1)} %get-tuple-element.43), channel_id=1, source_target_pairs={{0,32},{16,48},{32,0},{48,16},{1,33},{17,49},{33,1},{49,17},{2,34}... | collective-permute-start | bytes 393224 | tf_op jit(solution)/shard_map/ppermute | solution.py:341
  46.3 6.4 %collective-permute-start.5 = (bf16[4,128,128]{2,1,0:T(8,128)(2,1)S(1)}, bf16[4,128,128]{2,1,0:T(8,128)(2,1)S(1)}, u32[]{:S(2)}, u32[]{:S(2)}) collective-permute-start(bf16[4,128,128]{2,1,0:T(8,128)(2,1)S(1)} %get-tuple-element.44), channel_id=1, source_target_pairs={{0,48},{16,32},{32,16},{48,0},{1,49},{17,33},{33,17},{49,1},{2,50}... | collective-permute-start | bytes 393224 | tf_op jit(solution)/shard_map/ppermute | solution.py:341
  47.1 9.3 %collective-permute-start.12 = (bf16[1024,128]{1,0:T(8,128)(2,1)S(1)}, bf16[1024,128]{1,0:T(8,128)(2,1)S(1)}, u32[]{:S(2)}, u32[]{:S(2)}) collective-permute-start(bf16[1024,128]{1,0:T(8,128)(2,1)S(1)} %shard_map.108.refs_0_), channel_id=1, source_target_pairs={{0,64},{64,0},{128,192},{192,128},{1,65},{65,1},{129,193},{193,129... | collective-permute-start | bytes 786440 | tf_op jit(solution)/shard_map/ppermute | solution.py:341
  50.5 10.7 %collective-permute-start.13 = (bf16[1024,128]{1,0:T(8,128)(2,1)S(1)}, bf16[1024,128]{1,0:T(8,128)(2,1)S(1)}, u32[]{:S(2)}, u32[]{:S(2)}) collective-permute-start(bf16[1024,128]{1,0:T(8,128)(2,1)S(1)} %shard_map.108.refs_0_), channel_id=1, source_target_pairs={{0,128},{64,192},{128,0},{192,64},{1,129},{65,193},{129,1},{193,65... | collective-permute-start | bytes 786440 | tf_op jit(solution)/shard_map/ppermute | solution.py:341
  52.8 15.5 %collective-permute-start.14 = (bf16[1024,128]{1,0:T(8,128)(2,1)S(1)}, bf16[1024,128]{1,0:T(8,128)(2,1)S(1)}, u32[]{:S(2)}, u32[]{:S(2)}) collective-permute-start(bf16[1024,128]{1,0:T(8,128)(2,1)S(1)} %shard_map.108.refs_0_), channel_id=1, source_target_pairs={{0,192},{64,128},{128,64},{192,0},{1,193},{65,129},{129,65},{193,1... | collective-permute-start | bytes 786440 | tf_op jit(solution)/shard_map/ppermute | solution.py:341
  54.7 22.6 %collective-permute-start.6 = (bf16[4,128,128]{2,1,0:T(8,128)(2,1)S(1)}, bf16[4,128,128]{2,1,0:T(8,128)(2,1)S(1)}, u32[]{:S(2)}, u32[]{:S(2)}) collective-permute-start(bf16[4,128,128]{2,1,0:T(8,128)(2,1)S(1)} %get-tuple-element.46), channel_id=1, source_target_pairs={{0,64},{64,0},{128,192},{192,128},{1,65},{65,1},{129,193},{193,129... | collective-permute-start | bytes 393224 | tf_op jit(solution)/shard_map/ppermute | solution.py:341
  56.4 21.9 %collective-permute-start.7 = (bf16[4,128,128]{2,1,0:T(8,128)(2,1)S(1)}, bf16[4,128,128]{2,1,0:T(8,128)(2,1)S(1)}, u32[]{:S(2)}, u32[]{:S(2)}) collective-permute-start(bf16[4,128,128]{2,1,0:T(8,128)(2,1)S(1)} %get-tuple-element.47), channel_id=1, source_target_pairs={{0,128},{64,192},{128,0},{192,64},{1,129},{65,193},{129,1},{193,65... | collective-permute-start | bytes 393224 | tf_op jit(solution)/shard_map/ppermute | solution.py:341
  61.3 17.0 %collective-permute-start.8 = (bf16[4,128,128]{2,1,0:T(8,128)(2,1)S(1)}, bf16[4,128,128]{2,1,0:T(8,128)(2,1)S(1)}, u32[]{:S(2)}, u32[]{:S(2)}) collective-permute-start(bf16[4,128,128]{2,1,0:T(8,128)(2,1)S(1)} %get-tuple-element.48), channel_id=1, source_target_pairs={{0,192},{64,128},{128,64},{192,0},{1,193},{65,129},{129,65},{193,1... | collective-permute-start | bytes 393224 | tf_op jit(solution)/shard_map/ppermute | solution.py:341
  70.3 10.7 %collective-permute-start.20 = (bf16[64,512]{1,0:T(8,128)(2,1)S(1)}, bf16[64,512]{1,0:T(8,128)(2,1)S(1)}, u32[]{:S(2)}, u32[]{:S(2)}) collective-permute-start(bf16[64,512]{1,0:T(8,128)(2,1)S(1)} %get-tuple-element.57), channel_id=1, source_target_pairs={{0,12},{4,8},{8,4},{12,0},{1,13},{5,9},{9,5},{13,1},{2,14},{6,10},... | collective-permute-start | bytes 196616 | tf_op jit(solution)/shard_map/ppermute | solution.py:341
  75.8 10.1 %collective-permute-start.19 = (bf16[64,512]{1,0:T(8,128)(2,1)S(1)}, bf16[64,512]{1,0:T(8,128)(2,1)S(1)}, u32[]{:S(2)}, u32[]{:S(2)}) collective-permute-start(bf16[64,512]{1,0:T(8,128)(2,1)S(1)} %get-tuple-element.56), channel_id=1, source_target_pairs={{0,8},{4,12},{8,0},{12,4},{1,9},{5,13},{9,1},{13,5},{2,10},{6,14},... | collective-permute-start | bytes 196616 | tf_op jit(solution)/shard_map/ppermute | solution.py:341
  77.3 8.6 %collective-permute-start.18 = (bf16[64,512]{1,0:T(8,128)(2,1)S(1)}, bf16[64,512]{1,0:T(8,128)(2,1)S(1)}, u32[]{:S(2)}, u32[]{:S(2)}) collective-permute-start(bf16[64,512]{1,0:T(8,128)(2,1)S(1)} %get-tuple-element.55), channel_id=1, source_target_pairs={{0,4},{4,0},{8,12},{12,8},{1,5},{5,1},{9,13},{13,9},{2,6},{6,2},{1... | collective-permute-start | bytes 196616 | tf_op jit(solution)/shard_map/ppermute | solution.py:341

commit v6 on v5

--- a/solution.py
+++ b/solution.py
@@ -212,18 +212,6 @@
     return small(regroup_body, [like(got[0].shape)] * SIDE)(at, *got)
 
 
-def join_body(at_ref, *refs):
-    o_ref = refs[-1]
-    rows = refs[0].shape[0]
-    for j, ref in enumerate(refs[:-1]):
-        o_ref[j * rows : (j + 1) * rows, :] = ref[...]
-
-
-def joined(at, pieces):
-    rows = sum(p.shape[0] for p in pieces)
-    return small(join_body, [like((rows, DH))])(at, *pieces)[0]
-
-
 def inner_body(q_ref, k_ref, v_ref, o_ref):
     tokens, width = q_ref.shape[1:]
     half = tokens // 2
@@ -370,10 +358,10 @@
     from_c, from_z, from_zc, *before = lax.optimization_barrier(
         (from_c, from_z, from_zc, *before)
     )
-    mine = joined(at, (pieces[0], from_c, from_z, from_zc))
+    mine = jnp.concatenate((pieces[0], from_c, from_z, from_zc))
     heads = exchanged([mine] * SIDE, "x")
     beside = exchanged(before, "x")
-    row_of_heads = joined(at, heads)
+    row_of_heads = jnp.concatenate(heads)
     rows = exchanged([row_of_heads] * SIDE, "y")
     w_c = lax.ppermute(weight, "c", swap)
     w_zc = lax.ppermute(w_z, "c", swap)

time: 86.9 us -> 81.1 us (0.933)
  the two profiles are of different devices: /device:TPU:24 before, /device:TPU:1 now
where the time goes in v6:
time: 81.1 us; the launch traced here: 79.9 us
  starting transfers between devices  38 us (47%)
  Pallas kernels  20.3 us (25%)
  waiting for transfers between devices  19.2 us (24%)
  between operations  0.83 us (1%)
    ppermute x15, starting transfers between devices, exchanged(): got.append(lax.ppermute(arrays[s], axis, [(i, i ^ s) for i in range(SIDE)]))  24.1 us
    ppermute x15, waiting for transfers between devices, exchanged(): got.append(lax.ppermute(arrays[s], axis, [(i, i ^ s) for i in range(SIDE)]))  16.5 us
    pallas_call x1, Pallas kernels, inside(): pl.pallas_call(body, grid=(count,), in_specs=[big, big, big] + [pl.BlockS...  8.08 us
    all_to_all x1, starting transfers between devices, on_device(): got = lax.all_to_all(sent, SEQ, 0, 0, tiled=True)  7.58 us
    pallas_call x1, Pallas kernels, block_states(): pl.pallas_call(states_body, in_specs=[pl.BlockSpec(memory_space=pltpu.HBM...  3.9 us
    pallas_call x1, Pallas kernels, finish(): pl.pallas_call(finish_body, in_specs=[smem()] + vmem(2 + SIDE), out_specs...  2.87 us
    pallas_call x3, Pallas kernels, call(): pl.pallas_call(body, in_specs=[smem()] + vmem(len(arrays)), out_specs=vme...  2.24 us
    ppermute x1, starting transfers between devices, on_device(): from_c = lax.ppermute(pieces[1], 'c', swap)  2.23 us
  transfers between devices with their start and end apart: 22, of which 10 were waited for; matrix products, arithmetic and copies ran while one was open for 1% of the time, Pallas kernels for 21%

profile of v6, /device:TPU:1, one launch (start us, length us, event | category | flops | bytes accessed | tf_op | source)
XLA Modules:
  0.0 79.9 jit_solution(4906499406462245270)
XLA Ops:
  0.7 3.9 %block_states.1 = bf16[16,176,128]{2,1,0:T(8,128)(2,1)} custom-call(bf16[4,512,512]{2,1,0:T(8,128)(2,1)} %k_ref.3, bf16[4,512,512]{2,1,0:T(8,128)(2,1)} %v_ref.3, bf16[4,16,512]{2,1,0:T(8,128)(2,1)} %tq_ref.1, bf16[4,16,512]{2,1,0:T(8,128)(2,1)} %tk_ref.1, bf16[4,16,512]{2,1,0:T(8,128)(2,1)} %tv_ref.1), custom_call_target="tpu_custom_call" | custom-call | flops 268435456 | bytes 4194304 | tf_op jit(solution)/shard_map/block_states/pallas_call | solution.py:120
  4.6 7.6 %all-to-all-start = ((bf16[16,176,128]{2,1,0:T(8,128)(2,1)}), bf16[16,176,128]{2,1,0:T(8,128)(2,1)S(1)}, u32[]{:S(2)}, u32[]{:S(2)}) async-start(bf16[16,176,128]{2,1,0:T(8,128)(2,1)} %block_states.1), calls=%async_computation | async-start | bytes 1441792 | tf_op jit(solution)/shard_map/all_to_all | solution.py:344
  12.2 1.7 %collective-permute-start.16 = (bf16[512,512]{1,0:T(8,128)(2,1)S(1)}, bf16[512,512]{1,0:T(8,128)(2,1)S(1)}, u32[]{:S(2)}, u32[]{:S(2)}) collective-permute-start(bf16[512,512]{1,0:T(8,128)(2,1)S(1)} %copy-done.3), channel_id=1, source_target_pairs={{0,2},{2,0},{1,3},{3,1},{4,6},{6,4},{5,7},{7,5},{8,10},{10,8},{9,1... | collective-permute-start | bytes 1572872 | tf_op jit(solution)/shard_map/ppermute | solution.py:346
  14.0 0.7 constant_dynamic-slice_fusion.parents_ref
  14.7 8.1 %inside.1.inner_ref = bf16[4,512,512]{2,1,0:T(8,128)(2,1)} custom-call(bf16[4,512,512]{2,1,0:T(8,128)(2,1)} %q_ref.3, bf16[4,512,512]{2,1,0:T(8,128)(2,1)} %k_ref.3, bf16[4,512,512]{2,1,0:T(8,128)(2,1)} %v_ref.3), custom_call_target="tpu_custom_call" | custom-call | flops 1610612736 | bytes 8388608 | tf_op jit(solution)/shard_map/inside/pallas_call | solution.py:235
  22.7 1.6 %ancestors.1.reach_ref = f32[256,256]{1,0:T(8,128)S(1)} custom-call(s32[1,256]{1,0:T(1,128)S(1)} %constant_dynamic-slice_fusion.parents_ref), custom_call_target="tpu_custom_call" | custom-call | flops 268435456 | bytes 262144 | tf_op jit(solution)/shard_map/ancestors/pallas_call | solution.py:150
  24.7 1.0 %shard_map.104 = (bf16[64,128]{1,0:T(8,128)(2,1)S(1)}, bf16[64,128]{1,0:T(8,128)(2,1)S(1)}, bf16[64,128]{1,0:T(8,128)(2,1)S(1)}, bf16[64,128]{1,0:T(8,128)(2,1)S(1)}) custom-call(s32[4]{0:T(128)S(1)} %pad_add_fusion.at_ref, bf16[16,176,128]{2,1,0:T(8,128)(2,1)S(1)} %all-to-all-done.got_ref, f32[128,128]{1,0:T(8,128)S(1)} %dynamic-slice_bitcast_fusion.prior_ref, ...), custom_call_target="tpu_custom_call" | custom-call | flops 50331648 | bytes 2097152 | tf_op jit(solution)/shard_map/pallas_call | solution.py:54
  25.7 2.2 %collective-permute-start = (bf16[64,128]{1,0:T(8,128)(2,1)S(1)}, bf16[64,128]{1,0:T(8,128)(2,1)S(1)}, u32[]{:S(2)}, u32[]{:S(2)}) collective-permute-start(bf16[64,128]{1,0:T(8,128)(2,1)S(1)} %get-tuple-element.34), channel_id=1, source_target_pairs={{0,1},{1,0},{2,3},{3,2},{4,5},{5,4},{6,7},{7,6},{8,9},{9,8},{10,11... | collective-permute-start | bytes 49160 | tf_op jit(solution)/shard_map/ppermute | solution.py:354
  27.9 1.6 %collective-permute-start.1 = (bf16[64,128]{1,0:T(8,128)(2,1)S(1)}, bf16[64,128]{1,0:T(8,128)(2,1)S(1)}, u32[]{:S(2)}, u32[]{:S(2)}) collective-permute-start(bf16[64,128]{1,0:T(8,128)(2,1)S(1)} %get-tuple-element.35), channel_id=1, source_target_pairs={{0,2},{2,0},{1,3},{3,1},{4,6},{6,4},{5,7},{7,5},{8,10},{10,8},{9,1... | collective-permute-start | bytes 49160 | tf_op jit(solution)/shard_map/ppermute | solution.py:355
  30.7 2.0 %collective-permute-done.2 = bf16[64,128]{1,0:T(8,128)(2,1)S(1)} collective-permute-done((bf16[64,128]{1,0:T(8,128)(2,1)S(1)}, bf16[64,128]{1,0:T(8,128)(2,1)S(1)}, u32[]{:S(2)}, u32[]{:S(2)}) %collective-permute-start.2) | collective-permute-done | bytes 16416 | tf_op jit(solution)/shard_map/ppermute | solution.py:356
  33.1 0.7 collective-permute-start.15
  33.7 1.3 %collective-permute-start.10 = (bf16[256,128]{1,0:T(8,128)(2,1)S(1)}, bf16[256,128]{1,0:T(8,128)(2,1)S(1)}, u32[]{:S(2)}, u32[]{:S(2)}) collective-permute-start(bf16[256,128]{1,0:T(8,128)(2,1)S(1)} %get-tuple-element.58), channel_id=1, source_target_pairs={{0,32},{16,48},{32,0},{48,16},{1,33},{17,49},{33,1},{49,17},{2,34}... | collective-permute-start | bytes 196616 | tf_op jit(solution)/shard_map/ppermute | solution.py:329
  35.1 2.3 %collective-permute-start.11 = (bf16[256,128]{1,0:T(8,128)(2,1)S(1)}, bf16[256,128]{1,0:T(8,128)(2,1)S(1)}, u32[]{:S(2)}, u32[]{:S(2)}) collective-permute-start(bf16[256,128]{1,0:T(8,128)(2,1)S(1)} %get-tuple-element.58), channel_id=1, source_target_pairs={{0,48},{16,32},{32,16},{48,0},{1,49},{17,33},{33,17},{49,1},{2,50}... | collective-permute-start | bytes 196616 | tf_op jit(solution)/shard_map/ppermute | solution.py:329
  37.4 0.9 %collective-permute-done.10 = bf16[256,128]{1,0:T(8,128)(2,1)S(1)} collective-permute-done((bf16[256,128]{1,0:T(8,128)(2,1)S(1)}, bf16[256,128]{1,0:T(8,128)(2,1)S(1)}, u32[]{:S(2)}, u32[]{:S(2)}) %collective-permute-start.10) | collective-permute-done | bytes 65568 | tf_op jit(solution)/shard_map/ppermute | solution.py:329
  38.4 1.4 %collective-permute-start.4 = (bf16[4,128,128]{2,1,0:T(8,128)(2,1)S(1)}, bf16[4,128,128]{2,1,0:T(8,128)(2,1)S(1)}, u32[]{:S(2)}, u32[]{:S(2)}) collective-permute-start(bf16[4,128,128]{2,1,0:T(8,128)(2,1)S(1)} %get-tuple-element.43), channel_id=1, source_target_pairs={{0,32},{16,48},{32,0},{48,16},{1,33},{17,49},{33,1},{49,17},{2,34}... | collective-permute-start | bytes 393224 | tf_op jit(solution)/shard_map/ppermute | solution.py:329
  39.7 0.7 collective-permute-done.11
  40.4 1.8 %collective-permute-start.5 = (bf16[4,128,128]{2,1,0:T(8,128)(2,1)S(1)}, bf16[4,128,128]{2,1,0:T(8,128)(2,1)S(1)}, u32[]{:S(2)}, u32[]{:S(2)}) collective-permute-start(bf16[4,128,128]{2,1,0:T(8,128)(2,1)S(1)} %get-tuple-element.44), channel_id=1, source_target_pairs={{0,48},{16,32},{32,16},{48,0},{1,49},{17,33},{33,17},{49,1},{2,50}... | collective-permute-start | bytes 393224 | tf_op jit(solution)/shard_map/ppermute | solution.py:329
  42.4 1.9 %collective-permute-done.4.refs_2_ = bf16[4,128,128]{2,1,0:T(8,128)(2,1)S(1)} collective-permute-done((bf16[4,128,128]{2,1,0:T(8,128)(2,1)S(1)}, bf16[4,128,128]{2,1,0:T(8,128)(2,1)S(1)}, u32[]{:S(2)}, u32[]{:S(2)}) %collective-permute-start.4) | collective-permute-done | bytes 131104 | tf_op jit(solution)/shard_map/ppermute | solution.py:329
  44.2 3.3 %collective-permute-start.13 = (bf16[1024,128]{1,0:T(8,128)(2,1)S(1)}, bf16[1024,128]{1,0:T(8,128)(2,1)S(1)}, u32[]{:S(2)}, u32[]{:S(2)}) collective-permute-start(bf16[1024,128]{1,0:T(8,128)(2,1)S(1)} %constant_dynamic-update-slice_fusion.4.refs_0_), channel_id=1, source_target_pairs={{0,128},{64,192},{128,0},{192,64},{1,129},{65,193},{129,1},{193,65... | collective-permute-start | bytes 786440 | tf_op jit(solution)/shard_map/ppermute | solution.py:329
  47.6 0.9 %collective-permute-done.5.refs_3_ = bf16[4,128,128]{2,1,0:T(8,128)(2,1)S(1)} collective-permute-done((bf16[4,128,128]{2,1,0:T(8,128)(2,1)S(1)}, bf16[4,128,128]{2,1,0:T(8,128)(2,1)S(1)}, u32[]{:S(2)}, u32[]{:S(2)}) %collective-permute-start.5) | collective-permute-done | bytes 131104 | tf_op jit(solution)/shard_map/ppermute | solution.py:329
  48.4 1.4 %collective-permute-start.14 = (bf16[1024,128]{1,0:T(8,128)(2,1)S(1)}, bf16[1024,128]{1,0:T(8,128)(2,1)S(1)}, u32[]{:S(2)}, u32[]{:S(2)}) collective-permute-start(bf16[1024,128]{1,0:T(8,128)(2,1)S(1)} %constant_dynamic-update-slice_fusion.4.refs_0_), channel_id=1, source_target_pairs={{0,192},{64,128},{128,64},{192,0},{1,193},{65,129},{129,65},{193,1... | collective-permute-start | bytes 786440 | tf_op jit(solution)/shard_map/ppermute | solution.py:329
  50.5 2.4 %collective-permute-start.7 = (bf16[4,128,128]{2,1,0:T(8,128)(2,1)S(1)}, bf16[4,128,128]{2,1,0:T(8,128)(2,1)S(1)}, u32[]{:S(2)}, u32[]{:S(2)}) collective-permute-start(bf16[4,128,128]{2,1,0:T(8,128)(2,1)S(1)} %get-tuple-element.47), channel_id=1, source_target_pairs={{0,128},{64,192},{128,0},{192,64},{1,129},{65,193},{129,1},{193,65... | collective-permute-start | bytes 393224 | tf_op jit(solution)/shard_map/ppermute | solution.py:329
  53.0 2.3 %collective-permute-done.13.refs_2_ = bf16[1024,128]{1,0:T(8,128)(2,1)S(1)} collective-permute-done((bf16[1024,128]{1,0:T(8,128)(2,1)S(1)}, bf16[1024,128]{1,0:T(8,128)(2,1)S(1)}, u32[]{:S(2)}, u32[]{:S(2)}) %collective-permute-start.13) | collective-permute-done | bytes 262176 | tf_op jit(solution)/shard_map/ppermute | solution.py:329
  55.2 1.9 %collective-permute-start.8 = (bf16[4,128,128]{2,1,0:T(8,128)(2,1)S(1)}, bf16[4,128,128]{2,1,0:T(8,128)(2,1)S(1)}, u32[]{:S(2)}, u32[]{:S(2)}) collective-permute-start(bf16[4,128,128]{2,1,0:T(8,128)(2,1)S(1)} %get-tuple-element.48), channel_id=1, source_target_pairs={{0,192},{64,128},{128,64},{192,0},{1,193},{65,129},{129,65},{193,1... | collective-permute-start | bytes 393224 | tf_op jit(solution)/shard_map/ppermute | solution.py:329
  57.1 7.2 %collective-permute-done.14.refs_3_ = bf16[1024,128]{1,0:T(8,128)(2,1)S(1)} collective-permute-done((bf16[1024,128]{1,0:T(8,128)(2,1)S(1)}, bf16[1024,128]{1,0:T(8,128)(2,1)S(1)}, u32[]{:S(2)}, u32[]{:S(2)}) %collective-permute-start.14) | collective-permute-done | bytes 262176 | tf_op jit(solution)/shard_map/ppermute | solution.py:329
  64.4 1.7 %project.1 = (bf16[64,512]{1,0:T(8,128)(2,1)S(1)}, bf16[64,512]{1,0:T(8,128)(2,1)S(1)}, bf16[64,512]{1,0:T(8,128)(2,1)S(1)}, bf16[64,512]{1,0:T(8,128)(2,1)S(1)}) custom-call(s32[4]{0:T(128)S(1)} %pad_add_fusion.at_ref, bf16[1024,128]{1,0:T(8,128)(2,1)S(1)} %constant_dynamic-update-slice_fusion.4.refs_0_, ...), custom_call_target="tpu_custom_call" | custom-call | flops 536870912 | bytes 2097152 | tf_op jit(solution)/shard_map/project/pallas_call | solution.py:310
  66.0 5.6 %collective-permute-start.20 = (bf16[64,512]{1,0:T(8,128)(2,1)S(1)}, bf16[64,512]{1,0:T(8,128)(2,1)S(1)}, u32[]{:S(2)}, u32[]{:S(2)}) collective-permute-start(bf16[64,512]{1,0:T(8,128)(2,1)S(1)} %get-tuple-element.57), channel_id=1, source_target_pairs={{0,12},{4,8},{8,4},{12,0},{1,13},{5,9},{9,5},{13,1},{2,14},{6,10},... | collective-permute-start | bytes 196616 | tf_op jit(solution)/shard_map/ppermute | solution.py:329
  71.6 1.0 %collective-permute-start.19 = (bf16[64,512]{1,0:T(8,128)(2,1)S(1)}, bf16[64,512]{1,0:T(8,128)(2,1)S(1)}, u32[]{:S(2)}, u32[]{:S(2)}) collective-permute-start(bf16[64,512]{1,0:T(8,128)(2,1)S(1)} %get-tuple-element.56), channel_id=1, source_target_pairs={{0,8},{4,12},{8,0},{12,4},{1,9},{5,13},{9,1},{13,5},{2,10},{6,14},... | collective-permute-start | bytes 196616 | tf_op jit(solution)/shard_map/ppermute | solution.py:329
  72.6 1.2 %collective-permute-start.18 = (bf16[64,512]{1,0:T(8,128)(2,1)S(1)}, bf16[64,512]{1,0:T(8,128)(2,1)S(1)}, u32[]{:S(2)}, u32[]{:S(2)}) collective-permute-start(bf16[64,512]{1,0:T(8,128)(2,1)S(1)} %get-tuple-element.55), channel_id=1, source_target_pairs={{0,4},{4,0},{8,12},{12,8},{1,5},{5,1},{9,13},{13,9},{2,6},{6,2},{1... | collective-permute-start | bytes 196616 | tf_op jit(solution)/shard_map/ppermute | solution.py:329
  73.8 2.9 %finish.1 = bf16[4,512,512]{2,1,0:T(8,128)(2,1)} custom-call(s32[4]{0:T(128)S(1)} %pad_add_fusion.at_ref, bf16[4,512,512]{2,1,0:T(8,128)(2,1)S(1)} %copy-done.1, bf16[4,512,512]{2,1,0:T(8,128)(2,1)S(1)} %copy-done.2, bf16[4,128,128]{2,1,0:T(8,128)(2,1)S(1)} %get-tuple-element.45.refs_0_, bf16[4,128,128]{2,1,0:T(8,128)(2,1)S(1)} %collective-permute-done.6.refs_1_, ...), custom_call_target="tpu_custom_call" | custom-call | flops 268435456 | bytes 6291456 | tf_op jit(solution)/shard_map/finish/pallas_call | solution.py:266
  76.7 2.6 %collective-permute-done.19 = bf16[64,512]{1,0:T(8,128)(2,1)S(1)} collective-permute-done((bf16[64,512]{1,0:T(8,128)(2,1)S(1)}, bf16[64,512]{1,0:T(8,128)(2,1)S(1)}, u32[]{:S(2)}, u32[]{:S(2)}) %collective-permute-start.19) | collective-permute-done | bytes 65568 | tf_op jit(solution)/shard_map/ppermute | solution.py:329
  79.3 0.7 add_convert_fusion
  (39 shorter events, 2.7 us)
Async XLA Ops:
  0.6 14.0 %copy-start = (f32[4,4,128,128]{3,2,1,0:T(8,128)S(1)}, f32[4,4,128,128]{3,2,1,0:T(8,128)}, u32[]{:S(2)}) copy-start(f32[4,4,128,128]{3,2,1,0:T(8,128)} %param.12) | copy-start | bytes 3145732
  0.6 11.5 %copy-start.3 = (bf16[512,512]{1,0:T(8,128)(2,1)S(1)}, bf16[512,512]{1,0:T(8,128)(2,1)}, u32[]{:S(2)}) copy-start(bf16[512,512]{1,0:T(8,128)(2,1)} %refs_4_) | copy-start | bytes 1572868
  4.6 20.1 %all-to-all-start = ((bf16[16,176,128]{2,1,0:T(8,128)(2,1)}), bf16[16,176,128]{2,1,0:T(8,128)(2,1)S(1)}, u32[]{:S(2)}, u32[]{:S(2)}) async-start(bf16[16,176,128]{2,1,0:T(8,128)(2,1)} %block_states.1), calls=%async_computation | async-start | bytes 1441792 | tf_op jit(solution)/shard_map/all_to_all | solution.py:344
  12.2 21.6 %collective-permute-start.16 = (bf16[512,512]{1,0:T(8,128)(2,1)S(1)}, bf16[512,512]{1,0:T(8,128)(2,1)S(1)}, u32[]{:S(2)}, u32[]{:S(2)}) collective-permute-start(bf16[512,512]{1,0:T(8,128)(2,1)S(1)} %copy-done.3), channel_id=1, source_target_pairs={{0,2},{2,0},{1,3},{3,1},{4,6},{6,4},{5,7},{7,5},{8,10},{10,8},{9,1... | collective-permute-start | bytes 1572872 | tf_op jit(solution)/shard_map/ppermute | solution.py:346
  25.7 4.6 %collective-permute-start = (bf16[64,128]{1,0:T(8,128)(2,1)S(1)}, bf16[64,128]{1,0:T(8,128)(2,1)S(1)}, u32[]{:S(2)}, u32[]{:S(2)}) collective-permute-start(bf16[64,128]{1,0:T(8,128)(2,1)S(1)} %get-tuple-element.34), channel_id=1, source_target_pairs={{0,1},{1,0},{2,3},{3,2},{4,5},{5,4},{6,7},{7,6},{8,9},{9,8},{10,11... | collective-permute-start | bytes 49160 | tf_op jit(solution)/shard_map/ppermute | solution.py:354
  27.9 2.8 %collective-permute-start.1 = (bf16[64,128]{1,0:T(8,128)(2,1)S(1)}, bf16[64,128]{1,0:T(8,128)(2,1)S(1)}, u32[]{:S(2)}, u32[]{:S(2)}) collective-permute-start(bf16[64,128]{1,0:T(8,128)(2,1)S(1)} %get-tuple-element.35), channel_id=1, source_target_pairs={{0,2},{2,0},{1,3},{3,1},{4,6},{6,4},{5,7},{7,5},{8,10},{10,8},{9,1... | collective-permute-start | bytes 49160 | tf_op jit(solution)/shard_map/ppermute | solution.py:355
  29.6 3.2 %collective-permute-start.2 = (bf16[64,128]{1,0:T(8,128)(2,1)S(1)}, bf16[64,128]{1,0:T(8,128)(2,1)S(1)}, u32[]{:S(2)}, u32[]{:S(2)}) collective-permute-start(bf16[64,128]{1,0:T(8,128)(2,1)S(1)} %get-tuple-element.36), channel_id=1, source_target_pairs={{0,3},{1,2},{2,1},{3,0},{4,7},{5,6},{6,5},{7,4},{8,11},{9,10},{10,... | collective-permute-start | bytes 49160 | tf_op jit(solution)/shard_map/ppermute | solution.py:356
  32.7 41.0 %copy-start.2 = (bf16[4,512,512]{2,1,0:T(8,128)(2,1)S(1)}, bf16[4,512,512]{2,1,0:T(8,128)(2,1)}, u32[]{:S(2)}) copy-start(bf16[4,512,512]{2,1,0:T(8,128)(2,1)} %inside.1.inner_ref) | copy-start | bytes 6291460
  32.7 41.0 %copy-start.1 = (bf16[4,512,512]{2,1,0:T(8,128)(2,1)S(1)}, bf16[4,512,512]{2,1,0:T(8,128)(2,1)}, u32[]{:S(2)}) copy-start(bf16[4,512,512]{2,1,0:T(8,128)(2,1)} %q_ref.3) | copy-start | bytes 6291460
  32.8 4.6 %collective-permute-start.9 = (bf16[256,128]{1,0:T(8,128)(2,1)S(1)}, bf16[256,128]{1,0:T(8,128)(2,1)S(1)}, u32[]{:S(2)}, u32[]{:S(2)}) collective-permute-start(bf16[256,128]{1,0:T(8,128)(2,1)S(1)} %get-tuple-element.58), channel_id=1, source_target_pairs={{0,16},{16,0},{32,48},{48,32},{1,17},{17,1},{33,49},{49,33},{2,18}... | collective-permute-start | bytes 196616 | tf_op jit(solution)/shard_map/ppermute | solution.py:329
  33.1 17.3 %collective-permute-start.15 = (bf16[512,512]{1,0:T(8,128)(2,1)S(1)}, bf16[512,512]{1,0:T(8,128)(2,1)S(1)}, u32[]{:S(2)}, u32[]{:S(2)}) collective-permute-start(bf16[512,512]{1,0:T(8,128)(2,1)S(1)} %copy-done.3), channel_id=1, source_target_pairs={{0,1},{1,0},{2,3},{3,2},{4,5},{5,4},{6,7},{7,6},{8,9},{9,8},{10,11... | collective-permute-start | bytes 1572872 | tf_op jit(solution)/shard_map/ppermute | solution.py:366
  33.7 30.6 %collective-permute-start.17 = (bf16[512,512]{1,0:T(8,128)(2,1)S(1)}, bf16[512,512]{1,0:T(8,128)(2,1)S(1)}, u32[]{:S(2)}, u32[]{:S(2)}) collective-permute-start(bf16[512,512]{1,0:T(8,128)(2,1)S(1)} %collective-permute-done.16.refs_6_), channel_id=1, source_target_pairs={{0,1},{1,0},{2,3},{3,2},{4,5},{5,4},{6,7},{7,6},{8,9},{9,8},{10,11... | collective-permute-start | bytes 1572872 | tf_op jit(solution)/shard_map/ppermute | solution.py:367
  33.7 4.6 %collective-permute-start.10 = (bf16[256,128]{1,0:T(8,128)(2,1)S(1)}, bf16[256,128]{1,0:T(8,128)(2,1)S(1)}, u32[]{:S(2)}, u32[]{:S(2)}) collective-permute-start(bf16[256,128]{1,0:T(8,128)(2,1)S(1)} %get-tuple-element.58), channel_id=1, source_target_pairs={{0,32},{16,48},{32,0},{48,16},{1,33},{17,49},{33,1},{49,17},{2,34}... | collective-permute-start | bytes 196616 | tf_op jit(solution)/shard_map/ppermute | solution.py:329
  35.1 5.4 %collective-permute-start.11 = (bf16[256,128]{1,0:T(8,128)(2,1)S(1)}, bf16[256,128]{1,0:T(8,128)(2,1)S(1)}, u32[]{:S(2)}, u32[]{:S(2)}) collective-permute-start(bf16[256,128]{1,0:T(8,128)(2,1)S(1)} %get-tuple-element.58), channel_id=1, source_target_pairs={{0,48},{16,32},{32,16},{48,0},{1,49},{17,33},{33,17},{49,1},{2,50}... | collective-permute-start | bytes 196616 | tf_op jit(solution)/shard_map/ppermute | solution.py:329
  37.4 4.8 %collective-permute-start.3 = (bf16[4,128,128]{2,1,0:T(8,128)(2,1)S(1)}, bf16[4,128,128]{2,1,0:T(8,128)(2,1)S(1)}, u32[]{:S(2)}, u32[]{:S(2)}) collective-permute-start(bf16[4,128,128]{2,1,0:T(8,128)(2,1)S(1)} %get-tuple-element.42), channel_id=1, source_target_pairs={{0,16},{16,0},{32,48},{48,32},{1,17},{17,1},{33,49},{49,33},{2,18}... | collective-permute-start | bytes 393224 | tf_op jit(solution)/shard_map/ppermute | solution.py:329
  38.4 5.9 %collective-permute-start.4 = (bf16[4,128,128]{2,1,0:T(8,128)(2,1)S(1)}, bf16[4,128,128]{2,1,0:T(8,128)(2,1)S(1)}, u32[]{:S(2)}, u32[]{:S(2)}) collective-permute-start(bf16[4,128,128]{2,1,0:T(8,128)(2,1)S(1)} %get-tuple-element.43), channel_id=1, source_target_pairs={{0,32},{16,48},{32,0},{48,16},{1,33},{17,49},{33,1},{49,17},{2,34}... | collective-permute-start | bytes 393224 | tf_op jit(solution)/shard_map/ppermute | solution.py:329
  40.4 8.0 %collective-permute-start.5 = (bf16[4,128,128]{2,1,0:T(8,128)(2,1)S(1)}, bf16[4,128,128]{2,1,0:T(8,128)(2,1)S(1)}, u32[]{:S(2)}, u32[]{:S(2)}) collective-permute-start(bf16[4,128,128]{2,1,0:T(8,128)(2,1)S(1)} %get-tuple-element.44), channel_id=1, source_target_pairs={{0,48},{16,32},{32,16},{48,0},{1,49},{17,33},{33,17},{49,1},{2,50}... | collective-permute-start | bytes 393224 | tf_op jit(solution)/shard_map/ppermute | solution.py:329
  42.3 8.3 %collective-permute-start.12 = (bf16[1024,128]{1,0:T(8,128)(2,1)S(1)}, bf16[1024,128]{1,0:T(8,128)(2,1)S(1)}, u32[]{:S(2)}, u32[]{:S(2)}) collective-permute-start(bf16[1024,128]{1,0:T(8,128)(2,1)S(1)} %constant_dynamic-update-slice_fusion.4.refs_0_), channel_id=1, source_target_pairs={{0,64},{64,0},{128,192},{192,128},{1,65},{65,1},{129,193},{193,129... | collective-permute-start | bytes 786440 | tf_op jit(solution)/shard_map/ppermute | solution.py:329
  44.2 11.0 %collective-permute-start.13 = (bf16[1024,128]{1,0:T(8,128)(2,1)S(1)}, bf16[1024,128]{1,0:T(8,128)(2,1)S(1)}, u32[]{:S(2)}, u32[]{:S(2)}) collective-permute-start(bf16[1024,128]{1,0:T(8,128)(2,1)S(1)} %constant_dynamic-update-slice_fusion.4.refs_0_), channel_id=1, source_target_pairs={{0,128},{64,192},{128,0},{192,64},{1,129},{65,193},{129,1},{193,65... | collective-permute-start | bytes 786440 | tf_op jit(solution)/shard_map/ppermute | solution.py:329
  48.4 15.9 %collective-permute-start.14 = (bf16[1024,128]{1,0:T(8,128)(2,1)S(1)}, bf16[1024,128]{1,0:T(8,128)(2,1)S(1)}, u32[]{:S(2)}, u32[]{:S(2)}) collective-permute-start(bf16[1024,128]{1,0:T(8,128)(2,1)S(1)} %constant_dynamic-update-slice_fusion.4.refs_0_), channel_id=1, source_target_pairs={{0,192},{64,128},{128,64},{192,0},{1,193},{65,129},{129,65},{193,1... | collective-permute-start | bytes 786440 | tf_op jit(solution)/shard_map/ppermute | solution.py:329
  50.4 22.1 %collective-permute-start.6 = (bf16[4,128,128]{2,1,0:T(8,128)(2,1)S(1)}, bf16[4,128,128]{2,1,0:T(8,128)(2,1)S(1)}, u32[]{:S(2)}, u32[]{:S(2)}) collective-permute-start(bf16[4,128,128]{2,1,0:T(8,128)(2,1)S(1)} %get-tuple-element.46), channel_id=1, source_target_pairs={{0,64},{64,0},{128,192},{192,128},{1,65},{65,1},{129,193},{193,129... | collective-permute-start | bytes 393224 | tf_op jit(solution)/shard_map/ppermute | solution.py:329
  50.5 23.2 %collective-permute-start.7 = (bf16[4,128,128]{2,1,0:T(8,128)(2,1)S(1)}, bf16[4,128,128]{2,1,0:T(8,128)(2,1)S(1)}, u32[]{:S(2)}, u32[]{:S(2)}) collective-permute-start(bf16[4,128,128]{2,1,0:T(8,128)(2,1)S(1)} %get-tuple-element.47), channel_id=1, source_target_pairs={{0,128},{64,192},{128,0},{192,64},{1,129},{65,193},{129,1},{193,65... | collective-permute-start | bytes 393224 | tf_op jit(solution)/shard_map/ppermute | solution.py:329
  55.2 18.5 %collective-permute-start.8 = (bf16[4,128,128]{2,1,0:T(8,128)(2,1)S(1)}, bf16[4,128,128]{2,1,0:T(8,128)(2,1)S(1)}, u32[]{:S(2)}, u32[]{:S(2)}) collective-permute-start(bf16[4,128,128]{2,1,0:T(8,128)(2,1)S(1)} %get-tuple-element.48), channel_id=1, source_target_pairs={{0,192},{64,128},{128,64},{192,0},{1,193},{65,129},{129,65},{193,1... | collective-permute-start | bytes 393224 | tf_op jit(solution)/shard_map/ppermute | solution.py:329
  66.0 10.6 %collective-permute-start.20 = (bf16[64,512]{1,0:T(8,128)(2,1)S(1)}, bf16[64,512]{1,0:T(8,128)(2,1)S(1)}, u32[]{:S(2)}, u32[]{:S(2)}) collective-permute-start(bf16[64,512]{1,0:T(8,128)(2,1)S(1)} %get-tuple-element.57), channel_id=1, source_target_pairs={{0,12},{4,8},{8,4},{12,0},{1,13},{5,9},{9,5},{13,1},{2,14},{6,10},... | collective-permute-start | bytes 196616 | tf_op jit(solution)/shard_map/ppermute | solution.py:329
  71.6 7.7 %collective-permute-start.19 = (bf16[64,512]{1,0:T(8,128)(2,1)S(1)}, bf16[64,512]{1,0:T(8,128)(2,1)S(1)}, u32[]{:S(2)}, u32[]{:S(2)}) collective-permute-start(bf16[64,512]{1,0:T(8,128)(2,1)S(1)} %get-tuple-element.56), channel_id=1, source_target_pairs={{0,8},{4,12},{8,0},{12,4},{1,9},{5,13},{9,1},{13,5},{2,10},{6,14},... | collective-permute-start | bytes 196616 | tf_op jit(solution)/shard_map/ppermute | solution.py:329
  72.6 6.7 %collective-permute-start.18 = (bf16[64,512]{1,0:T(8,128)(2,1)S(1)}, bf16[64,512]{1,0:T(8,128)(2,1)S(1)}, u32[]{:S(2)}, u32[]{:S(2)}) collective-permute-start(bf16[64,512]{1,0:T(8,128)(2,1)S(1)} %get-tuple-element.55), channel_id=1, source_target_pairs={{0,4},{4,0},{8,12},{12,8},{1,5},{5,1},{9,13},{13,9},{2,6},{6,2},{1... | collective-permute-start | bytes 196616 | tf_op jit(solution)/shard_map/ppermute | solution.py:329

commit v7 on v6

--- a/solution.py
+++ b/solution.py
@@ -281,11 +281,8 @@
 
 def project_body(at_ref, *refs):
     rows, weights, outs = refs[:SIDE], refs[SIDE : 2 * SIDE], refs[2 * SIDE : 3 * SIDE]
-    hold, slab, sems = refs[-3:]
+    hold = refs[-1]
     nodes = outs[0].shape[0]
-    copies = [pltpu.make_async_copy(weights[j], slab.at[j], sems.at[j]) for j in range(SIDE)]
-    for copy in copies:
-        copy.start()
     total = None
     for j in range(SIDE):
         parts = []
@@ -296,8 +293,7 @@
             ]
             parts.append(jnp.concatenate(heads, axis=1))
         lhs = jnp.concatenate(parts, axis=0)
-        copies[j].wait()
-        part = mm(lhs, slab[j], 1, 0)
+        part = mm(lhs, weights[j][...], 1, 0)
         total = part if total is None else total + part
     hold[...] = total.astype(BF).reshape(hold.shape)
     for s, out in enumerate(outs):
@@ -309,12 +305,10 @@
     deep, wide = weights[0].shape
     return pl.pallas_call(
         project_body,
-        in_specs=[smem()] + vmem(SIDE) + [pl.BlockSpec(memory_space=pl.ANY)] * SIDE,
+        in_specs=[smem()] + vmem(2 * SIDE),
         out_specs=vmem(SIDE),
         scratch_shapes=[
             pltpu.VMEM((SIDE, nodes, wide), BF),
-            pltpu.VMEM((SIDE, deep, wide), BF),
-            pltpu.SemaphoreType.DMA((SIDE,)),
         ],
         out_shape=[like((nodes, wide))] * SIDE,
         cost_estimate=cost(2 * SIDE * SIDE * NODES * DH * wide, 8 * deep * wide),

time: 81.1 us -> 80.7 us (level)
  transfers between devices with their start and end apart: 22 -> 22, of which waited for: 10 -> 10; matrix products, arithmetic and copies ran while one was open for 1% -> 1% of each run, Pallas kernels for 21% -> 20%
where the time goes in v7:
time: 80.7 us; the launch traced here: 79.5 us
  starting transfers between devices  38 us (47%)
  Pallas kernels  19.9 us (25%)
  waiting for transfers between devices  19.2 us (24%)
  between operations  0.83 us (1%)
    ppermute x15, starting transfers between devices, exchanged(): got.append(lax.ppermute(arrays[s], axis, [(i, i ^ s) for i in range(SIDE)]))  24.1 us
    ppermute x15, waiting for transfers between devices, exchanged(): got.append(lax.ppermute(arrays[s], axis, [(i, i ^ s) for i in range(SIDE)]))  16.5 us
    pallas_call x1, Pallas kernels, inside(): pl.pallas_call(body, grid=(count,), in_specs=[big, big, big] + [pl.BlockS...  8.08 us
    all_to_all x1, starting transfers between devices, on_device(): got = lax.all_to_all(sent, SEQ, 0, 0, tiled=True)  7.58 us
    pallas_call x1, Pallas kernels, block_states(): pl.pallas_call(states_body, in_specs=[pl.BlockSpec(memory_space=pltpu.HBM...  3.9 us
    pallas_call x1, Pallas kernels, finish(): pl.pallas_call(finish_body, in_specs=[smem()] + vmem(2 + SIDE), out_specs...  2.87 us
    pallas_call x3, Pallas kernels, call(): pl.pallas_call(body, in_specs=[smem()] + vmem(len(arrays)), out_specs=vme...  2.24 us
    ppermute x1, starting transfers between devices, on_device(): from_c = lax.ppermute(pieces[1], 'c', swap)  2.23 us
  transfers between devices with their start and end apart: 22, of which 10 were waited for; matrix products, arithmetic and copies ran while one was open for 1% of the time, Pallas kernels for 20%

profile of v7, /device:TPU:1, one launch (start us, length us, event | category | flops | bytes accessed | tf_op | source)
XLA Modules:
  0.0 79.5 jit_solution(3083929527463729806)
XLA Ops:
  0.7 3.9 %block_states.1 = bf16[16,176,128]{2,1,0:T(8,128)(2,1)} custom-call(bf16[4,512,512]{2,1,0:T(8,128)(2,1)} %k_ref.3, bf16[4,512,512]{2,1,0:T(8,128)(2,1)} %v_ref.3, bf16[4,16,512]{2,1,0:T(8,128)(2,1)} %tq_ref.1, bf16[4,16,512]{2,1,0:T(8,128)(2,1)} %tk_ref.1, bf16[4,16,512]{2,1,0:T(8,128)(2,1)} %tv_ref.1), custom_call_target="tpu_custom_call" | custom-call | flops 268435456 | bytes 4194304 | tf_op jit(solution)/shard_map/block_states/pallas_call | solution.py:120
  4.6 7.6 %all-to-all-start = ((bf16[16,176,128]{2,1,0:T(8,128)(2,1)}), bf16[16,176,128]{2,1,0:T(8,128)(2,1)S(1)}, u32[]{:S(2)}, u32[]{:S(2)}) async-start(bf16[16,176,128]{2,1,0:T(8,128)(2,1)} %block_states.1), calls=%async_computation | async-start | bytes 1441792 | tf_op jit(solution)/shard_map/all_to_all | solution.py:338
  12.2 1.7 %collective-permute-start.16 = (bf16[512,512]{1,0:T(8,128)(2,1)S(1)}, bf16[512,512]{1,0:T(8,128)(2,1)S(1)}, u32[]{:S(2)}, u32[]{:S(2)}) collective-permute-start(bf16[512,512]{1,0:T(8,128)(2,1)S(1)} %copy-done.3), channel_id=1, source_target_pairs={{0,2},{2,0},{1,3},{3,1},{4,6},{6,4},{5,7},{7,5},{8,10},{10,8},{9,1... | collective-permute-start | bytes 1572872 | tf_op jit(solution)/shard_map/ppermute | solution.py:340
  14.0 0.7 constant_dynamic-slice_fusion.parents_ref
  14.7 8.1 %inside.1.inner_ref = bf16[4,512,512]{2,1,0:T(8,128)(2,1)} custom-call(bf16[4,512,512]{2,1,0:T(8,128)(2,1)} %q_ref.3, bf16[4,512,512]{2,1,0:T(8,128)(2,1)} %k_ref.3, bf16[4,512,512]{2,1,0:T(8,128)(2,1)} %v_ref.3), custom_call_target="tpu_custom_call" | custom-call | flops 1610612736 | bytes 8388608 | tf_op jit(solution)/shard_map/inside/pallas_call | solution.py:235
  22.7 1.6 %ancestors.1.reach_ref = f32[256,256]{1,0:T(8,128)S(1)} custom-call(s32[1,256]{1,0:T(1,128)S(1)} %constant_dynamic-slice_fusion.parents_ref), custom_call_target="tpu_custom_call" | custom-call | flops 268435456 | bytes 262144 | tf_op jit(solution)/shard_map/ancestors/pallas_call | solution.py:150
  24.7 1.0 %shard_map.104 = (bf16[64,128]{1,0:T(8,128)(2,1)S(1)}, bf16[64,128]{1,0:T(8,128)(2,1)S(1)}, bf16[64,128]{1,0:T(8,128)(2,1)S(1)}, bf16[64,128]{1,0:T(8,128)(2,1)S(1)}) custom-call(s32[4]{0:T(128)S(1)} %pad_add_fusion.at_ref, bf16[16,176,128]{2,1,0:T(8,128)(2,1)S(1)} %all-to-all-done.got_ref, f32[128,128]{1,0:T(8,128)S(1)} %dynamic-slice_bitcast_fusion.prior_ref, ...), custom_call_target="tpu_custom_call" | custom-call | flops 50331648 | bytes 2097152 | tf_op jit(solution)/shard_map/pallas_call | solution.py:54
  25.7 2.2 %collective-permute-start = (bf16[64,128]{1,0:T(8,128)(2,1)S(1)}, bf16[64,128]{1,0:T(8,128)(2,1)S(1)}, u32[]{:S(2)}, u32[]{:S(2)}) collective-permute-start(bf16[64,128]{1,0:T(8,128)(2,1)S(1)} %get-tuple-element.34), channel_id=1, source_target_pairs={{0,1},{1,0},{2,3},{3,2},{4,5},{5,4},{6,7},{7,6},{8,9},{9,8},{10,11... | collective-permute-start | bytes 49160 | tf_op jit(solution)/shard_map/ppermute | solution.py:348
  27.9 1.6 %collective-permute-start.1 = (bf16[64,128]{1,0:T(8,128)(2,1)S(1)}, bf16[64,128]{1,0:T(8,128)(2,1)S(1)}, u32[]{:S(2)}, u32[]{:S(2)}) collective-permute-start(bf16[64,128]{1,0:T(8,128)(2,1)S(1)} %get-tuple-element.35), channel_id=1, source_target_pairs={{0,2},{2,0},{1,3},{3,1},{4,6},{6,4},{5,7},{7,5},{8,10},{10,8},{9,1... | collective-permute-start | bytes 49160 | tf_op jit(solution)/shard_map/ppermute | solution.py:349
  30.7 2.0 %collective-permute-done.2 = bf16[64,128]{1,0:T(8,128)(2,1)S(1)} collective-permute-done((bf16[64,128]{1,0:T(8,128)(2,1)S(1)}, bf16[64,128]{1,0:T(8,128)(2,1)S(1)}, u32[]{:S(2)}, u32[]{:S(2)}) %collective-permute-start.2) | collective-permute-done | bytes 16416 | tf_op jit(solution)/shard_map/ppermute | solution.py:350
  33.1 0.7 collective-permute-start.15
  33.7 1.3 %collective-permute-start.10 = (bf16[256,128]{1,0:T(8,128)(2,1)S(1)}, bf16[256,128]{1,0:T(8,128)(2,1)S(1)}, u32[]{:S(2)}, u32[]{:S(2)}) collective-permute-start(bf16[256,128]{1,0:T(8,128)(2,1)S(1)} %get-tuple-element.58), channel_id=1, source_target_pairs={{0,32},{16,48},{32,0},{48,16},{1,33},{17,49},{33,1},{49,17},{2,34}... | collective-permute-start | bytes 196616 | tf_op jit(solution)/shard_map/ppermute | solution.py:323
  35.1 2.3 %collective-permute-start.11 = (bf16[256,128]{1,0:T(8,128)(2,1)S(1)}, bf16[256,128]{1,0:T(8,128)(2,1)S(1)}, u32[]{:S(2)}, u32[]{:S(2)}) collective-permute-start(bf16[256,128]{1,0:T(8,128)(2,1)S(1)} %get-tuple-element.58), channel_id=1, source_target_pairs={{0,48},{16,32},{32,16},{48,0},{1,49},{17,33},{33,17},{49,1},{2,50}... | collective-permute-start | bytes 196616 | tf_op jit(solution)/shard_map/ppermute | solution.py:323
  37.4 0.9 %collective-permute-done.10 = bf16[256,128]{1,0:T(8,128)(2,1)S(1)} collective-permute-done((bf16[256,128]{1,0:T(8,128)(2,1)S(1)}, bf16[256,128]{1,0:T(8,128)(2,1)S(1)}, u32[]{:S(2)}, u32[]{:S(2)}) %collective-permute-start.10) | collective-permute-done | bytes 65568 | tf_op jit(solution)/shard_map/ppermute | solution.py:323
  38.4 1.4 %collective-permute-start.4 = (bf16[4,128,128]{2,1,0:T(8,128)(2,1)S(1)}, bf16[4,128,128]{2,1,0:T(8,128)(2,1)S(1)}, u32[]{:S(2)}, u32[]{:S(2)}) collective-permute-start(bf16[4,128,128]{2,1,0:T(8,128)(2,1)S(1)} %get-tuple-element.43), channel_id=1, source_target_pairs={{0,32},{16,48},{32,0},{48,16},{1,33},{17,49},{33,1},{49,17},{2,34}... | collective-permute-start | bytes 393224 | tf_op jit(solution)/shard_map/ppermute | solution.py:323
  39.7 0.7 collective-permute-done.11
  40.4 1.8 %collective-permute-start.5 = (bf16[4,128,128]{2,1,0:T(8,128)(2,1)S(1)}, bf16[4,128,128]{2,1,0:T(8,128)(2,1)S(1)}, u32[]{:S(2)}, u32[]{:S(2)}) collective-permute-start(bf16[4,128,128]{2,1,0:T(8,128)(2,1)S(1)} %get-tuple-element.44), channel_id=1, source_target_pairs={{0,48},{16,32},{32,16},{48,0},{1,49},{17,33},{33,17},{49,1},{2,50}... | collective-permute-start | bytes 393224 | tf_op jit(solution)/shard_map/ppermute | solution.py:323
  42.4 1.9 %collective-permute-done.4.refs_2_ = bf16[4,128,128]{2,1,0:T(8,128)(2,1)S(1)} collective-permute-done((bf16[4,128,128]{2,1,0:T(8,128)(2,1)S(1)}, bf16[4,128,128]{2,1,0:T(8,128)(2,1)S(1)}, u32[]{:S(2)}, u32[]{:S(2)}) %collective-permute-start.4) | collective-permute-done | bytes 131104 | tf_op jit(solution)/shard_map/ppermute | solution.py:323
  44.2 3.3 %collective-permute-start.13 = (bf16[1024,128]{1,0:T(8,128)(2,1)S(1)}, bf16[1024,128]{1,0:T(8,128)(2,1)S(1)}, u32[]{:S(2)}, u32[]{:S(2)}) collective-permute-start(bf16[1024,128]{1,0:T(8,128)(2,1)S(1)} %constant_dynamic-update-slice_fusion.4.refs_0_), channel_id=1, source_target_pairs={{0,128},{64,192},{128,0},{192,64},{1,129},{65,193},{129,1},{193,65... | collective-permute-start | bytes 786440 | tf_op jit(solution)/shard_map/ppermute | solution.py:323
  47.6 0.9 %collective-permute-done.5.refs_3_ = bf16[4,128,128]{2,1,0:T(8,128)(2,1)S(1)} collective-permute-done((bf16[4,128,128]{2,1,0:T(8,128)(2,1)S(1)}, bf16[4,128,128]{2,1,0:T(8,128)(2,1)S(1)}, u32[]{:S(2)}, u32[]{:S(2)}) %collective-permute-start.5) | collective-permute-done | bytes 131104 | tf_op jit(solution)/shard_map/ppermute | solution.py:323
  48.4 1.4 %collective-permute-start.14 = (bf16[1024,128]{1,0:T(8,128)(2,1)S(1)}, bf16[1024,128]{1,0:T(8,128)(2,1)S(1)}, u32[]{:S(2)}, u32[]{:S(2)}) collective-permute-start(bf16[1024,128]{1,0:T(8,128)(2,1)S(1)} %constant_dynamic-update-slice_fusion.4.refs_0_), channel_id=1, source_target_pairs={{0,192},{64,128},{128,64},{192,0},{1,193},{65,129},{129,65},{193,1... | collective-permute-start | bytes 786440 | tf_op jit(solution)/shard_map/ppermute | solution.py:323
  50.5 2.4 %collective-permute-start.7 = (bf16[4,128,128]{2,1,0:T(8,128)(2,1)S(1)}, bf16[4,128,128]{2,1,0:T(8,128)(2,1)S(1)}, u32[]{:S(2)}, u32[]{:S(2)}) collective-permute-start(bf16[4,128,128]{2,1,0:T(8,128)(2,1)S(1)} %get-tuple-element.47), channel_id=1, source_target_pairs={{0,128},{64,192},{128,0},{192,64},{1,129},{65,193},{129,1},{193,65... | collective-permute-start | bytes 393224 | tf_op jit(solution)/shard_map/ppermute | solution.py:323
  53.0 2.3 %collective-permute-done.13.refs_2_ = bf16[1024,128]{1,0:T(8,128)(2,1)S(1)} collective-permute-done((bf16[1024,128]{1,0:T(8,128)(2,1)S(1)}, bf16[1024,128]{1,0:T(8,128)(2,1)S(1)}, u32[]{:S(2)}, u32[]{:S(2)}) %collective-permute-start.13) | collective-permute-done | bytes 262176 | tf_op jit(solution)/shard_map/ppermute | solution.py:323
  55.2 1.9 %collective-permute-start.8 = (bf16[4,128,128]{2,1,0:T(8,128)(2,1)S(1)}, bf16[4,128,128]{2,1,0:T(8,128)(2,1)S(1)}, u32[]{:S(2)}, u32[]{:S(2)}) collective-permute-start(bf16[4,128,128]{2,1,0:T(8,128)(2,1)S(1)} %get-tuple-element.48), channel_id=1, source_target_pairs={{0,192},{64,128},{128,64},{192,0},{1,193},{65,129},{129,65},{193,1... | collective-permute-start | bytes 393224 | tf_op jit(solution)/shard_map/ppermute | solution.py:323
  57.1 7.2 %collective-permute-done.14.refs_3_ = bf16[1024,128]{1,0:T(8,128)(2,1)S(1)} collective-permute-done((bf16[1024,128]{1,0:T(8,128)(2,1)S(1)}, bf16[1024,128]{1,0:T(8,128)(2,1)S(1)}, u32[]{:S(2)}, u32[]{:S(2)}) %collective-permute-start.14) | collective-permute-done | bytes 262176 | tf_op jit(solution)/shard_map/ppermute | solution.py:323
  64.4 1.3 %project.1 = (bf16[64,512]{1,0:T(8,128)(2,1)S(1)}, bf16[64,512]{1,0:T(8,128)(2,1)S(1)}, bf16[64,512]{1,0:T(8,128)(2,1)S(1)}, bf16[64,512]{1,0:T(8,128)(2,1)S(1)}) custom-call(s32[4]{0:T(128)S(1)} %pad_add_fusion.at_ref, bf16[1024,128]{1,0:T(8,128)(2,1)S(1)} %constant_dynamic-update-slice_fusion.4.refs_0_, ...), custom_call_target="tpu_custom_call" | custom-call | flops 536870912 | bytes 2097152 | tf_op jit(solution)/shard_map/project/pallas_call | solution.py:306
  65.6 5.6 %collective-permute-start.20 = (bf16[64,512]{1,0:T(8,128)(2,1)S(1)}, bf16[64,512]{1,0:T(8,128)(2,1)S(1)}, u32[]{:S(2)}, u32[]{:S(2)}) collective-permute-start(bf16[64,512]{1,0:T(8,128)(2,1)S(1)} %get-tuple-element.57), channel_id=1, source_target_pairs={{0,12},{4,8},{8,4},{12,0},{1,13},{5,9},{9,5},{13,1},{2,14},{6,10},... | collective-permute-start | bytes 196616 | tf_op jit(solution)/shard_map/ppermute | solution.py:323
  71.2 1.0 %collective-permute-start.19 = (bf16[64,512]{1,0:T(8,128)(2,1)S(1)}, bf16[64,512]{1,0:T(8,128)(2,1)S(1)}, u32[]{:S(2)}, u32[]{:S(2)}) collective-permute-start(bf16[64,512]{1,0:T(8,128)(2,1)S(1)} %get-tuple-element.56), channel_id=1, source_target_pairs={{0,8},{4,12},{8,0},{12,4},{1,9},{5,13},{9,1},{13,5},{2,10},{6,14},... | collective-permute-start | bytes 196616 | tf_op jit(solution)/shard_map/ppermute | solution.py:323
  72.2 1.2 %collective-permute-start.18 = (bf16[64,512]{1,0:T(8,128)(2,1)S(1)}, bf16[64,512]{1,0:T(8,128)(2,1)S(1)}, u32[]{:S(2)}, u32[]{:S(2)}) collective-permute-start(bf16[64,512]{1,0:T(8,128)(2,1)S(1)} %get-tuple-element.55), channel_id=1, source_target_pairs={{0,4},{4,0},{8,12},{12,8},{1,5},{5,1},{9,13},{13,9},{2,6},{6,2},{1... | collective-permute-start | bytes 196616 | tf_op jit(solution)/shard_map/ppermute | solution.py:323
  73.4 2.9 %finish.1 = bf16[4,512,512]{2,1,0:T(8,128)(2,1)} custom-call(s32[4]{0:T(128)S(1)} %pad_add_fusion.at_ref, bf16[4,512,512]{2,1,0:T(8,128)(2,1)S(1)} %copy-done.1, bf16[4,512,512]{2,1,0:T(8,128)(2,1)S(1)} %copy-done.2, bf16[4,128,128]{2,1,0:T(8,128)(2,1)S(1)} %get-tuple-element.45.refs_0_, bf16[4,128,128]{2,1,0:T(8,128)(2,1)S(1)} %collective-permute-done.6.refs_1_, ...), custom_call_target="tpu_custom_call" | custom-call | flops 268435456 | bytes 6291456 | tf_op jit(solution)/shard_map/finish/pallas_call | solution.py:266
  76.3 2.6 %collective-permute-done.19 = bf16[64,512]{1,0:T(8,128)(2,1)S(1)} collective-permute-done((bf16[64,512]{1,0:T(8,128)(2,1)S(1)}, bf16[64,512]{1,0:T(8,128)(2,1)S(1)}, u32[]{:S(2)}, u32[]{:S(2)}) %collective-permute-start.19) | collective-permute-done | bytes 65568 | tf_op jit(solution)/shard_map/ppermute | solution.py:323
  78.9 0.7 add_convert_fusion
  (39 shorter events, 2.7 us)
Async XLA Ops:
  0.6 14.0 %copy-start = (f32[4,4,128,128]{3,2,1,0:T(8,128)S(1)}, f32[4,4,128,128]{3,2,1,0:T(8,128)}, u32[]{:S(2)}) copy-start(f32[4,4,128,128]{3,2,1,0:T(8,128)} %param.12) | copy-start | bytes 3145732
  0.6 11.5 %copy-start.3 = (bf16[512,512]{1,0:T(8,128)(2,1)S(1)}, bf16[512,512]{1,0:T(8,128)(2,1)}, u32[]{:S(2)}) copy-start(bf16[512,512]{1,0:T(8,128)(2,1)} %refs_4_) | copy-start | bytes 1572868
  4.6 20.1 %all-to-all-start = ((bf16[16,176,128]{2,1,0:T(8,128)(2,1)}), bf16[16,176,128]{2,1,0:T(8,128)(2,1)S(1)}, u32[]{:S(2)}, u32[]{:S(2)}) async-start(bf16[16,176,128]{2,1,0:T(8,128)(2,1)} %block_states.1), calls=%async_computation | async-start | bytes 1441792 | tf_op jit(solution)/shard_map/all_to_all | solution.py:338
  12.2 21.6 %collective-permute-start.16 = (bf16[512,512]{1,0:T(8,128)(2,1)S(1)}, bf16[512,512]{1,0:T(8,128)(2,1)S(1)}, u32[]{:S(2)}, u32[]{:S(2)}) collective-permute-start(bf16[512,512]{1,0:T(8,128)(2,1)S(1)} %copy-done.3), channel_id=1, source_target_pairs={{0,2},{2,0},{1,3},{3,1},{4,6},{6,4},{5,7},{7,5},{8,10},{10,8},{9,1... | collective-permute-start | bytes 1572872 | tf_op jit(solution)/shard_map/ppermute | solution.py:340
  25.7 4.6 %collective-permute-start = (bf16[64,128]{1,0:T(8,128)(2,1)S(1)}, bf16[64,128]{1,0:T(8,128)(2,1)S(1)}, u32[]{:S(2)}, u32[]{:S(2)}) collective-permute-start(bf16[64,128]{1,0:T(8,128)(2,1)S(1)} %get-tuple-element.34), channel_id=1, source_target_pairs={{0,1},{1,0},{2,3},{3,2},{4,5},{5,4},{6,7},{7,6},{8,9},{9,8},{10,11... | collective-permute-start | bytes 49160 | tf_op jit(solution)/shard_map/ppermute | solution.py:348
  27.9 2.8 %collective-permute-start.1 = (bf16[64,128]{1,0:T(8,128)(2,1)S(1)}, bf16[64,128]{1,0:T(8,128)(2,1)S(1)}, u32[]{:S(2)}, u32[]{:S(2)}) collective-permute-start(bf16[64,128]{1,0:T(8,128)(2,1)S(1)} %get-tuple-element.35), channel_id=1, source_target_pairs={{0,2},{2,0},{1,3},{3,1},{4,6},{6,4},{5,7},{7,5},{8,10},{10,8},{9,1... | collective-permute-start | bytes 49160 | tf_op jit(solution)/shard_map/ppermute | solution.py:349
  29.6 3.2 %collective-permute-start.2 = (bf16[64,128]{1,0:T(8,128)(2,1)S(1)}, bf16[64,128]{1,0:T(8,128)(2,1)S(1)}, u32[]{:S(2)}, u32[]{:S(2)}) collective-permute-start(bf16[64,128]{1,0:T(8,128)(2,1)S(1)} %get-tuple-element.36), channel_id=1, source_target_pairs={{0,3},{1,2},{2,1},{3,0},{4,7},{5,6},{6,5},{7,4},{8,11},{9,10},{10,... | collective-permute-start | bytes 49160 | tf_op jit(solution)/shard_map/ppermute | solution.py:350
  32.7 40.7 %copy-start.2 = (bf16[4,512,512]{2,1,0:T(8,128)(2,1)S(1)}, bf16[4,512,512]{2,1,0:T(8,128)(2,1)}, u32[]{:S(2)}) copy-start(bf16[4,512,512]{2,1,0:T(8,128)(2,1)} %inside.1.inner_ref) | copy-start | bytes 6291460
  32.7 40.6 %copy-start.1 = (bf16[4,512,512]{2,1,0:T(8,128)(2,1)S(1)}, bf16[4,512,512]{2,1,0:T(8,128)(2,1)}, u32[]{:S(2)}) copy-start(bf16[4,512,512]{2,1,0:T(8,128)(2,1)} %q_ref.3) | copy-start | bytes 6291460
  32.8 4.6 %collective-permute-start.9 = (bf16[256,128]{1,0:T(8,128)(2,1)S(1)}, bf16[256,128]{1,0:T(8,128)(2,1)S(1)}, u32[]{:S(2)}, u32[]{:S(2)}) collective-permute-start(bf16[256,128]{1,0:T(8,128)(2,1)S(1)} %get-tuple-element.58), channel_id=1, source_target_pairs={{0,16},{16,0},{32,48},{48,32},{1,17},{17,1},{33,49},{49,33},{2,18}... | collective-permute-start | bytes 196616 | tf_op jit(solution)/shard_map/ppermute | solution.py:323
  33.1 17.3 %collective-permute-start.15 = (bf16[512,512]{1,0:T(8,128)(2,1)S(1)}, bf16[512,512]{1,0:T(8,128)(2,1)S(1)}, u32[]{:S(2)}, u32[]{:S(2)}) collective-permute-start(bf16[512,512]{1,0:T(8,128)(2,1)S(1)} %copy-done.3), channel_id=1, source_target_pairs={{0,1},{1,0},{2,3},{3,2},{4,5},{5,4},{6,7},{7,6},{8,9},{9,8},{10,11... | collective-permute-start | bytes 1572872 | tf_op jit(solution)/shard_map/ppermute | solution.py:360
  33.7 30.6 %collective-permute-start.17 = (bf16[512,512]{1,0:T(8,128)(2,1)S(1)}, bf16[512,512]{1,0:T(8,128)(2,1)S(1)}, u32[]{:S(2)}, u32[]{:S(2)}) collective-permute-start(bf16[512,512]{1,0:T(8,128)(2,1)S(1)} %collective-permute-done.16.refs_6_), channel_id=1, source_target_pairs={{0,1},{1,0},{2,3},{3,2},{4,5},{5,4},{6,7},{7,6},{8,9},{9,8},{10,11... | collective-permute-start | bytes 1572872 | tf_op jit(solution)/shard_map/ppermute | solution.py:361
  33.7 4.6 %collective-permute-start.10 = (bf16[256,128]{1,0:T(8,128)(2,1)S(1)}, bf16[256,128]{1,0:T(8,128)(2,1)S(1)}, u32[]{:S(2)}, u32[]{:S(2)}) collective-permute-start(bf16[256,128]{1,0:T(8,128)(2,1)S(1)} %get-tuple-element.58), channel_id=1, source_target_pairs={{0,32},{16,48},{32,0},{48,16},{1,33},{17,49},{33,1},{49,17},{2,34}... | collective-permute-start | bytes 196616 | tf_op jit(solution)/shard_map/ppermute | solution.py:323
  35.1 5.4 %collective-permute-start.11 = (bf16[256,128]{1,0:T(8,128)(2,1)S(1)}, bf16[256,128]{1,0:T(8,128)(2,1)S(1)}, u32[]{:S(2)}, u32[]{:S(2)}) collective-permute-start(bf16[256,128]{1,0:T(8,128)(2,1)S(1)} %get-tuple-element.58), channel_id=1, source_target_pairs={{0,48},{16,32},{32,16},{48,0},{1,49},{17,33},{33,17},{49,1},{2,50}... | collective-permute-start | bytes 196616 | tf_op jit(solution)/shard_map/ppermute | solution.py:323
  37.4 4.8 %collective-permute-start.3 = (bf16[4,128,128]{2,1,0:T(8,128)(2,1)S(1)}, bf16[4,128,128]{2,1,0:T(8,128)(2,1)S(1)}, u32[]{:S(2)}, u32[]{:S(2)}) collective-permute-start(bf16[4,128,128]{2,1,0:T(8,128)(2,1)S(1)} %get-tuple-element.42), channel_id=1, source_target_pairs={{0,16},{16,0},{32,48},{48,32},{1,17},{17,1},{33,49},{49,33},{2,18}... | collective-permute-start | bytes 393224 | tf_op jit(solution)/shard_map/ppermute | solution.py:323
  38.4 5.9 %collective-permute-start.4 = (bf16[4,128,128]{2,1,0:T(8,128)(2,1)S(1)}, bf16[4,128,128]{2,1,0:T(8,128)(2,1)S(1)}, u32[]{:S(2)}, u32[]{:S(2)}) collective-permute-start(bf16[4,128,128]{2,1,0:T(8,128)(2,1)S(1)} %get-tuple-element.43), channel_id=1, source_target_pairs={{0,32},{16,48},{32,0},{48,16},{1,33},{17,49},{33,1},{49,17},{2,34}... | collective-permute-start | bytes 393224 | tf_op jit(solution)/shard_map/ppermute | solution.py:323
  40.4 8.0 %collective-permute-start.5 = (bf16[4,128,128]{2,1,0:T(8,128)(2,1)S(1)}, bf16[4,128,128]{2,1,0:T(8,128)(2,1)S(1)}, u32[]{:S(2)}, u32[]{:S(2)}) collective-permute-start(bf16[4,128,128]{2,1,0:T(8,128)(2,1)S(1)} %get-tuple-element.44), channel_id=1, source_target_pairs={{0,48},{16,32},{32,16},{48,0},{1,49},{17,33},{33,17},{49,1},{2,50}... | collective-permute-start | bytes 393224 | tf_op jit(solution)/shard_map/ppermute | solution.py:323
  42.3 8.3 %collective-permute-start.12 = (bf16[1024,128]{1,0:T(8,128)(2,1)S(1)}, bf16[1024,128]{1,0:T(8,128)(2,1)S(1)}, u32[]{:S(2)}, u32[]{:S(2)}) collective-permute-start(bf16[1024,128]{1,0:T(8,128)(2,1)S(1)} %constant_dynamic-update-slice_fusion.4.refs_0_), channel_id=1, source_target_pairs={{0,64},{64,0},{128,192},{192,128},{1,65},{65,1},{129,193},{193,129... | collective-permute-start | bytes 786440 | tf_op jit(solution)/shard_map/ppermute | solution.py:323
  44.2 11.0 %collective-permute-start.13 = (bf16[1024,128]{1,0:T(8,128)(2,1)S(1)}, bf16[1024,128]{1,0:T(8,128)(2,1)S(1)}, u32[]{:S(2)}, u32[]{:S(2)}) collective-permute-start(bf16[1024,128]{1,0:T(8,128)(2,1)S(1)} %constant_dynamic-update-slice_fusion.4.refs_0_), channel_id=1, source_target_pairs={{0,128},{64,192},{128,0},{192,64},{1,129},{65,193},{129,1},{193,65... | collective-permute-start | bytes 786440 | tf_op jit(solution)/shard_map/ppermute | solution.py:323
  48.4 15.9 %collective-permute-start.14 = (bf16[1024,128]{1,0:T(8,128)(2,1)S(1)}, bf16[1024,128]{1,0:T(8,128)(2,1)S(1)}, u32[]{:S(2)}, u32[]{:S(2)}) collective-permute-start(bf16[1024,128]{1,0:T(8,128)(2,1)S(1)} %constant_dynamic-update-slice_fusion.4.refs_0_), channel_id=1, source_target_pairs={{0,192},{64,128},{128,64},{192,0},{1,193},{65,129},{129,65},{193,1... | collective-permute-start | bytes 786440 | tf_op jit(solution)/shard_map/ppermute | solution.py:323
  50.4 21.8 %collective-permute-start.6 = (bf16[4,128,128]{2,1,0:T(8,128)(2,1)S(1)}, bf16[4,128,128]{2,1,0:T(8,128)(2,1)S(1)}, u32[]{:S(2)}, u32[]{:S(2)}) collective-permute-start(bf16[4,128,128]{2,1,0:T(8,128)(2,1)S(1)} %get-tuple-element.46), channel_id=1, source_target_pairs={{0,64},{64,0},{128,192},{192,128},{1,65},{65,1},{129,193},{193,129... | collective-permute-start | bytes 393224 | tf_op jit(solution)/shard_map/ppermute | solution.py:323
  50.5 22.8 %collective-permute-start.7 = (bf16[4,128,128]{2,1,0:T(8,128)(2,1)S(1)}, bf16[4,128,128]{2,1,0:T(8,128)(2,1)S(1)}, u32[]{:S(2)}, u32[]{:S(2)}) collective-permute-start(bf16[4,128,128]{2,1,0:T(8,128)(2,1)S(1)} %get-tuple-element.47), channel_id=1, source_target_pairs={{0,128},{64,192},{128,0},{192,64},{1,129},{65,193},{129,1},{193,65... | collective-permute-start | bytes 393224 | tf_op jit(solution)/shard_map/ppermute | solution.py:323
  55.2 18.1 %collective-permute-start.8 = (bf16[4,128,128]{2,1,0:T(8,128)(2,1)S(1)}, bf16[4,128,128]{2,1,0:T(8,128)(2,1)S(1)}, u32[]{:S(2)}, u32[]{:S(2)}) collective-permute-start(bf16[4,128,128]{2,1,0:T(8,128)(2,1)S(1)} %get-tuple-element.48), channel_id=1, source_target_pairs={{0,192},{64,128},{128,64},{192,0},{1,193},{65,129},{129,65},{193,1... | collective-permute-start | bytes 393224 | tf_op jit(solution)/shard_map/ppermute | solution.py:323
  65.6 10.6 %collective-permute-start.20 = (bf16[64,512]{1,0:T(8,128)(2,1)S(1)}, bf16[64,512]{1,0:T(8,128)(2,1)S(1)}, u32[]{:S(2)}, u32[]{:S(2)}) collective-permute-start(bf16[64,512]{1,0:T(8,128)(2,1)S(1)} %get-tuple-element.57), channel_id=1, source_target_pairs={{0,12},{4,8},{8,4},{12,0},{1,13},{5,9},{9,5},{13,1},{2,14},{6,10},... | collective-permute-start | bytes 196616 | tf_op jit(solution)/shard_map/ppermute | solution.py:323
  71.2 7.7 %collective-permute-start.19 = (bf16[64,512]{1,0:T(8,128)(2,1)S(1)}, bf16[64,512]{1,0:T(8,128)(2,1)S(1)}, u32[]{:S(2)}, u32[]{:S(2)}) collective-permute-start(bf16[64,512]{1,0:T(8,128)(2,1)S(1)} %get-tuple-element.56), channel_id=1, source_target_pairs={{0,8},{4,12},{8,0},{12,4},{1,9},{5,13},{9,1},{13,5},{2,10},{6,14},... | collective-permute-start | bytes 196616 | tf_op jit(solution)/shard_map/ppermute | solution.py:323
  72.2 6.7 %collective-permute-start.18 = (bf16[64,512]{1,0:T(8,128)(2,1)S(1)}, bf16[64,512]{1,0:T(8,128)(2,1)S(1)}, u32[]{:S(2)}, u32[]{:S(2)}) collective-permute-start(bf16[64,512]{1,0:T(8,128)(2,1)S(1)} %get-tuple-element.55), channel_id=1, source_target_pairs={{0,4},{4,0},{8,12},{12,8},{1,5},{5,1},{9,13},{13,9},{2,6},{6,2},{1... | collective-permute-start | bytes 196616 | tf_op jit(solution)/shard_map/ppermute | solution.py:323
